TPU v7x, 128 devices: a whole 4x4x4 slice. The times are simulated.
128 devices in a mesh: layer: 4 (over y), latent: 16 (over x, z), tok: 2 (over core).
Axes of the slice: x: 4, y: 4, z: 4, core: 2. Of those that a mesh axis runs over, the one named last changes fastest.
Arguments:
- resid_in: bfloat16 [4, 1024, 2304], P('layer', 'tok'), may hold values from -6 to 6
- resid_out: bfloat16 [4, 1024, 2304], P('layer', 'tok', 'latent'), may hold values from -6 to 6
- enc_weight: bfloat16 [4, 2304, 8192], P('layer', None, 'latent'), may hold values from -0.125 to 0.125
- enc_bias: float32 [4, 8192], P('layer', 'latent'), may hold values from -1 to 1
- dec_weight: bfloat16 [4, 4, 8192, 2304], P('layer', None, 'latent'), may hold values from -0.09375 to 0.09375
- dec_bias: float32 [4, 2304], P('layer', 'latent'), may hold values from -3 to 3
Outputs:
- dec_grad: float32 [4, 4, 8192, 2304], P('layer', None, 'latent', 'tok')
- dec_bias_grad: float32 [4, 2304], P('layer', 'latent')
- enc_grad: float32 [4, 2304, 8192], P('layer', 'tok', 'latent')
- enc_bias_grad: float32 [4, 8192], P('layer', 'latent')
All inputs are finite; a program needn't handle non-finite values.
Results may differ from a plain program's by a relative error of at most 0.0045.
Values may be sent and summed in bfloat16 or wider, within the bound.
No kernel may reach another device: no remote copies, remote signals or barrier semaphores. Data moves between devices by JAX's collectives and lax.ppermute only.
A program may use at most 128 MiB of HBM per device.

v0:
```python
import math

import jax
import jax.numpy as jnp
from jax import lax
from jax.sharding import PartitionSpec as P


def smooth(values):
    return jax.nn.gelu(values, approximate=True)


def on_device(resid_in, resid_out, enc_weight, enc_bias, dec_weight, dec_bias):
    source = lax.axis_index("layer")
    shards = lax.axis_size("latent")
    layers = dec_weight.shape[1]
    latent_dev = dec_weight.shape[2]
    model_width = dec_weight.shape[3]
    piece_cols = model_width // shards
    tok_dev = resid_in.shape[1]
    loss_scale = 1.0 / math.sqrt(tok_dev * lax.axis_size("tok"))
    inputs = resid_in[0]
    pre_act = jnp.dot(inputs, enc_weight[0], preferred_element_type=jnp.float32) + enc_bias[0]
    latents = smooth(pre_act).astype(jnp.bfloat16)
    blocked = dec_weight[0].reshape(layers, latent_dev, shards, piece_cols)
    row_ids = jnp.arange(1 * lax.axis_size(("layer", "latent")), dtype=jnp.int32)
    target = row_ids // shards
    blocks = blocked[target, :, row_ids % shards, :]
    is_live = (target >= source)[:, None, None]
    product = jnp.einsum("kf,rfd->rkd", latents, blocks, preferred_element_type=jnp.float32)
    rebuilt = lax.psum_scatter(
        jnp.where(is_live, product, jnp.zeros_like(product)),
        ("layer", "latent"),
        scatter_dimension=0,
        tiled=True,
    )[0]
    errors = ((rebuilt + dec_bias[0] - resid_out[0].astype(jnp.float32)) * loss_scale).astype(
        jnp.bfloat16
    )
    block_in = lax.all_gather(errors[None], ("layer", "latent"), axis=0, tiled=True)
    row_ids = jnp.arange(block_in.shape[0], dtype=jnp.int32)
    err_rows = block_in
    target = row_ids // shards
    blocks = blocked[target, :, row_ids % shards, :]
    is_live = (target >= source)[:, None, None]
    err_rows = jnp.where(is_live, err_rows, jnp.zeros_like(err_rows))
    act_adds = jnp.einsum("rkd,rfd->kf", err_rows, blocks, preferred_element_type=jnp.float32)
    grad_part = jnp.einsum("kf,rkd->rfd", latents, err_rows, preferred_element_type=jnp.float32)
    act_adds, grad_part = (act_adds, grad_part)
    dec_full = (
        grad_part.reshape(layers, shards, latent_dev, piece_cols)
        .transpose(0, 2, 1, 3)
        .reshape(layers, latent_dev, model_width)
    )
    pre_grad = jax.vjp(smooth, pre_act)[1](act_adds)[0].astype(jnp.bfloat16)
    enc_full = lax.dot_general(
        inputs, pre_grad, (((0,), (0,)), ((), ())), preferred_element_type=jnp.float32
    )
    enc_bias_part = jnp.sum(pre_grad.astype(jnp.float32), axis=0)
    dec_bias_part = jnp.sum(errors.astype(jnp.float32), axis=0)
    dec_grad = lax.psum_scatter(dec_full[None], "tok", scatter_dimension=3, tiled=True)
    enc_grad = lax.psum_scatter(enc_full[None], "tok", scatter_dimension=1, tiled=True)
    enc_bias_grad, dec_bias_grad = lax.psum((enc_bias_part[None], dec_bias_part[None]), "tok")
    return (dec_grad, dec_bias_grad, enc_grad, enc_bias_grad)


def solution(mesh):
    in_specs = (
        P("layer", "tok", None),
        P("layer", "tok", "latent"),
        P("layer", None, "latent"),
        P("layer", "latent"),
        P("layer", None, "latent", None),
        P("layer", "latent"),
    )
    out_specs = (
        P("layer", None, "latent", "tok"),
        P("layer", "latent"),
        P("layer", "tok", "latent"),
        P("layer", "latent"),
    )
    return jax.shard_map(
        on_device, mesh=mesh, in_specs=in_specs, out_specs=out_specs, check_vma=False
    )
```

profile of v0, /device:TPU:1, one launch (start us, length us, event | category | flops | bytes accessed | tf_op | source)
XLA Modules:
  0.0 455.1 jit_solution(11266010121538422311)
XLA Ops:
  7.2 0.0 copy-start
  7.2 0.0 reduce-scatter.4.cloned.1.call-start
  7.3 12.8 %copy.15 = bf16[1,4,512,2304]{2,3,1,0:T(8,128)(2,1)} copy(bf16[1,4,512,2304]{3,2,1,0:T(8,128)(2,1)} %param.10) | data formatting | bytes 18874368 | tf_op args[4]
  20.0 0.0 copy-start.4
  20.0 10.1 %gather_fusion = bf16[64,512,144]{1,2,0:T(8,128)(2,1)} fusion(bf16[4,512,16,144]{1,3,2,0:T(8,128)(2,1)} %bitcast.60, s32[64]{0:T(128)S(1)} %fusion.29), kind=kCustom, calls=%fused_computation | custom fusion | bytes 18874880 | tf_op jit(solution)/shard_map/gather | solution.py:28
  30.1 0.0 copy-done
  30.1 0.0 copy-done.4
  30.1 3.0 fusion.7
  33.2 0.0 copy-start.5
  33.2 1.0 copy-done.5
  34.2 13.0 %select_bitcast_fusion = f32[64,512,144]{1,2,0:T(8,128)} fusion(pred[64]{0:T(512)(128)(4,1)S(1)} %fusion.30, bf16[64,512,144]{1,2,0:T(8,128)(2,1)} %gather_fusion, f32[512,512]{1,0:T(8,128)S(1)} %fusion.7), kind=kOutput, calls=%fused_computation.1 | convolution fusion | flops 4838916096 | bytes 29360192 | tf_op jit(solution)/shard_map/kf,rfd->rkd/dot_general | solution.py:30
  47.2 0.0 copy-start.2
  47.2 0.0 copy-start.3
  47.2 0.0 reduce-scatter.4.cloned.1.call-update
  47.2 0.0 all-gather.2.cloned.1.call-start
  47.2 239.4 %reduce-scatter.4.cloned.1.call-done = f32[1,512,144]{1,2,0:T(8,128)} async-done(((f32[64,512,144]{1,2,0:T(8,128)}), f32[1,512,144]{1,2,0:T(8,128)}) %reduce-scatter.4.cloned.1.call-update) | async-done | bytes 294928 | tf_op jit(solution)/shard_map/reduce_scatter | solution.py:31
  286.7 0.0 copy-done.2
  286.7 0.0 copy-done.3
  286.7 1.7 fusion.22
  288.4 0.0 all-gather.2.cloned.1.call-update
  288.5 0.0 reduce-scatter.8.cloned.1.call-start
  288.5 82.9 %all-gather.2.cloned.1.call-done = bf16[64,512,144]{1,2,0:T(8,128)(2,1)} async-done(((bf16[1,512,144]{1,2,0:T(8,128)(2,1)}), bf16[64,512,144]{1,2,0:T(8,128)(2,1)}) %all-gather.2.cloned.1.call-update) | async-done | bytes 9437200 | tf_op jit(solution)/shard_map/all_gather | solution.py:40
  371.4 14.0 %convert_reduce_fusion = (f32[512]{0:T(512)S(1)}, bf16[512,512]{1,0:T(8,128)(2,1)S(1)}) fusion(f32[512,512]{1,0:T(8,128)} %copy-done.5, bf16[64,512,144]{1,2,0:T(8,128)(2,1)} %gather_fusion, bf16[64,512,144]{1,2,0:T(8,128)(2,1)} %all-gather.2.cloned.1.call-done, pred[64]{0:T(512)(128)(4,1)S(1)} %fusion.30), kind=kOutput, calls=%fused_computation.21 | convolution fusion | flops 4842323456 | bytes 20449344 | tf_op jit(solution)/shard_map/rkd,rfd->kf/dot_general | solution.py:47
  385.4 3.6 convolution_bitcast_fusion
  389.0 0.0 reduce-scatter.8.cloned.1.call-update
  389.0 0.2 reduce-scatter.6.cloned.1.call-start
  389.3 13.5 %fusion.1 = f32[64,144,512]{2,1,0:T(8,128)} fusion(bf16[64,512,144]{1,2,0:T(8,128)(2,1)} %all-gather.2.cloned.1.call-done, pred[64]{0:T(512)(128)(4,1)S(1)} %fusion.30, f32[512,512]{1,0:T(8,128)} %copy-done.5), kind=kOutput, calls=%fused_computation.5 | convolution fusion | flops 4838916096 | bytes 29360192 | tf_op jit(solution)/shard_map/kf,rkd->rfd/dot_general | solution.py:48
  402.8 0.0 copy-start.1
  402.8 0.0 reduce-scatter.6.cloned.1.call-update
  402.8 1.0 copy-done.1
  403.8 0.2 convert_reduce_fusion.1
  404.0 3.5 all-reduce
  407.4 0.0 reduce-scatter.8.cloned.1.call-done
  407.4 3.0 copy.17
  410.5 28.5 %reduce-scatter.6.cloned.1.call-done = f32[1,4,512,1152]{2,3,1,0:T(8,128)} async-done(((f32[1,4,512,2304]{2,3,1,0:T(8,128)}), f32[1,4,512,1152]{2,3,1,0:T(8,128)}) %reduce-scatter.6.cloned.1.call-update) | async-done | bytes 9437200 | tf_op jit(solution)/shard_map/reduce_scatter | solution.py:61
  439.0 9.6 %copy.16 = f32[1,4,512,1152]{3,2,1,0:T(8,128)} copy(f32[1,4,512,1152]{2,3,1,0:T(8,128)} %reduce-scatter.6.cloned.1.call-done) | data formatting | bytes 18874368
  (2 shorter events, 0.0 us)
Async XLA Ops:
  7.2 23.0 %copy-start = (bf16[1,512,2304]{2,1,0:T(8,128)(2,1)S(1)}, bf16[1,512,2304]{2,1,0:T(8,128)(2,1)}, u32[]{:S(2)}) copy-start(bf16[1,512,2304]{2,1,0:T(8,128)(2,1)} %param.6) | copy-start | bytes 7077892
  7.2 279.5 %reduce-scatter.4.cloned.1.call-start = ((), (), s32[]{:S(2)}) async-start(), calls=%async_computation.3 | async-start | bytes 19169280 | tf_op jit(solution)/shard_map/reduce_scatter | solution.py:31
  20.0 10.1 %copy-start.4 = (f32[1,512]{1,0:T(1,128)S(1)}, f32[1,512]{1,0:T(1,128)}, u32[]{:S(2)}) copy-start(f32[1,512]{1,0:T(1,128)} %param.9) | copy-start | bytes 6148
  33.2 1.0 copy-start.5
  47.2 239.5 %copy-start.2 = (bf16[1,512,144]{1,2,0:T(8,128)(2,1)S(1)}, bf16[1,512,144]{1,2,0:T(8,128)(2,1)}, u32[]{:S(2)}) copy-start(bf16[1,512,144]{1,2,0:T(8,128)(2,1)} %param.7) | copy-start | bytes 442372
  47.2 239.5 %copy-start.3 = (f32[1,144]{1,0:T(1,128)S(1)}, f32[1,144]{1,0:T(1,128)}, u32[]{:S(2)}) copy-start(f32[1,144]{1,0:T(1,128)} %param.11) | copy-start | bytes 1732
  47.2 324.2 %all-gather.2.cloned.1.call-start = ((), (), s32[]{:S(2)}) async-start(), calls=%async_computation.4 | async-start | bytes 9584640 | tf_op jit(solution)/shard_map/all_gather | solution.py:40
  288.5 119.0 %reduce-scatter.8.cloned.1.call-start = ((), (), s32[]{:S(2)}) async-start(), calls=%async_computation.6 | async-start | bytes 7077888 | tf_op jit(solution)/shard_map/reduce_scatter | solution.py:62
  389.0 50.0 %reduce-scatter.6.cloned.1.call-start = ((), (), s32[]{:S(2)}) async-start(), calls=%async_computation.5 | async-start | bytes 28311552 | tf_op jit(solution)/shard_map/reduce_scatter | solution.py:61
  402.8 1.0 copy-start.1
Sparse Core Ops, SparseCore 0:
  47.3 239.3 reduce-scatter.3
  290.5 80.8 all-gather.1
  389.2 15.2 reduce-scatter.7
  406.7 32.2 reduce-scatter.5
where the time goes:
time: 456 us; the launch traced here: 455 us
  waiting for transfers between devices  351 us (77%)
  matrix products  47.2 us (10%)
  local copies, waits for them, and re-layouts  37.4 us (8%)
  between operations  13.8 us (3%)
    reduce_scatter x1, waiting for transfers between devices, on_device(): lax.psum_scatter(jnp.where(is_live, product, jnp.zeros_like(product)), ('...  239 us
    all_gather x1, waiting for transfers between devices, on_device(): lax.all_gather(errors[None], ('layer', 'latent'), axis=0, tiled=True)  82.9 us
    reduce_scatter x1, waiting for transfers between devices, on_device(): lax.psum_scatter(dec_full[None], 'tok', scatter_dimension=3, tiled=True)  28.5 us
    unnamed x15, local copies, waits for them, and re-layouts  27.4 us
    dot_general x1, matrix products, on_device(): jnp.einsum('rkd,rfd->kf', err_rows, blocks, preferred_element_type=jnp.fl...  14 us
    dot_general x1, matrix products, on_device(): jnp.einsum('kf,rkd->rfd', latents, err_rows, preferred_element_type=jnp.f...  13.5 us
    dot_general x1, matrix products, on_device(): jnp.einsum('kf,rfd->rkd', latents, blocks, preferred_element_type=jnp.flo...  13 us
    gather x1, local copies, waits for them, and re-layouts, on_device(): blocks = blocked[target, :, row_ids % shards, :]  10.1 us
  transfers between devices with their start and end apart: 4, of which 3 were waited for; matrix products, arithmetic and copies ran while one was open for 4% of the time, Pallas kernels for 0%

commit v1 on v0

v1 whole, which is shorter than its diff:
```python
import functools
import math

import jax
import jax.numpy as jnp
from jax import lax
from jax.experimental import pallas as pl
from jax.experimental.pallas import tpu as pltpu
from jax.sharding import PartitionSpec as P

LAYER, LX, LZ, TOK = "layer", "lx", "lz", "tok"
BF16, F32 = jnp.bfloat16, jnp.float32


def smooth(values):
    return jax.nn.gelu(values, approximate=True)


def shift(value, axis, step):
    n = lax.axis_size(axis)
    return lax.ppermute(value, axis, [(i, (i + step) % n) for i in range(n)])


def send_up(value, step):
    n = lax.axis_size(LAYER)
    pairs = [(i, i + step) for i in range(n) if 0 <= i + step < n]
    return lax.ppermute(value, LAYER, pairs)


def swap(value):
    return lax.ppermute(value, TOK, [(0, 1), (1, 0)])


def turned(value, axis, by):
    n = value.shape[axis]
    return lax.dynamic_slice_in_dim(jnp.concatenate([value, value], axis), by, n, axis)


def spread(value, axis):
    return [value[0]] + [shift(value[k], axis, k) for k in range(1, len(value))]


def gathered(value, axis):
    n = lax.axis_size(axis)
    return [value] + [shift(value, axis, -k) for k in range(1, n)]


def total(values):
    return functools.reduce(jnp.add, [v.astype(F32) for v in values])


def params():
    return pltpu.CompilerParams(vmem_limit_bytes=56 * 2**20)


def y_kernel(where, lat_ref, w_ref, y_ref, *, cols):
    live = where[0] + pl.program_id(0) < pl.num_programs(0)

    @pl.when(live)
    def _():
        y_ref[0] = jnp.dot(
            lat_ref[...], w_ref[0, :, :cols], preferred_element_type=F32
        ).astype(BF16)

    @pl.when(jnp.logical_not(live))
    def _():
        y_ref[0] = jnp.zeros_like(y_ref[0])


def x_kernel(where, lat_ref, w_ref, *out_refs, cols):
    rows = out_refs[0].shape[1]
    for i, out in enumerate(out_refs):
        out[0] = jnp.dot(
            lat_ref[i * rows : (i + 1) * rows, :],
            w_ref[0, :, cols:],
            preferred_element_type=F32,
        ).astype(BF16)


def rebuild_y(where, lat, weights, width, cols):
    layers, feats, _ = weights.shape
    rows = lat.shape[0]
    return pl.pallas_call(
        functools.partial(y_kernel, cols=cols),
        out_shape=jax.ShapeDtypeStruct((layers, rows, cols), BF16),
        grid_spec=pltpu.PrefetchScalarGridSpec(
            num_scalar_prefetch=1,
            grid=(layers,),
            in_specs=[
                pl.BlockSpec((rows, feats), lambda k, w: (0, 0)),
                pl.BlockSpec((1, feats, width), lambda k, w: (lax.rem(w[0] + k, layers), 0, w[1])),
            ],
            out_specs=pl.BlockSpec((1, rows, cols), lambda k, w: (lax.rem(w[0] + k, layers), 0, 0)),
        ),
        compiler_params=params(),
        cost_estimate=pl.CostEstimate(
            flops=2 * layers * rows * feats * cols, bytes_accessed=10 * 2**20, transcendentals=0
        ),
    )(where, lat, weights)


def rebuild_x(where, lat, weights, width, cols, first, count, parts):
    layers, feats, _ = weights.shape
    rows = lat.shape[0]
    step = rows // parts
    return pl.pallas_call(
        functools.partial(x_kernel, cols=cols),
        out_shape=[jax.ShapeDtypeStruct((count, step, width - cols), BF16)] * parts,
        grid_spec=pltpu.PrefetchScalarGridSpec(
            num_scalar_prefetch=1,
            grid=(count,),
            in_specs=[
                pl.BlockSpec((rows, feats), lambda k, w: (0, 0)),
                pl.BlockSpec(
                    (1, feats, width), lambda k, w: (lax.rem(w[0] + first + k, layers), 0, w[1])
                ),
            ],
            out_specs=[pl.BlockSpec((1, step, width - cols), lambda k, w: (k, 0, 0))] * parts,
        ),
        compiler_params=params(),
        cost_estimate=pl.CostEstimate(
            flops=2 * count * rows * feats * (width - cols),
            bytes_accessed=8 * 2**20,
            transcendentals=0,
        ),
    )(where, lat, weights)


def grad_kernel(where, lat_t_ref, w_ref, y_ref, *refs, parts, cols, ring):
    x_refs = refs[:parts]
    dec_ref, own_ref, other_ref, sum_ref, err_ref, act_ref = refs[parts:]
    k = pl.program_id(0)
    live = where[0] + k < pl.num_programs(0)
    rows = err_ref.shape[0]
    step = rows // parts

    @pl.when(live)
    def _():
        err_ref[:, :cols] = y_ref[0]
        for i, x_ref in enumerate(x_refs):
            err_ref[i * step : (i + 1) * step, cols:] = x_ref[0]
        half = lat_t_ref.shape[0] // 2
        for i in range(2):
            dec_ref[0, i * half : (i + 1) * half, :] = jnp.dot(
                lat_t_ref[i * half : (i + 1) * half, :], err_ref[...], preferred_element_type=F32
            )
        for i in range(2):
            add = lax.dot_general(
                err_ref[...],
                w_ref[0, i * half : (i + 1) * half, :],
                (((1,), (1,)), ((), ())),
                preferred_element_type=F32,
            )
            here = slice(i * half, (i + 1) * half)

            @pl.when(k == 0)
            def _():
                act_ref[:, here] = add

            @pl.when(k > 0)
            def _():
                act_ref[:, here] += add

    @pl.when(jnp.logical_not(live))
    def _():
        dec_ref[0] = jnp.zeros_like(dec_ref[0])

    @pl.when(k == 0)
    def _():
        sum_ref[...] = jnp.sum(err_ref[...].astype(F32), axis=0, keepdims=True)

    @pl.when(k == pl.num_programs(0) - 1)
    def _():
        own_ref[...] = act_ref[: rows // 2, :]
        piece = rows // 2 // ring // ring
        for i in range(ring):
            for j in range(ring):
                to, at = (i * ring + j) * piece, rows // 2 + (j * ring + i) * piece
                other_ref[to : to + piece, :] = act_ref[at : at + piece, :]


def grads(where, lat_t, weights, err_y, err_x, width, ring):
    layers, feats, _ = weights.shape
    rows = lat_t.shape[1]
    cols, parts = err_y.shape[2], len(err_x)
    return pl.pallas_call(
        functools.partial(grad_kernel, parts=parts, cols=cols, ring=ring),
        out_shape=[
            jax.ShapeDtypeStruct((layers, feats, width), F32),
            jax.ShapeDtypeStruct((rows // 2, feats), F32),
            jax.ShapeDtypeStruct((rows // 2, feats), F32),
            jax.ShapeDtypeStruct((1, width), F32),
        ],
        grid_spec=pltpu.PrefetchScalarGridSpec(
            num_scalar_prefetch=1,
            grid=(layers,),
            in_specs=[
                pl.BlockSpec((feats, rows), lambda k, w: (0, 0)),
                pl.BlockSpec((1, feats, width), lambda k, w: (lax.rem(w[0] + k, layers), 0, w[1])),
                pl.BlockSpec((1, rows, cols), lambda k, w: (lax.rem(w[0] + k, layers), 0, 0)),
            ]
            + [pl.BlockSpec((1, rows // parts, width - cols), lambda k, w: (k, 0, 0))] * parts,
            out_specs=[
                pl.BlockSpec((1, feats, width), lambda k, w: (lax.rem(w[0] + k, layers), 0, 0)),
                pl.BlockSpec((rows // 2, feats), lambda k, w: (0, 0)),
                pl.BlockSpec((rows // 2, feats), lambda k, w: (0, 0)),
                pl.BlockSpec((1, width), lambda k, w: (0, 0)),
            ],
            scratch_shapes=[pltpu.VMEM((rows, width), BF16), pltpu.VMEM((rows, feats), F32)],
        ),
        compiler_params=params(),
        cost_estimate=pl.CostEstimate(
            flops=4 * layers * rows * feats * width, bytes_accessed=40 * 2**20, transcendentals=0
        ),
    )(where, lat_t, weights, err_y, *err_x)


def on_device(resid_in, resid_out, enc_weight, enc_bias, dec_weight, dec_bias):
    s, x, z, c = (lax.axis_index(a) for a in (LAYER, LX, LZ, TOK))
    ring = lax.axis_size(LX)
    layers, feats, model = dec_weight.shape[1:]
    tok = resid_in.shape[1]
    width = model // 2
    cols = width // 3
    piece = tok // (ring * ring)
    scale = 1.0 / math.sqrt(tok * lax.axis_size(TOK))
    where = jnp.stack([s, c]).astype(jnp.int32)
    inputs, weights = resid_in[0], dec_weight[0]

    def mine_first(rows):
        blocks = rows.reshape(ring, ring, piece, rows.shape[1])
        return turned(turned(blocks, 0, x), 1, z).reshape(rows.shape)

    def crossed(rows):
        blocks = rows.reshape(ring, ring, -1, rows.shape[1])
        return blocks.transpose(1, 0, 2, 3).reshape(rows.shape)

    pre = mine_first(jnp.dot(inputs, enc_weight[0], preferred_element_type=F32) + enc_bias[0])
    own_lat = smooth(pre).astype(BF16)
    lat = jnp.concatenate([own_lat, crossed(swap(own_lat))], 0)

    y_part = rebuild_y(where, lat, weights, width, cols)
    y_sum = lax.psum_scatter(y_part, LAYER, scatter_dimension=0, tiled=True)[0]

    got_a, got_b = [], []
    for first in (0, 2):
        out = rebuild_x(where, lat, weights, width, cols, first, 2, 2 * ring)
        a, b = spread(out[:ring], LX), spread(out[ring:], LZ)
        got_a.append(total(a))
        got_b.append(total(b))
    lat, own_lat, anchor = lax.optimization_barrier((lat, own_lat, resid_out))
    lat_t = lat.T
    x_a, x_b = (jnp.concatenate(g, 0).astype(BF16) for g in (got_a, got_b))

    own_base = anchor[0].reshape(ring * ring, piece, -1)
    base = jnp.stack([own_base, swap(own_base)]).astype(F32)
    base = lax.all_to_all(dec_bias[0] - base, (LX, LZ), 1, 1, tiled=True)
    base = lax.dynamic_slice_in_dim(base, c * (ring * ring // 2), ring * ring // 2, 1)
    base = base.transpose(0, 2, 1, 3).reshape(2, piece, width)

    def second(a, b):
        a, b = (v.reshape(*v.shape[:-2], ring, piece, v.shape[-1]) for v in (a, b))
        a = total(spread([a[..., i, :, :] for i in range(ring)], LZ))
        b = total(spread([b[..., i, :, :] for i in range(ring)], LX))
        return jnp.stack([a, b])

    x_part = second(x_a, x_b)
    x_sum = x_part[:, 0]
    for k in range(1, layers):
        x_sum = x_sum + send_up(x_part[:, k].astype(BF16), k).astype(F32)

    y_a, y_b = (v.reshape(ring, ring * piece, cols) for v in (y_sum[:tok], y_sum[tok:]))
    y_a, y_b = (total(spread(list(v), d)).astype(BF16) for v, d in ((y_a, LX), (y_b, LZ)))
    rebuilt = jnp.concatenate([second(y_a, y_b), x_sum], 2)
    errors = ((rebuilt + base) * scale).astype(BF16)

    y_err, x_err = errors[..., :cols], errors[..., cols:]
    a = jnp.concatenate(gathered(jnp.concatenate(gathered(y_err[0], LZ), 0), LX), 0)
    b = jnp.concatenate(gathered(jnp.concatenate(gathered(y_err[1], LX), 0), LZ), 0)
    err_y = lax.all_gather(jnp.concatenate([a, b], 0)[None], LAYER, axis=0, tiled=True)
    x_all = jnp.stack([x_err] + [send_up(x_err, -k) for k in range(1, layers)], 1)
    a = gathered(jnp.concatenate(gathered(x_all[0], LZ), 1), LX)
    b = gathered(jnp.concatenate(gathered(x_all[1], LX), 1), LZ)

    dec_grad, own_act, other_act, sums = grads(where, lat_t, weights, err_y, a + b, width, ring)
    act = own_act + swap(other_act)
    pre_grad = jax.vjp(smooth, pre)[1](act)[0].astype(BF16)

    ordered = mine_first(inputs)
    own_in = lax.dynamic_slice_in_dim(ordered, c * width, width, 1)
    other_in = swap(lax.dynamic_slice_in_dim(ordered, (1 - c) * width, width, 1))
    both_in = jnp.concatenate([own_in, other_in], 0)
    both_grad = jnp.concatenate([pre_grad, swap(pre_grad)], 0)
    enc_grad = lax.dot_general(
        both_in, both_grad, (((0,), (0,)), ((), ())), preferred_element_type=F32
    )
    own_sum = jnp.sum(pre_grad.astype(F32), axis=0, keepdims=True)
    enc_bias_grad = own_sum + swap(own_sum)
    both = turned(jnp.concatenate([sums, swap(sums)], 0), 0, c).reshape(1, model)
    size = dec_bias.shape[1]
    dec_bias_grad = lax.dynamic_slice_in_dim(both, (x * ring + z) * size, size, 1)
    return dec_grad[None], dec_bias_grad, enc_grad[None], enc_bias_grad


def solution(mesh):
    ring = math.isqrt(mesh.shape["latent"])
    shape = (mesh.shape["layer"], ring, ring, mesh.shape["tok"])
    fine = jax.sharding.Mesh(mesh.devices.reshape(shape), (LAYER, LX, LZ, TOK))
    latent = (LX, LZ)
    in_specs = (
        P(LAYER, TOK, None),
        P(LAYER, TOK, latent),
        P(LAYER, None, latent),
        P(LAYER, latent),
        P(LAYER, None, latent, None),
        P(LAYER, latent),
    )
    out_specs = (
        P(LAYER, None, latent, TOK),
        P(LAYER, latent),
        P(LAYER, TOK, latent),
        P(LAYER, latent),
    )
    return jax.shard_map(
        on_device, mesh=fine, in_specs=in_specs, out_specs=out_specs, check_vma=False
    )
```

time: 456 us -> 319 us (0.70)
  waiting for transfers between devices: 351 us -> 93.3 us
  starting transfers between devices: 0.34 us -> 122 us
  Pallas kernels: 0 us -> 42.5 us
  matrix products: 47.2 us -> 7.6 us
  local copies, waits for them, and re-layouts: 37.4 us -> 18.6 us
  other arithmetic: 1.96 us -> 14.8 us
    reduce_scatter x3 -> x1, waiting for transfers between devices: 268 us -> 0.01 us  [on_device(): y_sum = lax.psum_scatter(y_part, LAYER, scatter_dimension=0, tiled=True)[0]]
    ppermute x0 -> x67, starting transfers between devices: none -> 116 us  [the longest x54 75.9 us: shift(): return lax.ppermute(value, axis, [(i, (i + step) % n) for i in range(n)])]
    ppermute x0 -> x67, waiting for transfers between devices: none -> 93.2 us  [the longest x54 83.6 us: shift(): return lax.ppermute(value, axis, [(i, (i + step) % n) for i in range(n)])]
    all_gather x1, waiting for transfers between devices: 82.9 us -> 0.01 us  [on_device(): lax.all_gather(jnp.concatenate([a, b], 0)[None], LAYER, axis=0, tiled=True)]
    pallas_call x0 -> x4, Pallas kernels: none -> 42.5 us  [the longest x1 25.1 us: grads(): pl.pallas_call(functools.partial(grad_kernel, parts=parts, cols=cols, rin...]
    dot_general x5 -> x2, matrix products: 47.2 us -> 7.6 us  [the longest x1 4.55 us: on_device(): lax.dot_general(both_in, both_grad, (((0,), (0,)), ((), ())), preferred_e...]
    unnamed x15 -> x56, local copies, waits for them, and re-layouts: 27.4 us -> 6.1 us
    gather x1 -> x0, local copies, waits for them, and re-layouts: 10.1 us -> none  [on_device(): blocks = blocked[target, :, row_ids % shards, :]]
  transfers between devices with their start and end apart: 4 -> 70, of which waited for: 3 -> 32; matrix products, arithmetic and copies ran while one was open for 4% -> 6% of each run, Pallas kernels for 0% -> 3%
where the time goes in v1:
time: 319 us; the launch traced here: 314 us
  starting transfers between devices  122 us (38%)
  waiting for transfers between devices  93.3 us (29%)
  Pallas kernels  42.5 us (13%)
  local copies, waits for them, and re-layouts  18.6 us (6%)
  other arithmetic  14.8 us (5%)
  between operations  14.8 us (5%)
  matrix products  7.6 us (2%)
    ppermute x54, waiting for transfers between devices, shift(): return lax.ppermute(value, axis, [(i, (i + step) % n) for i in range(n)])  83.6 us
    ppermute x54, starting transfers between devices, shift(): return lax.ppermute(value, axis, [(i, (i + step) % n) for i in range(n)])  75.9 us
    ppermute x7, starting transfers between devices, swap(): return lax.ppermute(value, TOK, [(0, 1), (1, 0)])  26.8 us
    pallas_call x1, Pallas kernels, grads(): pl.pallas_call(functools.partial(grad_kernel, parts=parts, cols=cols, rin...  25.1 us
    ppermute x6, starting transfers between devices, send_up(): return lax.ppermute(value, LAYER, pairs)  13.7 us
    pallas_call x2, Pallas kernels, rebuild_x(): pl.pallas_call(functools.partial(x_kernel, cols=cols), out_shape=[jax.Sha...  10.5 us
    ppermute x6, waiting for transfers between devices, send_up(): return lax.ppermute(value, LAYER, pairs)  7.08 us
    pallas_call x1, Pallas kernels, rebuild_y(): pl.pallas_call(functools.partial(y_kernel, cols=cols), out_shape=jax.Shap...  6.98 us
  transfers between devices with their start and end apart: 70, of which 32 were waited for; matrix products, arithmetic and copies ran while one was open for 6% of the time, Pallas kernels for 3%

profile of v1, /device:TPU:1, one launch (start us, length us, event | category | flops | bytes accessed | tf_op | source)
XLA Modules:
  0.0 313.8 jit_solution(1520698803103277513)
XLA Ops:
  8.8 3.0 fusion.8
  18.1 7.0 %shard_map.93 = bf16[4,1024,384]{2,1,0:T(8,128)(2,1)} custom-call(s32[2]{0:T(128)} %pad_add_fusion.where, bf16[1024,512]{1,0:T(8,128)(2,1)} %copy.55.lat_ref, bf16[4,512,2304]{2,1,0:T(8,128)(2,1)} %bitcast.149), custom_call_target="tpu_custom_call" | custom-call | flops 1610612736 | bytes 10485760 | tf_op jit(solution)/shard_map/pallas_call | solution.py:83
  25.1 5.3 %shard_map.95 = (bf16[2,128,768]{2,1,0:T(8,128)(2,1)}, bf16[2,128,768]{2,1,0:T(8,128)(2,1)}, bf16[2,128,768]{2,1,0:T(8,128)(2,1)}, bf16[2,128,768]{2,1,0:T(8,128...) custom-call(s32[2]{0:T(128)} %pad_add_fusion.where, ...), custom_call_target="tpu_custom_call" | custom-call | flops 1610612736 | bytes 8388608 | tf_op jit(solution)/shard_map/pallas_call | solution.py:106
  30.4 1.7 collective-permute-start.25
  32.1 3.3 %collective-permute-start.26 = (bf16[2,128,768]{2,1,0:T(8,128)(2,1)}, bf16[2,128,768]{2,1,0:T(8,128)(2,1)}, u32[]{:S(2)}, u32[]{:S(2)}) collective-permute-start(bf16[2,128,768]{2,1,0:T(8,128)(2,1)} %get-tuple-element.41), channel_id=1, source_target_pairs={{0,4},{2,6},{4,0},{6,2},{1,5},{3,7},{5,1},{7,3},{8,12},{10,14},{12... | collective-permute-start | bytes 1179656 | tf_op jit(solution)/shard_map/ppermute | solution.py:21
  37.6 5.2 %shard_map.94 = (bf16[2,128,768]{2,1,0:T(8,128)(2,1)}, bf16[2,128,768]{2,1,0:T(8,128)(2,1)}, bf16[2,128,768]{2,1,0:T(8,128)(2,1)}, bf16[2,128,768]{2,1,0:T(8,128...) custom-call(s32[2]{0:T(128)} %pad_add_fusion.where, ...), custom_call_target="tpu_custom_call" | custom-call | flops 1610612736 | bytes 8388608 | tf_op jit(solution)/shard_map/pallas_call | solution.py:106
  44.2 1.9 collective-permute-start.24
  47.3 5.8 %all-to-all-start = ((f32[2,16,32,144]{3,2,0,1:T(8,128)}), f32[2,16,32,144]{3,2,0,1:T(8,128)S(1)}, u32[]{:S(2)}, u32[]{:S(2)}) async-start(f32[2,16,32,144]{3,2,0,1:T(8,128)} %copy.64), calls=%async_computation.1 | async-start | bytes 2097152 | tf_op jit(solution)/shard_map/all_to_all | solution.py:257
  54.6 2.4 collective-permute-start.17
  58.5 8.7 %collective-permute-done.22 = bf16[2,128,768]{2,1,0:T(8,128)(2,1)} collective-permute-done((bf16[2,128,768]{2,1,0:T(8,128)(2,1)}, bf16[2,128,768]{2,1,0:T(8,128)(2,1)}, u32[]{:S(2)}, u32[]{:S(2)}) %collective-permute-start.22) | collective-permute-done | bytes 393248 | tf_op jit(solution)/shard_map/ppermute | solution.py:21
  67.2 3.3 %collective-permute-start.18 = (bf16[2,128,768]{2,1,0:T(8,128)(2,1)}, bf16[2,128,768]{2,1,0:T(8,128)(2,1)S(1)}, u32[]{:S(2)}, u32[]{:S(2)}) collective-permute-start(bf16[2,128,768]{2,1,0:T(8,128)(2,1)} %get-tuple-element.34), channel_id=1, source_target_pairs={{0,24},{8,0},{16,8},{24,16},{1,25},{9,1},{17,9},{25,17},{2,26},{10... | collective-permute-start | bytes 1179656 | tf_op jit(solution)/shard_map/ppermute | solution.py:21
  70.5 9.2 %collective-permute-done.23 = bf16[2,128,768]{2,1,0:T(8,128)(2,1)} collective-permute-done((bf16[2,128,768]{2,1,0:T(8,128)(2,1)}, bf16[2,128,768]{2,1,0:T(8,128)(2,1)}, u32[]{:S(2)}, u32[]{:S(2)}) %collective-permute-start.23) | collective-permute-done | bytes 393248 | tf_op jit(solution)/shard_map/ppermute | solution.py:21
  80.0 2.3 collective-permute-start.14
  86.7 6.6 %collective-permute-done.13 = bf16[2,128,768]{2,1,0:T(8,128)(2,1)S(1)} collective-permute-done((bf16[2,128,768]{2,1,0:T(8,128)(2,1)}, bf16[2,128,768]{2,1,0:T(8,128)(2,1)S(1)}, u32[]{:S(2)}, u32[]{:S(2)}) %collective-permute-start.13) | collective-permute-done | bytes 393248 | tf_op jit(solution)/shard_map/ppermute | solution.py:21
  93.6 7.1 %collective-permute-done.14 = bf16[2,128,768]{2,1,0:T(8,128)(2,1)S(1)} collective-permute-done((bf16[2,128,768]{2,1,0:T(8,128)(2,1)}, bf16[2,128,768]{2,1,0:T(8,128)(2,1)S(1)}, u32[]{:S(2)}, u32[]{:S(2)}) %collective-permute-start.14) | collective-permute-done | bytes 393248 | tf_op jit(solution)/shard_map/ppermute | solution.py:21
  100.7 1.6 collective-permute-done.15
  102.7 1.9 collective-permute-start.20
  106.6 2.5 collective-permute-done.29
  111.9 3.0 collective-permute-start.31
  114.9 5.0 %collective-permute-start.32 = (bf16[2,32,768]{2,1,0:T(8,128)(2,1)}, bf16[2,32,768]{2,1,0:T(8,128)(2,1)}, u32[]{:S(2)}, u32[]{:S(2)}) collective-permute-start(bf16[2,32,768]{2,1,0:T(8,128)(2,1)} %get-tuple-element.70), channel_id=1, source_target_pairs={{0,64},{32,96},{1,65},{33,97},{2,66},{34,98},{3,67},{35,99},{4,68}... | collective-permute-start | bytes 294920 | tf_op jit(solution)/shard_map/ppermute | solution.py:27
  119.9 1.9 collective-permute-start.33
  121.8 1.8 slice_bitcast_fusion.11
  123.6 4.3 %collective-permute-start.1 = (bf16[128,384]{1,0:T(8,128)(2,1)S(1)}, bf16[128,384]{1,0:T(8,128)(2,1)S(1)}, u32[]{:S(2)}, u32[]{:S(2)}) collective-permute-start(bf16[128,384]{1,0:T(8,128)(2,1)S(1)} %get-tuple-element.54), channel_id=1, source_target_pairs={{0,8},{8,16},{16,24},{24,0},{1,9},{9,17},{17,25},{25,1},{2,10},{10... | collective-permute-start | bytes 294920 | tf_op jit(solution)/shard_map/ppermute | solution.py:21
  129.6 2.0 collective-permute-start.2
  132.0 2.8 collective-permute-start.7
  142.7 2.6 collective-permute-start.5
  147.5 2.4 collective-permute-start.12
  149.9 1.7 collective-permute-done.11
  151.6 2.3 collective-permute-start.41
  154.0 2.6 collective-permute-start.36
  158.2 2.3 collective-permute-done.37
  160.5 1.7 collective-permute-start.38
  177.3 3.1 collective-permute-done.48
  180.4 2.5 collective-permute-done.49
  183.0 12.1 %collective-permute-start.56 = (bf16[4,32,768]{2,1,0:T(8,128)(2,1)S(1)}, bf16[4,32,768]{2,1,0:T(8,128)(2,1)S(1)}, u32[]{:S(2)}, u32[]{:S(2)}) collective-permute-start(bf16[4,32,768]{2,1,0:T(8,128)(2,1)S(1)} %get-tuple-element.66), channel_id=1, source_target_pairs={{0,24},{8,0},{16,8},{24,16},{1,25},{9,1},{17,9},{25,17},{2,26},{10... | collective-permute-start | bytes 589832 | tf_op jit(solution)/shard_map/ppermute | solution.py:21
  195.8 4.1 %collective-permute-done.56 = bf16[4,32,768]{2,1,0:T(8,128)(2,1)S(1)} collective-permute-done((bf16[4,32,768]{2,1,0:T(8,128)(2,1)S(1)}, bf16[4,32,768]{2,1,0:T(8,128)(2,1)S(1)}, u32[]{:S(2)}, u32[]{:S(2)}) %collective-permute-start.56) | collective-permute-done | bytes 196640 | tf_op jit(solution)/shard_map/ppermute | solution.py:21
  201.3 2.4 collective-permute-done.58
  204.8 2.3 collective-permute-start.51
  207.1 2.7 collective-permute-start.60
  209.8 7.4 %collective-permute-done.50 = bf16[4,32,768]{2,1,0:T(8,128)(2,1)S(1)} collective-permute-done((bf16[4,32,768]{2,1,0:T(8,128)(2,1)S(1)}, bf16[4,32,768]{2,1,0:T(8,128)(2,1)S(1)}, u32[]{:S(2)}, u32[]{:S(2)}) %collective-permute-start.50) | collective-permute-done | bytes 196640 | tf_op jit(solution)/shard_map/ppermute | solution.py:21
  218.9 2.6 collective-permute-done.60.refs_6_
  221.4 14.4 %collective-permute-done.61.refs_7_ = bf16[4,128,768]{2,1,0:T(8,128)(2,1)S(1)} collective-permute-done((bf16[4,128,768]{2,1,0:T(8,128)(2,1)S(1)}, bf16[4,128,768]{2,1,0:T(8,128)(2,1)S(1)}, u32[]{:S(2)}, u32[]{:S(2)}) %collective-permute-start.61) | collective-permute-done | bytes 786464 | tf_op jit(solution)/shard_map/ppermute | solution.py:21
  238.7 25.1 %shard_map.96 = (f32[4,512,1152]{2,1,0:T(8,128)}, f32[512,512]{1,0:T(8,128)}, f32[512,512]{1,0:T(8,128)}, f32[1,1152]{1,0:T(1,128)}) custom-call(s32[2]{0:T(128)} %pad_add_fusion.where, bf16[512,1024]{1,0:T(8,128)(2,1)} %bitcast.155, bf16[4,512,2304]{2,1,0:T(8,128)(2,1)} %bitcast.152, bf16[4,1024,384]{2,1,0:T(8,128)(2,1)} %bitcast.178, ...), custom_call_target="tpu_custom_call" | custom-call | flops 9663676416 | bytes 41943040 | tf_op jit(solution)/shard_map/pallas_call | solution.py:186
  263.8 2.5 copy.69
  266.4 22.9 %collective-permute-start.64 = (f32[512,512]{0,1:T(8,128)}, f32[512,512]{0,1:T(8,128)}, u32[]{:S(2)}, u32[]{:S(2)}) collective-permute-start(f32[512,512]{0,1:T(8,128)} %copy.69), channel_id=1, source_target_pairs={{0,1},{1,0},{2,3},{3,2},{4,5},{5,4},{6,7},{7,6},{8,9},{9,8},{10,11... | collective-permute-start | bytes 3145736 | tf_op jit(solution)/shard_map/ppermute | solution.py:31
  289.3 2.5 fusion.1
  295.6 2.8 convert_reduce_fusion
  302.2 4.6 %convolution_bitcast_fusion = f32[1,1152,512]{2,1,0:T(8,128)} fusion(bf16[512,1152]{1,0:T(8,128)(2,1)} %collective-permute-done.63, bf16[512,1152]{1,0:T(8,128)(2,1)S(1)} %get-tuple-element.50, bf16[512,512]{0,1:T(8,128)(2,1)} %collective-permute-done.65, bf16[512,512]{0,1:T(8,128)(2,1)} %get-tuple-element.49), kind=kOutput, calls=%fused_computation.4 | convolution fusion | flops 1214775296 | bytes 5767168 | tf_op jit(solution)/shard_map/dot_general | solution.py:294
  (208 shorter events, 69.9 us)
Async XLA Ops:
  7.2 114.6 %reduce-scatter.2.cloned.1.call-start = ((), (), s32[]{:S(2)}) async-start(), calls=%async_computation.2 | async-start | bytes 3932160 | tf_op jit(solution)/shard_map/reduce_scatter | solution.py:243
  30.4 13.7 %collective-permute-start.25 = (bf16[2,128,768]{2,1,0:T(8,128)(2,1)}, bf16[2,128,768]{2,1,0:T(8,128)(2,1)}, u32[]{:S(2)}, u32[]{:S(2)}) collective-permute-start(bf16[2,128,768]{2,1,0:T(8,128)(2,1)} %get-tuple-element.40), channel_id=1, source_target_pairs={{0,2},{2,4},{4,6},{6,0},{1,3},{3,5},{5,7},{7,1},{8,10},{10,12},{12... | collective-permute-start | bytes 1179656 | tf_op jit(solution)/shard_map/ppermute | solution.py:21
  32.1 21.0 %collective-permute-start.26 = (bf16[2,128,768]{2,1,0:T(8,128)(2,1)}, bf16[2,128,768]{2,1,0:T(8,128)(2,1)}, u32[]{:S(2)}, u32[]{:S(2)}) collective-permute-start(bf16[2,128,768]{2,1,0:T(8,128)(2,1)} %get-tuple-element.41), channel_id=1, source_target_pairs={{0,4},{2,6},{4,0},{6,2},{1,5},{3,7},{5,1},{7,3},{8,12},{10,14},{12... | collective-permute-start | bytes 1179656 | tf_op jit(solution)/shard_map/ppermute | solution.py:21
  35.4 19.2 %collective-permute-start.27 = (bf16[2,128,768]{2,1,0:T(8,128)(2,1)}, bf16[2,128,768]{2,1,0:T(8,128)(2,1)}, u32[]{:S(2)}, u32[]{:S(2)}) collective-permute-start(bf16[2,128,768]{2,1,0:T(8,128)(2,1)} %get-tuple-element.42), channel_id=1, source_target_pairs={{0,6},{2,0},{4,2},{6,4},{1,7},{3,1},{5,3},{7,5},{8,14},{10,8},{12,... | collective-permute-start | bytes 1179656 | tf_op jit(solution)/shard_map/ppermute | solution.py:21
  36.3 7.2 %collective-permute-start.34 = (bf16[16,32,144]{2,1,0:T(8,128)(2,1)S(1)}, bf16[16,32,144]{2,1,0:T(8,128)(2,1)S(1)}, u32[]{:S(2)}, u32[]{:S(2)}) collective-permute-start(bf16[16,32,144]{2,1,0:T(8,128)(2,1)S(1)} %bitcast.168), channel_id=1, source_target_pairs={{0,1},{1,0},{2,3},{3,2},{4,5},{5,4},{6,7},{7,6},{8,9},{9,8},{10,11... | collective-permute-start | bytes 442376 | tf_op jit(solution)/shard_map/ppermute | solution.py:31
  42.8 24.3 %collective-permute-start.22 = (bf16[2,128,768]{2,1,0:T(8,128)(2,1)}, bf16[2,128,768]{2,1,0:T(8,128)(2,1)}, u32[]{:S(2)}, u32[]{:S(2)}) collective-permute-start(bf16[2,128,768]{2,1,0:T(8,128)(2,1)} %get-tuple-element.36), channel_id=1, source_target_pairs={{0,2},{2,4},{4,6},{6,0},{1,3},{3,5},{5,7},{7,1},{8,10},{10,12},{12... | collective-permute-start | bytes 1179656 | tf_op jit(solution)/shard_map/ppermute | solution.py:21
  43.6 36.1 %collective-permute-start.23 = (bf16[2,128,768]{2,1,0:T(8,128)(2,1)}, bf16[2,128,768]{2,1,0:T(8,128)(2,1)}, u32[]{:S(2)}, u32[]{:S(2)}) collective-permute-start(bf16[2,128,768]{2,1,0:T(8,128)(2,1)} %get-tuple-element.37), channel_id=1, source_target_pairs={{0,4},{2,6},{4,0},{6,2},{1,5},{3,7},{5,1},{7,3},{8,12},{10,14},{12... | collective-permute-start | bytes 1179656 | tf_op jit(solution)/shard_map/ppermute | solution.py:21
  44.2 35.8 %collective-permute-start.24 = (bf16[2,128,768]{2,1,0:T(8,128)(2,1)}, bf16[2,128,768]{2,1,0:T(8,128)(2,1)}, u32[]{:S(2)}, u32[]{:S(2)}) collective-permute-start(bf16[2,128,768]{2,1,0:T(8,128)(2,1)} %get-tuple-element.38), channel_id=1, source_target_pairs={{0,6},{2,0},{4,2},{6,4},{1,7},{3,1},{5,3},{7,5},{8,14},{10,8},{12,... | collective-permute-start | bytes 1179656 | tf_op jit(solution)/shard_map/ppermute | solution.py:21
  47.3 90.6 %all-to-all-start = ((f32[2,16,32,144]{3,2,0,1:T(8,128)}), f32[2,16,32,144]{3,2,0,1:T(8,128)S(1)}, u32[]{:S(2)}, u32[]{:S(2)}) async-start(f32[2,16,32,144]{3,2,0,1:T(8,128)} %copy.64), calls=%async_computation.1 | async-start | bytes 2097152 | tf_op jit(solution)/shard_map/all_to_all | solution.py:257
  53.1 185.6 %all-gather.3.cloned.1.call-start = ((), (), s32[]{:S(2)}) async-start(), calls=%async_computation.3 | async-start | bytes 3932160 | tf_op jit(solution)/shard_map/all_gather | solution.py:280
  53.2 30.6 %collective-permute-start.16 = (bf16[2,128,768]{2,1,0:T(8,128)(2,1)}, bf16[2,128,768]{2,1,0:T(8,128)(2,1)S(1)}, u32[]{:S(2)}, u32[]{:S(2)}) collective-permute-start(bf16[2,128,768]{2,1,0:T(8,128)(2,1)} %get-tuple-element.32), channel_id=1, source_target_pairs={{0,8},{8,16},{16,24},{24,0},{1,9},{9,17},{17,25},{25,1},{2,10},{10... | collective-permute-start | bytes 1179656 | tf_op jit(solution)/shard_map/ppermute | solution.py:21
  54.6 30.7 %collective-permute-start.17 = (bf16[2,128,768]{2,1,0:T(8,128)(2,1)}, bf16[2,128,768]{2,1,0:T(8,128)(2,1)S(1)}, u32[]{:S(2)}, u32[]{:S(2)}) collective-permute-start(bf16[2,128,768]{2,1,0:T(8,128)(2,1)} %get-tuple-element.33), channel_id=1, source_target_pairs={{0,16},{8,24},{16,0},{24,8},{1,17},{9,25},{17,1},{25,9},{2,18},{10... | collective-permute-start | bytes 1179656 | tf_op jit(solution)/shard_map/ppermute | solution.py:21
  67.2 18.3 %collective-permute-start.18 = (bf16[2,128,768]{2,1,0:T(8,128)(2,1)}, bf16[2,128,768]{2,1,0:T(8,128)(2,1)S(1)}, u32[]{:S(2)}, u32[]{:S(2)}) collective-permute-start(bf16[2,128,768]{2,1,0:T(8,128)(2,1)} %get-tuple-element.34), channel_id=1, source_target_pairs={{0,24},{8,0},{16,8},{24,16},{1,25},{9,1},{17,9},{25,17},{2,26},{10... | collective-permute-start | bytes 1179656 | tf_op jit(solution)/shard_map/ppermute | solution.py:21
  79.7 13.7 %collective-permute-start.13 = (bf16[2,128,768]{2,1,0:T(8,128)(2,1)}, bf16[2,128,768]{2,1,0:T(8,128)(2,1)S(1)}, u32[]{:S(2)}, u32[]{:S(2)}) collective-permute-start(bf16[2,128,768]{2,1,0:T(8,128)(2,1)} %get-tuple-element.28), channel_id=1, source_target_pairs={{0,8},{8,16},{16,24},{24,0},{1,9},{9,17},{17,25},{25,1},{2,10},{10... | collective-permute-start | bytes 1179656 | tf_op jit(solution)/shard_map/ppermute | solution.py:21
  80.0 20.7 %collective-permute-start.14 = (bf16[2,128,768]{2,1,0:T(8,128)(2,1)}, bf16[2,128,768]{2,1,0:T(8,128)(2,1)S(1)}, u32[]{:S(2)}, u32[]{:S(2)}) collective-permute-start(bf16[2,128,768]{2,1,0:T(8,128)(2,1)} %get-tuple-element.29), channel_id=1, source_target_pairs={{0,16},{8,24},{16,0},{24,8},{1,17},{9,25},{17,1},{25,9},{2,18},{10... | collective-permute-start | bytes 1179656 | tf_op jit(solution)/shard_map/ppermute | solution.py:21
  83.8 18.5 %collective-permute-start.15 = (bf16[2,128,768]{2,1,0:T(8,128)(2,1)S(1)}, bf16[2,128,768]{2,1,0:T(8,128)(2,1)S(1)}, u32[]{:S(2)}, u32[]{:S(2)}) collective-permute-start(bf16[2,128,768]{2,1,0:T(8,128)(2,1)S(1)} %copy-done.20), channel_id=1, source_target_pairs={{0,24},{8,0},{16,8},{24,16},{1,25},{9,1},{17,9},{25,17},{2,26},{10... | collective-permute-start | bytes 1179656 | tf_op jit(solution)/shard_map/ppermute | solution.py:21
  85.3 20.6 %collective-permute-start.28 = (bf16[4,32,768]{2,1,0:T(8,128)(2,1)S(1)}, bf16[4,32,768]{2,1,0:T(8,128)(2,1)S(1)}, u32[]{:S(2)}, u32[]{:S(2)}) collective-permute-start(bf16[4,32,768]{2,1,0:T(8,128)(2,1)S(1)} %get-tuple-element.60), channel_id=1, source_target_pairs={{0,8},{8,16},{16,24},{24,0},{1,9},{9,17},{17,25},{25,1},{2,10},{10... | collective-permute-start | bytes 589832 | tf_op jit(solution)/shard_map/ppermute | solution.py:21
  85.5 23.7 %collective-permute-start.29 = (bf16[4,32,768]{2,1,0:T(8,128)(2,1)S(1)}, bf16[4,32,768]{2,1,0:T(8,128)(2,1)S(1)}, u32[]{:S(2)}, u32[]{:S(2)}) collective-permute-start(bf16[4,32,768]{2,1,0:T(8,128)(2,1)S(1)} %get-tuple-element.62), channel_id=1, source_target_pairs={{0,16},{8,24},{16,0},{24,8},{1,17},{9,25},{17,1},{25,9},{2,18},{10... | collective-permute-start | bytes 589832 | tf_op jit(solution)/shard_map/ppermute | solution.py:21
  93.3 15.8 %collective-permute-start.30 = (bf16[4,32,768]{2,1,0:T(8,128)(2,1)S(1)}, bf16[4,32,768]{2,1,0:T(8,128)(2,1)S(1)}, u32[]{:S(2)}, u32[]{:S(2)}) collective-permute-start(bf16[4,32,768]{2,1,0:T(8,128)(2,1)S(1)} %get-tuple-element.61), channel_id=1, source_target_pairs={{0,24},{8,0},{16,8},{24,16},{1,25},{9,1},{17,9},{25,17},{2,26},{10... | collective-permute-start | bytes 589832 | tf_op jit(solution)/shard_map/ppermute | solution.py:21
  102.6 8.2 %collective-permute-start.19 = (bf16[4,32,768]{2,1,0:T(8,128)(2,1)S(1)}, bf16[4,32,768]{2,1,0:T(8,128)(2,1)S(1)}, u32[]{:S(2)}, u32[]{:S(2)}) collective-permute-start(bf16[4,32,768]{2,1,0:T(8,128)(2,1)S(1)} %get-tuple-element.63), channel_id=1, source_target_pairs={{0,2},{2,4},{4,6},{6,0},{1,3},{3,5},{5,7},{7,1},{8,10},{10,12},{12... | collective-permute-start | bytes 589832 | tf_op jit(solution)/shard_map/ppermute | solution.py:21
  102.7 8.1 %collective-permute-start.20 = (bf16[4,32,768]{2,1,0:T(8,128)(2,1)S(1)}, bf16[4,32,768]{2,1,0:T(8,128)(2,1)S(1)}, u32[]{:S(2)}, u32[]{:S(2)}) collective-permute-start(bf16[4,32,768]{2,1,0:T(8,128)(2,1)S(1)} %get-tuple-element.65), channel_id=1, source_target_pairs={{0,4},{2,6},{4,0},{6,2},{1,5},{3,7},{5,1},{7,3},{8,12},{10,14},{12... | collective-permute-start | bytes 589832 | tf_op jit(solution)/shard_map/ppermute | solution.py:21
  111.9 15.9 %collective-permute-start.31 = (bf16[2,32,768]{2,1,0:T(8,128)(2,1)}, bf16[2,32,768]{2,1,0:T(8,128)(2,1)S(1)}, u32[]{:S(2)}, u32[]{:S(2)}) collective-permute-start(bf16[2,32,768]{2,1,0:T(8,128)(2,1)} %get-tuple-element.68), channel_id=1, source_target_pairs={{0,32},{32,64},{64,96},{1,33},{33,65},{65,97},{2,34},{34,66},{66,9... | collective-permute-start | bytes 294920 | tf_op jit(solution)/shard_map/ppermute | solution.py:27
  114.9 13.0 %collective-permute-start.32 = (bf16[2,32,768]{2,1,0:T(8,128)(2,1)}, bf16[2,32,768]{2,1,0:T(8,128)(2,1)}, u32[]{:S(2)}, u32[]{:S(2)}) collective-permute-start(bf16[2,32,768]{2,1,0:T(8,128)(2,1)} %get-tuple-element.70), channel_id=1, source_target_pairs={{0,64},{32,96},{1,65},{33,97},{2,66},{34,98},{3,67},{35,99},{4,68}... | collective-permute-start | bytes 294920 | tf_op jit(solution)/shard_map/ppermute | solution.py:27
  119.9 8.7 %collective-permute-start.33 = (bf16[2,32,768]{2,1,0:T(8,128)(2,1)S(1)}, bf16[2,32,768]{2,1,0:T(8,128)(2,1)}, u32[]{:S(2)}, u32[]{:S(2)}) collective-permute-start(bf16[2,32,768]{2,1,0:T(8,128)(2,1)S(1)} %get-tuple-element.69), channel_id=1, source_target_pairs={{0,96},{1,97},{2,98},{3,99},{4,100},{5,101},{6,102},{7,103},{8,104... | collective-permute-start | bytes 294920 | tf_op jit(solution)/shard_map/ppermute | solution.py:27
  123.6 12.4 %collective-permute-start.1 = (bf16[128,384]{1,0:T(8,128)(2,1)S(1)}, bf16[128,384]{1,0:T(8,128)(2,1)S(1)}, u32[]{:S(2)}, u32[]{:S(2)}) collective-permute-start(bf16[128,384]{1,0:T(8,128)(2,1)S(1)} %get-tuple-element.54), channel_id=1, source_target_pairs={{0,8},{8,16},{16,24},{24,0},{1,9},{9,17},{17,25},{25,1},{2,10},{10... | collective-permute-start | bytes 294920 | tf_op jit(solution)/shard_map/ppermute | solution.py:21
  129.6 9.0 %collective-permute-start.2 = (bf16[128,384]{1,0:T(8,128)(2,1)}, bf16[128,384]{1,0:T(8,128)(2,1)}, u32[]{:S(2)}, u32[]{:S(2)}) collective-permute-start(bf16[128,384]{1,0:T(8,128)(2,1)} %get-tuple-element.59), channel_id=1, source_target_pairs={{0,16},{8,24},{16,0},{24,8},{1,17},{9,25},{17,1},{25,9},{2,18},{10... | collective-permute-start | bytes 294920 | tf_op jit(solution)/shard_map/ppermute | solution.py:21
  131.6 6.9 %collective-permute-start.3 = (bf16[128,384]{1,0:T(8,128)(2,1)S(1)}, bf16[128,384]{1,0:T(8,128)(2,1)}, u32[]{:S(2)}, u32[]{:S(2)}) collective-permute-start(bf16[128,384]{1,0:T(8,128)(2,1)S(1)} %get-tuple-element.58), channel_id=1, source_target_pairs={{0,24},{8,0},{16,8},{24,16},{1,25},{9,1},{17,9},{25,17},{2,26},{10... | collective-permute-start | bytes 294920 | tf_op jit(solution)/shard_map/ppermute | solution.py:21
  132.0 6.5 %collective-permute-start.7 = (bf16[128,384]{1,0:T(8,128)(2,1)S(1)}, bf16[128,384]{1,0:T(8,128)(2,1)}, u32[]{:S(2)}, u32[]{:S(2)}) collective-permute-start(bf16[128,384]{1,0:T(8,128)(2,1)S(1)} %get-tuple-element.57), channel_id=1, source_target_pairs={{0,2},{2,4},{4,6},{6,0},{1,3},{3,5},{5,7},{7,1},{8,10},{10,12},{12... | collective-permute-start | bytes 294920 | tf_op jit(solution)/shard_map/ppermute | solution.py:21
  142.7 7.2 %collective-permute-start.5 = (bf16[32,384]{1,0:T(8,128)(2,1)S(1)}, bf16[32,384]{1,0:T(8,128)(2,1)S(1)}, u32[]{:S(2)}, u32[]{:S(2)}) collective-permute-start(bf16[32,384]{1,0:T(8,128)(2,1)S(1)} %get-tuple-element.77), channel_id=1, source_target_pairs={{0,4},{2,6},{4,0},{6,2},{1,5},{3,7},{5,1},{7,3},{8,12},{10,14},{12... | collective-permute-start | bytes 73736 | tf_op jit(solution)/shard_map/ppermute | solution.py:21
  151.6 12.0 %collective-permute-start.41 = (bf16[32,384]{1,0:T(8,128)(2,1)S(1)}, bf16[32,384]{1,0:T(8,128)(2,1)S(1)}, u32[]{:S(2)}, u32[]{:S(2)}) collective-permute-start(bf16[32,384]{1,0:T(8,128)(2,1)S(1)} %get-tuple-element.73), channel_id=1, source_target_pairs={{0,24},{8,0},{16,8},{24,16},{1,25},{9,1},{17,9},{25,17},{2,26},{10... | collective-permute-start | bytes 73736 | tf_op jit(solution)/shard_map/ppermute | solution.py:21
  153.9 10.5 %collective-permute-start.42 = (bf16[32,384]{1,0:T(8,128)(2,1)S(1)}, bf16[32,384]{1,0:T(8,128)(2,1)S(1)}, u32[]{:S(2)}, u32[]{:S(2)}) collective-permute-start(bf16[32,384]{1,0:T(8,128)(2,1)S(1)} %get-tuple-element.73), channel_id=1, source_target_pairs={{0,16},{8,24},{16,0},{24,8},{1,17},{9,25},{17,1},{25,9},{2,18},{10... | collective-permute-start | bytes 73736 | tf_op jit(solution)/shard_map/ppermute | solution.py:21
  156.9 7.5 %collective-permute-start.43 = (bf16[32,384]{1,0:T(8,128)(2,1)S(1)}, bf16[32,384]{1,0:T(8,128)(2,1)S(1)}, u32[]{:S(2)}, u32[]{:S(2)}) collective-permute-start(bf16[32,384]{1,0:T(8,128)(2,1)S(1)} %get-tuple-element.73), channel_id=1, source_target_pairs={{0,8},{8,16},{16,24},{24,0},{1,9},{9,17},{17,25},{25,1},{2,10},{10... | collective-permute-start | bytes 73736 | tf_op jit(solution)/shard_map/ppermute | solution.py:21
  173.3 7.2 %collective-permute-start.48 = (bf16[2,32,768]{2,1,0:T(8,128)(2,1)S(1)}, bf16[2,32,768]{2,1,0:T(8,128)(2,1)S(1)}, u32[]{:S(2)}, u32[]{:S(2)}) collective-permute-start(bf16[2,32,768]{2,1,0:T(8,128)(2,1)S(1)} %get-tuple-element.72), channel_id=1, source_target_pairs={{64,0},{96,32},{65,1},{97,33},{66,2},{98,34},{67,3},{99,35},{68,4}... | collective-permute-start | bytes 294920 | tf_op jit(solution)/shard_map/ppermute | solution.py:27
  174.6 8.4 %collective-permute-start.49 = (bf16[2,32,768]{2,1,0:T(8,128)(2,1)S(1)}, bf16[2,32,768]{2,1,0:T(8,128)(2,1)S(1)}, u32[]{:S(2)}, u32[]{:S(2)}) collective-permute-start(bf16[2,32,768]{2,1,0:T(8,128)(2,1)S(1)} %get-tuple-element.72), channel_id=1, source_target_pairs={{96,0},{97,1},{98,2},{99,3},{100,4},{101,5},{102,6},{103,7},{104,8... | collective-permute-start | bytes 294920 | tf_op jit(solution)/shard_map/ppermute | solution.py:27
  183.0 16.8 %collective-permute-start.56 = (bf16[4,32,768]{2,1,0:T(8,128)(2,1)S(1)}, bf16[4,32,768]{2,1,0:T(8,128)(2,1)S(1)}, u32[]{:S(2)}, u32[]{:S(2)}) collective-permute-start(bf16[4,32,768]{2,1,0:T(8,128)(2,1)S(1)} %get-tuple-element.66), channel_id=1, source_target_pairs={{0,24},{8,0},{16,8},{24,16},{1,25},{9,1},{17,9},{25,17},{2,26},{10... | collective-permute-start | bytes 589832 | tf_op jit(solution)/shard_map/ppermute | solution.py:21
  195.2 6.1 %collective-permute-start.57 = (bf16[4,32,768]{2,1,0:T(8,128)(2,1)S(1)}, bf16[4,32,768]{2,1,0:T(8,128)(2,1)S(1)}, u32[]{:S(2)}, u32[]{:S(2)}) collective-permute-start(bf16[4,32,768]{2,1,0:T(8,128)(2,1)S(1)} %get-tuple-element.66), channel_id=1, source_target_pairs={{0,16},{8,24},{16,0},{24,8},{1,17},{9,25},{17,1},{25,9},{2,18},{10... | collective-permute-start | bytes 589832 | tf_op jit(solution)/shard_map/ppermute | solution.py:21
  195.6 8.1 %collective-permute-start.58 = (bf16[4,32,768]{2,1,0:T(8,128)(2,1)S(1)}, bf16[4,32,768]{2,1,0:T(8,128)(2,1)S(1)}, u32[]{:S(2)}, u32[]{:S(2)}) collective-permute-start(bf16[4,32,768]{2,1,0:T(8,128)(2,1)S(1)} %get-tuple-element.66), channel_id=1, source_target_pairs={{0,8},{8,16},{16,24},{24,0},{1,9},{9,17},{17,25},{25,1},{2,10},{10... | collective-permute-start | bytes 589832 | tf_op jit(solution)/shard_map/ppermute | solution.py:21
  203.8 14.3 %collective-permute-start.59 = (bf16[4,128,768]{2,1,0:T(8,128)(2,1)S(1)}, bf16[4,128,768]{2,1,0:T(8,128)(2,1)S(1)}, u32[]{:S(2)}, u32[]{:S(2)}) collective-permute-start(bf16[4,128,768]{2,1,0:T(8,128)(2,1)S(1)} %pad_maximum_fusion.3.refs_4_), channel_id=1, source_target_pairs={{0,6},{2,0},{4,2},{6,4},{1,7},{3,1},{5,3},{7,5},{8,14},{10,8},{12,... | collective-permute-start | bytes 2359304 | tf_op jit(solution)/shard_map/ppermute | solution.py:21
  204.7 12.4 %collective-permute-start.50 = (bf16[4,32,768]{2,1,0:T(8,128)(2,1)S(1)}, bf16[4,32,768]{2,1,0:T(8,128)(2,1)S(1)}, u32[]{:S(2)}, u32[]{:S(2)}) collective-permute-start(bf16[4,32,768]{2,1,0:T(8,128)(2,1)S(1)} %get-tuple-element.67), channel_id=1, source_target_pairs={{0,6},{2,0},{4,2},{6,4},{1,7},{3,1},{5,3},{7,5},{8,14},{10,8},{12,... | collective-permute-start | bytes 589832 | tf_op jit(solution)/shard_map/ppermute | solution.py:21
  204.8 12.4 %collective-permute-start.51 = (bf16[4,32,768]{2,1,0:T(8,128)(2,1)S(1)}, bf16[4,32,768]{2,1,0:T(8,128)(2,1)S(1)}, u32[]{:S(2)}, u32[]{:S(2)}) collective-permute-start(bf16[4,32,768]{2,1,0:T(8,128)(2,1)S(1)} %get-tuple-element.67), channel_id=1, source_target_pairs={{0,4},{2,6},{4,0},{6,2},{1,5},{3,7},{5,1},{7,3},{8,12},{10,14},{12... | collective-permute-start | bytes 589832 | tf_op jit(solution)/shard_map/ppermute | solution.py:21
  207.1 10.1 %collective-permute-start.52 = (bf16[4,32,768]{2,1,0:T(8,128)(2,1)S(1)}, bf16[4,32,768]{2,1,0:T(8,128)(2,1)S(1)}, u32[]{:S(2)}, u32[]{:S(2)}) collective-permute-start(bf16[4,32,768]{2,1,0:T(8,128)(2,1)S(1)} %get-tuple-element.67), channel_id=1, source_target_pairs={{0,2},{2,4},{4,6},{6,0},{1,3},{3,5},{5,7},{7,1},{8,10},{10,12},{12... | collective-permute-start | bytes 589832 | tf_op jit(solution)/shard_map/ppermute | solution.py:21
  207.1 14.4 %collective-permute-start.60 = (bf16[4,128,768]{2,1,0:T(8,128)(2,1)S(1)}, bf16[4,128,768]{2,1,0:T(8,128)(2,1)S(1)}, u32[]{:S(2)}, u32[]{:S(2)}) collective-permute-start(bf16[4,128,768]{2,1,0:T(8,128)(2,1)S(1)} %pad_maximum_fusion.3.refs_4_), channel_id=1, source_target_pairs={{0,4},{2,6},{4,0},{6,2},{1,5},{3,7},{5,1},{7,3},{8,12},{10,14},{12... | collective-permute-start | bytes 2359304 | tf_op jit(solution)/shard_map/ppermute | solution.py:21
  217.2 18.7 %collective-permute-start.61 = (bf16[4,128,768]{2,1,0:T(8,128)(2,1)S(1)}, bf16[4,128,768]{2,1,0:T(8,128)(2,1)S(1)}, u32[]{:S(2)}, u32[]{:S(2)}) collective-permute-start(bf16[4,128,768]{2,1,0:T(8,128)(2,1)S(1)} %pad_maximum_fusion.3.refs_4_), channel_id=1, source_target_pairs={{0,2},{2,4},{4,6},{6,0},{1,3},{3,5},{5,7},{7,1},{8,10},{10,12},{12... | collective-permute-start | bytes 2359304 | tf_op jit(solution)/shard_map/ppermute | solution.py:21
  217.3 18.6 %collective-permute-start.53 = (bf16[4,128,768]{2,1,0:T(8,128)(2,1)S(1)}, bf16[4,128,768]{2,1,0:T(8,128)(2,1)S(1)}, u32[]{:S(2)}, u32[]{:S(2)}) collective-permute-start(bf16[4,128,768]{2,1,0:T(8,128)(2,1)S(1)} %pad_maximum_fusion.2.refs_0_), channel_id=1, source_target_pairs={{0,24},{8,0},{16,8},{24,16},{1,25},{9,1},{17,9},{25,17},{2,26},{10... | collective-permute-start | bytes 2359304 | tf_op jit(solution)/shard_map/ppermute | solution.py:21
  217.7 18.2 %collective-permute-start.54 = (bf16[4,128,768]{2,1,0:T(8,128)(2,1)S(1)}, bf16[4,128,768]{2,1,0:T(8,128)(2,1)S(1)}, u32[]{:S(2)}, u32[]{:S(2)}) collective-permute-start(bf16[4,128,768]{2,1,0:T(8,128)(2,1)S(1)} %pad_maximum_fusion.2.refs_0_), channel_id=1, source_target_pairs={{0,16},{8,24},{16,0},{24,8},{1,17},{9,25},{17,1},{25,9},{2,18},{10... | collective-permute-start | bytes 2359304 | tf_op jit(solution)/shard_map/ppermute | solution.py:21
  218.1 20.7 %collective-permute-start.55 = (bf16[4,128,768]{2,1,0:T(8,128)(2,1)S(1)}, bf16[4,128,768]{2,1,0:T(8,128)(2,1)}, u32[]{:S(2)}, u32[]{:S(2)}) collective-permute-start(bf16[4,128,768]{2,1,0:T(8,128)(2,1)S(1)} %pad_maximum_fusion.2.refs_0_), channel_id=1, source_target_pairs={{0,8},{8,16},{16,24},{24,0},{1,9},{9,17},{17,25},{25,1},{2,10},{10... | collective-permute-start | bytes 2359304 | tf_op jit(solution)/shard_map/ppermute | solution.py:21
  266.4 29.2 %collective-permute-start.64 = (f32[512,512]{0,1:T(8,128)}, f32[512,512]{0,1:T(8,128)}, u32[]{:S(2)}, u32[]{:S(2)}) collective-permute-start(f32[512,512]{0,1:T(8,128)} %copy.69), channel_id=1, source_target_pairs={{0,1},{1,0},{2,3},{3,2},{4,5},{5,4},{6,7},{7,6},{8,9},{9,8},{10,11... | collective-permute-start | bytes 3145736 | tf_op jit(solution)/shard_map/ppermute | solution.py:31
  293.9 8.4 %collective-permute-start.63 = (bf16[512,1152]{1,0:T(8,128)(2,1)}, bf16[512,1152]{1,0:T(8,128)(2,1)}, u32[]{:S(2)}, u32[]{:S(2)}) collective-permute-start(bf16[512,1152]{1,0:T(8,128)(2,1)} %get-tuple-element.51), channel_id=1, source_target_pairs={{0,1},{1,0},{2,3},{3,2},{4,5},{5,4},{6,7},{7,6},{8,9},{9,8},{10,11... | collective-permute-start | bytes 3538952 | tf_op jit(solution)/shard_map/ppermute | solution.py:31
  (43 other events, 353.2 us)
Sparse Core Ops, SparseCore 0:
  25.3 39.8 reduce-scatter.1
  172.1 48.8 all-gather.2

commit v2 on v0

v2 whole, which is shorter than its diff:
```python
import functools
import math

import jax
import jax.numpy as jnp
from jax import lax
from jax.experimental import pallas as pl
from jax.experimental.pallas import tpu as pltpu
from jax.sharding import PartitionSpec as P

LAYER, LX, LZ, TOK = "layer", "lx", "lz", "tok"
BF16, F32 = jnp.bfloat16, jnp.float32


def smooth(values):
    return jax.nn.gelu(values, approximate=True)


def shift(value, axis, step):
    n = lax.axis_size(axis)
    return lax.ppermute(value, axis, [(i, (i + step) % n) for i in range(n)])


def send_up(value, step):
    n = lax.axis_size(LAYER)
    pairs = [(i, i + step) for i in range(n) if 0 <= i + step < n]
    return lax.ppermute(value, LAYER, pairs)


def swap(value):
    return lax.ppermute(value, TOK, [(0, 1), (1, 0)])


def turned(value, axis, by):
    n = value.shape[axis]
    return lax.dynamic_slice_in_dim(jnp.concatenate([value, value], axis), by, n, axis)


def total(values):
    return functools.reduce(jnp.add, [v.astype(F32) for v in values])


def spread(value, axis):
    return [value[0]] + [shift(value[k], axis, k) for k in range(1, len(value))]


def gathered(value, axis):
    n = lax.axis_size(axis)
    return [value] + [shift(value, axis, -k) for k in range(1, n)]


def ring_spread(own, up, down, far_up, far_down, axis):
    half = far_up.shape[1]
    from_below, from_above = shift(far_up, axis, 1), shift(far_down, axis, -1)
    up = jnp.concatenate([total([up[:, :half], from_below]).astype(BF16), up[:, half:]], 1)
    down = jnp.concatenate([down[:, :half], total([down[:, half:], from_above]).astype(BF16)], 1)
    return total([own, shift(up, axis, 1), shift(down, axis, -1)])


def ring_gather(value, axis):
    half = value.shape[1] // 2
    above, below = shift(value, axis, -1), shift(value, axis, 1)
    return [value, above, below], [
        shift(above[:, :half], axis, -1),
        shift(below[:, half:], axis, 1),
    ]


def call(kernel, where, inputs, in_specs, outs, out_specs, grid, scratch, flops, moved, aliases=None):
    return pl.pallas_call(
        kernel,
        out_shape=[jax.ShapeDtypeStruct(shape, dtype) for shape, dtype in outs],
        grid_spec=pltpu.PrefetchScalarGridSpec(
            num_scalar_prefetch=1,
            grid=(grid,),
            in_specs=in_specs,
            out_specs=out_specs,
            scratch_shapes=scratch,
        ),
        input_output_aliases=aliases or {},
        compiler_params=pltpu.CompilerParams(vmem_limit_bytes=56 * 2**20),
        cost_estimate=pl.CostEstimate(flops=flops, bytes_accessed=moved, transcendentals=0),
    )(where, *inputs)


def fixed(*shape):
    return pl.BlockSpec(shape, lambda k, w: (0,) * len(shape))


def each(*shape):
    return pl.BlockSpec(shape, lambda k, w: (k,) + (0,) * (len(shape) - 1))


def encode_kernel(where, in_ref, w_ref, bias_ref, pre_ref, lat_ref, acc_ref, *, ring):
    k = pl.program_id(0)

    @pl.when(k == 0)
    def _():
        acc_ref[...] = jnp.broadcast_to(bias_ref[...], acc_ref.shape)

    acc_ref[...] += jnp.dot(in_ref[...], w_ref[...], preferred_element_type=F32)

    @pl.when(k == pl.num_programs(0) - 1)
    def _():
        piece = acc_ref.shape[0] // (ring * ring)
        for i in range(ring):
            for j in range(ring):
                row = lax.rem(i + ring - where[2], ring) * ring + lax.rem(j + ring - where[3], ring)
                pre = acc_ref[(i * ring + j) * piece : (i * ring + j + 1) * piece, :]
                to = pl.ds(pl.multiple_of(row * piece, piece), piece)
                pre_ref[to, :] = pre
                lat_ref[to, :] = smooth(pre).astype(BF16)


def encode(where, inputs, weight, bias, ring, steps=3):
    rows, model = inputs.shape
    feats = weight.shape[1]
    return call(
        functools.partial(encode_kernel, ring=ring),
        where,
        (inputs, weight, bias),
        [
            pl.BlockSpec((rows, model // steps), lambda k, w: (0, k)),
            pl.BlockSpec((model // steps, feats), lambda k, w: (k, 0)),
            fixed(1, feats),
        ],
        [((rows, feats), F32), ((rows, feats), BF16)],
        [fixed(rows, feats), fixed(rows, feats)],
        steps,
        [pltpu.VMEM((rows, feats), F32)],
        2 * rows * model * feats,
        8 * 2**20,
    )


def rebuild_kernel(where, lat_ref, w_ref, own_ref, up_ref, down_ref, far_up_ref, far_down_ref):
    out = jnp.dot(lat_ref[...], w_ref[0], preferred_element_type=F32)
    n = own_ref.shape[1]
    own_ref[0] = out[:n]
    out = out.astype(BF16)
    up_ref[0] = out[n : 2 * n]
    far_up_ref[0] = out[2 * n : 2 * n + n // 2]
    far_down_ref[0] = out[2 * n + n // 2 : 3 * n]
    down_ref[0] = out[3 * n :]


def rebuild(where, lat, weights, width):
    layers, feats, _ = weights.shape
    rows = lat.shape[0]
    n = rows // 4
    return call(
        rebuild_kernel,
        where,
        (lat, weights),
        [
            fixed(rows, feats),
            pl.BlockSpec((1, feats, width), lambda k, w: (lax.rem(w[0] + k, layers), 0, w[1])),
        ],
        [((layers, n, width), F32)]
        + [((layers, n, width), BF16)] * 2
        + [((layers, n // 2, width), BF16)] * 2,
        [each(1, n, width)] * 3 + [each(1, n // 2, width)] * 2,
        layers,
        [],
        2 * layers * rows * feats * width,
        12 * 2**20,
    )


def near_kernel(where, lat_ref, w_ref, *refs):
    *x_refs, dec_ref, act_ref, sum_ref, err_ref = refs
    k = pl.program_id(0)
    live = where[0] + k < pl.num_programs(0)
    step = x_refs[0].shape[1]

    @pl.when(k == 0)
    def _():
        act_ref[...] = jnp.zeros_like(act_ref)

    @pl.when(live)
    def _():
        for i, x_ref in enumerate(x_refs):
            err_ref[i * step : (i + 1) * step, :] = x_ref[0]
        dec_ref[0] = lax.dot_general(
            lat_ref[...], err_ref[...], (((0,), (0,)), ((), ())), preferred_element_type=F32
        )
        for i in range(0, err_ref.shape[0], 256):
            act_ref[i : i + 256, :] += lax.dot_general(
                err_ref[i : i + 256, :], w_ref[0], (((1,), (1,)), ((), ())), preferred_element_type=F32
            )

    @pl.when(jnp.logical_not(live))
    def _():
        dec_ref[0] = jnp.zeros_like(dec_ref[0])

    @pl.when(k == 0)
    def _():
        sum_ref[...] = jnp.sum(err_ref[...].astype(F32), axis=0, keepdims=True)


def far_kernel(where, lat_ref, w_ref, last_dec_ref, last_act_ref, last_sum_ref, *refs, ring):
    *x_refs, dec_ref, own_ref, other_ref, sum_ref, err_ref, act_ref = refs
    k = pl.program_id(0)
    live = where[0] + k < pl.num_programs(0)
    step = x_refs[0].shape[1]

    @pl.when(k == 0)
    def _():
        act_ref[...] = jnp.zeros_like(act_ref)

    @pl.when(live)
    def _():
        for i, x_ref in enumerate(x_refs):
            err_ref[i * step : (i + 1) * step, :] = x_ref[0]
        dec_ref[0] = last_dec_ref[0] + lax.dot_general(
            lat_ref[...], err_ref[...], (((0,), (0,)), ((), ())), preferred_element_type=F32
        )
        act_ref[...] += lax.dot_general(
            err_ref[...], w_ref[0], (((1,), (1,)), ((), ())), preferred_element_type=F32
        )

    @pl.when(jnp.logical_not(live))
    def _():
        dec_ref[0] = jnp.zeros_like(dec_ref[0])

    @pl.when(k == 0)
    def _():
        sum_ref[...] = last_sum_ref[...] + jnp.sum(err_ref[...].astype(F32), axis=0, keepdims=True)

    @pl.when(k == pl.num_programs(0) - 1)
    def _():
        n = act_ref.shape[0] // 2
        piece = n // ring
        for side in range(2):
            for i in range(ring):
                ref, at = {
                    0: (last_act_ref, 3 * n * side),
                    1: (last_act_ref, 3 * n * side + n),
                    2: (act_ref, n * side),
                    3: (last_act_ref, 3 * n * side + 2 * n),
                }[i]
                if side == 0:
                    own_ref[i * n : (i + 1) * n, :] = ref[at : at + n, :]
                else:
                    for j in range(ring):
                        to = (j * ring + i) * piece
                        other_ref[to : to + piece, :] = ref[at + j * piece : at + (j + 1) * piece, :]


def grads(where, lat, weights, near, far, width, ring):
    layers, feats, _ = weights.shape
    n = near[0].shape[1]
    blocks = [lat[i * n : (i + 1) * n] for i in range(2 * ring)]
    first = jnp.concatenate([blocks[i] for i in (0, 1, 3, 4, 5, 7)], 0)
    second = jnp.concatenate([blocks[2], blocks[6]], 0)
    target = pl.BlockSpec((1, feats, width), lambda k, w: (lax.rem(w[0] + k, layers), 0, w[1]))
    placed = pl.BlockSpec((1, feats, width), lambda k, w: (lax.rem(w[0] + k, layers), 0, 0))
    dec, act, sums = call(
        near_kernel,
        where,
        (first, weights, *near),
        [fixed(6 * n, feats), target] + [each(1, n, width)] * 6,
        [((layers, feats, width), F32), ((6 * n, feats), F32), ((1, width), F32)],
        [placed, fixed(6 * n, feats), fixed(1, width)],
        layers,
        [pltpu.VMEM((6 * n, width), BF16)],
        4 * layers * 6 * n * feats * width,
        25 * 2**20,
    )
    return call(
        functools.partial(far_kernel, ring=ring),
        where,
        (second, weights, dec, act, sums, *far),
        [fixed(2 * n, feats), target, placed, fixed(6 * n, feats), fixed(1, width)]
        + [each(1, n // 2, width)] * 4,
        [((layers, feats, width), F32)] + [((4 * n, feats), F32)] * 2 + [((1, width), F32)],
        [placed, fixed(4 * n, feats), fixed(4 * n, feats), fixed(1, width)],
        layers,
        [pltpu.VMEM((2 * n, width), BF16), pltpu.VMEM((2 * n, feats), F32)],
        4 * layers * 2 * n * feats * width,
        30 * 2**20,
        {3: 0},
    )


def pre_grad_kernel(where, pre_ref, own_ref, other_ref, out_ref, sum_ref):
    back = jax.vjp(smooth, pre_ref[...])[1]
    grad = back(own_ref[...] + other_ref[...])[0].astype(BF16)
    out_ref[...] = grad
    sum_ref[...] = jnp.sum(grad.astype(F32), axis=0, keepdims=True)


def enc_kernel(where, in_ref, grad_ref, *refs):
    *last, out_ref = refs
    out = lax.dot_general(
        in_ref[...], grad_ref[...], (((0,), (0,)), ((), ())), preferred_element_type=F32
    )
    out_ref[...] = last[0][...] + out if last else out


def enc_add(where, inputs, grad, last=None, steps=3):
    rows, width = inputs.shape
    feats = grad.shape[1]
    tile = pl.BlockSpec((width // steps, feats), lambda k, w: (k, 0))
    more = [] if last is None else [last]
    return call(
        enc_kernel,
        where,
        (inputs, grad, *more),
        [pl.BlockSpec((rows, width // steps), lambda k, w: (0, k)), fixed(rows, feats)] + [tile] * len(more),
        [((width, feats), F32)],
        [tile],
        steps,
        [],
        2 * rows * width * feats,
        4 * 2**20,
        {3: 0} if more else None,
    )[0]


def on_device(resid_in, resid_out, enc_weight, enc_bias, dec_weight, dec_bias):
    s, x, z, c = (lax.axis_index(a) for a in (LAYER, LX, LZ, TOK))
    ring = lax.axis_size(LX)
    layers, feats, model = dec_weight.shape[1:]
    tok = resid_in.shape[1]
    width = model // 2
    piece = tok // (ring * ring)
    scale = 1.0 / math.sqrt(tok * lax.axis_size(TOK))
    where = jnp.stack([s, c, x, z]).astype(jnp.int32)
    inputs, weights = resid_in[0], dec_weight[0]

    def mine_first(rows):
        blocks = rows.reshape(ring, ring, piece, rows.shape[1])
        return turned(turned(blocks, 0, x), 1, z).reshape(rows.shape)

    def crossed(rows):
        blocks = rows.reshape(ring, ring, -1, rows.shape[1])
        return blocks.transpose(1, 0, 2, 3).reshape(rows.shape)

    pre, own_lat = encode(where, inputs, enc_weight[0], enc_bias, ring)
    other_lat = crossed(swap(own_lat))

    part_a = rebuild(where, own_lat, weights, width)
    part_b = rebuild(where, other_lat, weights, width)
    a, b = ring_spread(*part_a, LX), ring_spread(*part_b, LZ)

    out_in, _ = lax.optimization_barrier((resid_out[0], part_b[3]))
    own_base = out_in.reshape(ring * ring, piece, -1)
    base = jnp.stack([own_base, swap(own_base)]).astype(F32)
    base = lax.all_to_all(dec_bias[0] - base, (LX, LZ), 1, 1, tiled=True)
    base = lax.dynamic_slice_in_dim(base, c * (ring * ring // 2), ring * ring // 2, 1)
    base = base.transpose(0, 2, 1, 3).reshape(2, piece, width)

    a, b = (v.reshape(layers, ring, piece, width) for v in (a, b))
    a = total(spread([a[:, 0]] + [a[:, i].astype(BF16) for i in range(1, ring)], LZ))
    b = total(spread([b[:, 0]] + [b[:, i].astype(BF16) for i in range(1, ring)], LX))
    pieces = jnp.stack([a, b], 1)
    rebuilt = pieces[0] + base
    for k in range(1, layers):
        rebuilt = rebuilt + send_up(pieces[k].astype(BF16), k).astype(F32)
    errors = (rebuilt * scale).astype(BF16)

    errors = jnp.stack([errors] + [send_up(errors, -k) for k in range(1, layers)], 1)
    near_a, far_a = ring_gather(jnp.concatenate(gathered(errors[0], LZ), 1), LX)
    near_b, far_b = ring_gather(jnp.concatenate(gathered(errors[1], LX), 1), LZ)

    ordered = mine_first(inputs)
    own_in = lax.dynamic_slice_in_dim(ordered, c * width, width, 1)
    other_in = swap(lax.dynamic_slice_in_dim(ordered, (1 - c) * width, width, 1))
    lat = jnp.concatenate([own_lat, other_lat], 0)
    own_in, other_in, *near = lax.optimization_barrier((own_in, other_in, *near_a, *near_b))

    dec_grad, own_act, other_act, sums = grads(
        where, lat, weights, near, far_a + far_b, width, ring
    )
    pre_grad, own_sum = call(
        pre_grad_kernel,
        where,
        (pre, own_act, swap(other_act)),
        [fixed(tok, feats)] * 3,
        [((tok, feats), BF16), ((1, feats), F32)],
        [fixed(tok, feats), fixed(1, feats)],
        1,
        [],
        20 * tok * feats,
        4 * 2**20,
    )
    enc_grad = enc_add(where, own_in, pre_grad)
    enc_grad = enc_add(where, other_in, swap(pre_grad), enc_grad)
    enc_bias_grad = own_sum + swap(own_sum)
    both = turned(jnp.concatenate([sums, swap(sums)], 0), 0, c).reshape(1, model)
    size = dec_bias.shape[1]
    dec_bias_grad = lax.dynamic_slice_in_dim(both, (x * ring + z) * size, size, 1)
    return dec_grad[None], dec_bias_grad, enc_grad[None], enc_bias_grad


def solution(mesh):
    ring = math.isqrt(mesh.shape["latent"])
    shape = (mesh.shape["layer"], ring, ring, mesh.shape["tok"])
    fine = jax.sharding.Mesh(mesh.devices.reshape(shape), (LAYER, LX, LZ, TOK))
    latent = (LX, LZ)
    in_specs = (
        P(LAYER, TOK, None),
        P(LAYER, TOK, latent),
        P(LAYER, None, latent),
        P(LAYER, latent),
        P(LAYER, None, latent, None),
        P(LAYER, latent),
    )
    out_specs = (
        P(LAYER, None, latent, TOK),
        P(LAYER, latent),
        P(LAYER, TOK, latent),
        P(LAYER, latent),
    )
    return jax.shard_map(
        on_device, mesh=fine, in_specs=in_specs, out_specs=out_specs, check_vma=False
    )
```

time: 456 us -> 248 us (0.54)
  waiting for transfers between devices: 351 us -> 79.6 us
  starting transfers between devices: 0.34 us -> 68.5 us
  Pallas kernels: 0 us -> 64.3 us
  matrix products: 47.2 us -> 0 us
  local copies, waits for them, and re-layouts: 37.4 us -> 15.4 us
  other arithmetic: 1.96 us -> 17.3 us
  between operations: 13.8 us -> 1.21 us
    reduce_scatter x3 -> x0, waiting for transfers between devices: 268 us -> none  [the longest x1 239 us: on_device(): lax.psum_scatter(jnp.where(is_live, product, jnp.zeros_like(product)), ('...]
    all_gather x1 -> x0, waiting for transfers between devices: 82.9 us -> none  [on_device(): lax.all_gather(errors[None], ('layer', 'latent'), axis=0, tiled=True)]
    ppermute x0 -> x41, waiting for transfers between devices: none -> 79.6 us  [the longest x28 70.3 us: shift(): return lax.ppermute(value, axis, [(i, (i + step) % n) for i in range(n)])]
    pallas_call x0 -> x8, Pallas kernels: none -> 64.3 us  [call(): pl.pallas_call(kernel, out_shape=[jax.ShapeDtypeStruct(shape, dtype) for...]
    ppermute x0 -> x41, starting transfers between devices: none -> 63.1 us  [the longest x28 38.1 us: shift(): return lax.ppermute(value, axis, [(i, (i + step) % n) for i in range(n)])]
    dot_general x5 -> x0, matrix products: 47.2 us -> none  [the longest x1 14 us: on_device(): jnp.einsum('rkd,rfd->kf', err_rows, blocks, preferred_element_type=jnp.fl...]
    unnamed x15 -> x58, local copies, waits for them, and re-layouts: 27.4 us -> 4.45 us
    gather x1 -> x0, local copies, waits for them, and re-layouts: 10.1 us -> none  [on_device(): blocks = blocked[target, :, row_ids % shards, :]]
  transfers between devices with their start and end apart: 4 -> 42, of which waited for: 3 -> 16; matrix products, arithmetic and copies ran while one was open for 4% -> 10% of each run, Pallas kernels for 0% -> 14%
where the time goes in v2:
time: 248 us; the launch traced here: 246 us
  waiting for transfers between devices  79.6 us (32%)
  starting transfers between devices  68.5 us (28%)
  Pallas kernels  64.3 us (26%)
  other arithmetic  17.3 us (7%)
  local copies, waits for them, and re-layouts  15.4 us (6%)
    ppermute x28, waiting for transfers between devices, shift(): return lax.ppermute(value, axis, [(i, (i + step) % n) for i in range(n)])  70.3 us
    pallas_call x8, Pallas kernels, call(): pl.pallas_call(kernel, out_shape=[jax.ShapeDtypeStruct(shape, dtype) for...  64.3 us
    ppermute x28, starting transfers between devices, shift(): return lax.ppermute(value, axis, [(i, (i + step) % n) for i in range(n)])  38.1 us
    ppermute x6, starting transfers between devices, send_up(): return lax.ppermute(value, LAYER, pairs)  13.6 us
    ppermute x7, starting transfers between devices, swap(): return lax.ppermute(value, TOK, [(0, 1), (1, 0)])  11.4 us
    ppermute x6, waiting for transfers between devices, send_up(): return lax.ppermute(value, LAYER, pairs)  5.44 us
    all_to_all x1, starting transfers between devices, on_device(): base = lax.all_to_all(dec_bias[0] - base, (LX, LZ), 1, 1, tiled=True)  5.42 us
  transfers between devices with their start and end apart: 42, of which 16 were waited for; matrix products, arithmetic and copies ran while one was open for 10% of the time, Pallas kernels for 14%

profile of v2, /device:TPU:1, one launch (start us, length us, event | category | flops | bytes accessed | tf_op | source)
XLA Modules:
  0.0 246.3 jit_solution(11164903380086445126)
XLA Ops:
  1.2 6.2 %shard_map.93 = (f32[512,512]{1,0:T(8,128)}, bf16[512,512]{1,0:T(8,128)(2,1)}) custom-call(s32[4]{0:T(128)} %pad_add_fusion.where, bf16[512,2304]{1,0:T(8,128)(2,1)} %bitcast.112, bf16[2304,512]{1,0:T(8,128)(2,1)} %bitcast.120, f32[1,512]{1,0:T(1,128)} %bias_ref.1), custom_call_target="tpu_custom_call" | custom-call | flops 1207959552 | bytes 8388608 | tf_op jit(solution)/shard_map/pallas_call | solution.py:70
  7.4 1.4 collective-permute-start
  8.9 7.7 %shard_map.94 = (f32[4,128,1152]{2,1,0:T(8,128)}, bf16[4,128,1152]{2,1,0:T(8,128)(2,1)}, bf16[4,128,1152]{2,1,0:T(8,128)(2,1)}, bf16[4,64,1152]{2,1,0:T(8,128)(2,1)}, bf16[4,64,1152]{2,1,0:T(8,128)(2,1)}) custom-call(s32[4]{0:T(128)} %pad_add_fusion.where, bf16[512,512]{1,0:T(8,128)(2,1)} %get-tuple-element.34.lat_ref, bf16[4,512,2304]{2,1,0:T(8,128)(2,1)} %bitcast.105), custom_call_target="tpu_custom_call" | custom-call | flops 2415919104 | bytes 12582912 | tf_op jit(solution)/shard_map/pallas_call | solution.py:70
  16.5 2.6 %collective-permute-start.4 = (bf16[4,64,1152]{2,1,0:T(8,128)(2,1)}, bf16[4,64,1152]{2,1,0:T(8,128)(2,1)S(1)}, u32[]{:S(2)}, u32[]{:S(2)}) collective-permute-start(bf16[4,64,1152]{2,1,0:T(8,128)(2,1)} %get-tuple-element.39), channel_id=1, source_target_pairs={{0,24},{8,0},{16,8},{24,16},{1,25},{9,1},{17,9},{25,17},{2,26},{10... | collective-permute-start | bytes 1769480 | tf_op jit(solution)/shard_map/ppermute | solution.py:21
  22.4 7.5 %shard_map.95 = (f32[4,128,1152]{2,1,0:T(8,128)}, bf16[4,128,1152]{2,1,0:T(8,128)(2,1)}, bf16[4,128,1152]{2,1,0:T(8,128)(2,1)}, bf16[4,64,1152]{2,1,0:T(8,128)(2,1)}, bf16[4,64,1152]{2,1,0:T(8,128)(2,1)}) custom-call(s32[4]{0:T(128)} %pad_add_fusion.where, bf16[512,512]{1,0:T(8,128)(2,1)} %bitcast.118, bf16[4,512,2304]{2,1,0:T(8,128)(2,1)} %bitcast.106), custom_call_target="tpu_custom_call" | custom-call | flops 2415919104 | bytes 12582912 | tf_op jit(solution)/shard_map/pallas_call | solution.py:70
  29.9 1.7 collective-permute-start.9
  34.4 2.0 collective-permute-start.11
  37.8 3.0 %collective-permute-start.5 = (bf16[4,128,1152]{2,1,0:T(8,128)(2,1)}, bf16[4,128,1152]{2,1,0:T(8,128)(2,1)S(1)}, u32[]{:S(2)}, u32[]{:S(2)}) collective-permute-start(bf16[4,128,1152]{2,1,0:T(8,128)(2,1)} %pad_maximum_fusion.2), channel_id=1, source_target_pairs={{0,24},{8,0},{16,8},{24,16},{1,25},{9,1},{17,9},{25,17},{2,26},{10... | collective-permute-start | bytes 3538952 | tf_op jit(solution)/shard_map/ppermute | solution.py:21
  43.3 5.4 %all-to-all-start = ((f32[2,16,32,144]{3,2,0,1:T(8,128)}), f32[2,16,32,144]{3,2,0,1:T(8,128)S(1)}, u32[]{:S(2)}, u32[]{:S(2)}) async-start(f32[2,16,32,144]{3,2,0,1:T(8,128)} %copy.34), calls=%async_computation | async-start | bytes 2097152 | tf_op jit(solution)/shard_map/all_to_all | solution.py:350
  48.7 1.5 add_convert_fusion.1
  50.3 1.4 collective-permute-start.10
  53.1 1.5 collective-permute-start.12
  54.6 13.6 %collective-permute-done.5 = bf16[4,128,1152]{2,1,0:T(8,128)(2,1)S(1)} collective-permute-done((bf16[4,128,1152]{2,1,0:T(8,128)(2,1)}, bf16[4,128,1152]{2,1,0:T(8,128)(2,1)S(1)}, u32[]{:S(2)}, u32[]{:S(2)}) %collective-permute-start.5) | collective-permute-done | bytes 1179680 | tf_op jit(solution)/shard_map/ppermute | solution.py:21
  68.2 2.1 collective-permute-done.3
  70.4 1.8 convert_add_fusion.1
  72.5 2.5 %collective-permute-start.8 = (bf16[4,32,1152]{2,1,0:T(8,128)(2,1)S(1)}, bf16[4,32,1152]{2,1,0:T(8,128)(2,1)S(1)}, u32[]{:S(2)}, u32[]{:S(2)}) collective-permute-start(bf16[4,32,1152]{2,1,0:T(8,128)(2,1)S(1)} %get-tuple-element.70), channel_id=1, source_target_pairs={{0,6},{2,0},{4,2},{6,4},{1,7},{3,1},{5,3},{7,5},{8,14},{10,8},{12,... | collective-permute-start | bytes 884744 | tf_op jit(solution)/shard_map/ppermute | solution.py:21
  75.5 13.2 %collective-permute-done.10 = bf16[4,128,1152]{2,1,0:T(8,128)(2,1)S(1)} collective-permute-done((bf16[4,128,1152]{2,1,0:T(8,128)(2,1)S(1)}, bf16[4,128,1152]{2,1,0:T(8,128)(2,1)S(1)}, u32[]{:S(2)}, u32[]{:S(2)}) %collective-permute-start.10) | collective-permute-done | bytes 1179680 | tf_op jit(solution)/shard_map/ppermute | solution.py:21
  90.4 1.5 collective-permute-start.15
  92.0 3.4 %collective-permute-done.6 = bf16[4,32,1152]{2,1,0:T(8,128)(2,1)S(1)} collective-permute-done((bf16[4,32,1152]{2,1,0:T(8,128)(2,1)S(1)}, bf16[4,32,1152]{2,1,0:T(8,128)(2,1)S(1)}, u32[]{:S(2)}, u32[]{:S(2)}) %collective-permute-start.6) | collective-permute-done | bytes 294944 | tf_op jit(solution)/shard_map/ppermute | solution.py:21
  95.4 2.7 %collective-permute-start.14 = (bf16[4,32,1152]{2,1,0:T(8,128)(2,1)S(1)}, bf16[4,32,1152]{2,1,0:T(8,128)(2,1)S(1)}, u32[]{:S(2)}, u32[]{:S(2)}) collective-permute-start(bf16[4,32,1152]{2,1,0:T(8,128)(2,1)S(1)} %get-tuple-element.68), channel_id=1, source_target_pairs={{0,16},{8,24},{16,0},{24,8},{1,17},{9,25},{17,1},{25,9},{2,18},{10... | collective-permute-start | bytes 884744 | tf_op jit(solution)/shard_map/ppermute | solution.py:21
  98.0 3.0 %collective-permute-done.7 = bf16[4,32,1152]{2,1,0:T(8,128)(2,1)S(1)} collective-permute-done((bf16[4,32,1152]{2,1,0:T(8,128)(2,1)S(1)}, bf16[4,32,1152]{2,1,0:T(8,128)(2,1)S(1)}, u32[]{:S(2)}, u32[]{:S(2)}) %collective-permute-start.7) | collective-permute-done | bytes 294944 | tf_op jit(solution)/shard_map/ppermute | solution.py:21
  101.2 4.8 %collective-permute-done.14 = bf16[4,32,1152]{2,1,0:T(8,128)(2,1)S(1)} collective-permute-done((bf16[4,32,1152]{2,1,0:T(8,128)(2,1)S(1)}, bf16[4,32,1152]{2,1,0:T(8,128)(2,1)S(1)}, u32[]{:S(2)}, u32[]{:S(2)}) %collective-permute-start.14) | collective-permute-done | bytes 294944 | tf_op jit(solution)/shard_map/ppermute | solution.py:21
  106.9 3.9 %collective-permute-start.17 = (bf16[2,32,1152]{2,1,0:T(8,128)(2,1)}, bf16[2,32,1152]{2,1,0:T(8,128)(2,1)}, u32[]{:S(2)}, u32[]{:S(2)}) collective-permute-start(bf16[2,32,1152]{2,1,0:T(8,128)(2,1)} %get-tuple-element.74), channel_id=1, source_target_pairs={{0,32},{32,64},{64,96},{1,33},{33,65},{65,97},{2,34},{34,66},{66,9... | collective-permute-start | bytes 442376 | tf_op jit(solution)/shard_map/ppermute | solution.py:27
  110.8 2.7 %collective-permute-start.19 = (bf16[2,32,1152]{2,1,0:T(8,128)(2,1)}, bf16[2,32,1152]{2,1,0:T(8,128)(2,1)}, u32[]{:S(2)}, u32[]{:S(2)}) collective-permute-start(bf16[2,32,1152]{2,1,0:T(8,128)(2,1)} %get-tuple-element.75), channel_id=1, source_target_pairs={{0,96},{1,97},{2,98},{3,99},{4,100},{5,101},{6,102},{7,103},{8,104... | collective-permute-start | bytes 442376 | tf_op jit(solution)/shard_map/ppermute | solution.py:27
  113.5 3.1 %collective-permute-start.18 = (bf16[2,32,1152]{2,1,0:T(8,128)(2,1)}, bf16[2,32,1152]{2,1,0:T(8,128)(2,1)}, u32[]{:S(2)}, u32[]{:S(2)}) collective-permute-start(bf16[2,32,1152]{2,1,0:T(8,128)(2,1)} %get-tuple-element.76), channel_id=1, source_target_pairs={{0,64},{32,96},{1,65},{33,97},{2,66},{34,98},{3,67},{35,99},{4,68}... | collective-permute-start | bytes 442376 | tf_op jit(solution)/shard_map/ppermute | solution.py:27
  118.4 2.1 fusion.18
  121.8 1.3 collective-permute-start.21
  124.4 3.4 %collective-permute-done.22 = bf16[2,32,1152]{2,1,0:T(8,128)(2,1)S(1)} collective-permute-done((bf16[2,32,1152]{2,1,0:T(8,128)(2,1)}, bf16[2,32,1152]{2,1,0:T(8,128)(2,1)S(1)}, u32[]{:S(2)}, u32[]{:S(2)}) %collective-permute-start.22) | collective-permute-done | bytes 147488 | tf_op jit(solution)/shard_map/ppermute | solution.py:27
  127.8 1.6 collective-permute-done.21
  132.6 2.0 collective-permute-start.29
  135.1 1.8 collective-permute-start.24
  138.6 7.1 %collective-permute-done.24 = bf16[4,32,1152]{2,1,0:T(8,128)(2,1)} collective-permute-done((bf16[4,32,1152]{2,1,0:T(8,128)(2,1)S(1)}, bf16[4,32,1152]{2,1,0:T(8,128)(2,1)}, u32[]{:S(2)}, u32[]{:S(2)}) %collective-permute-start.24) | collective-permute-done | bytes 294944 | tf_op jit(solution)/shard_map/ppermute | solution.py:21
  145.7 1.3 collective-permute-done.23
  148.9 2.2 collective-permute-start.26
  152.2 1.4 constant_dynamic-slice_fusion.1
  153.6 7.3 %collective-permute-start.1 = (bf16[512,1152]{1,0:T(8,128)(2,1)S(1)}, bf16[512,1152]{1,0:T(8,128)(2,1)S(1)}, u32[]{:S(2)}, u32[]{:S(2)}) collective-permute-start(bf16[512,1152]{1,0:T(8,128)(2,1)S(1)} %get-tuple-element.64), channel_id=1, source_target_pairs={{0,1},{1,0},{2,3},{3,2},{4,5},{5,4},{6,7},{7,6},{8,9},{9,8},{10,11... | collective-permute-start | bytes 3538952 | tf_op jit(solution)/shard_map/ppermute | solution.py:31
  160.9 2.9 %collective-permute-start.31 = (bf16[4,128,1152]{2,1,0:T(8,128)(2,1)S(1)}, bf16[4,128,1152]{2,1,0:T(8,128)(2,1)S(1)}, u32[]{:S(2)}, u32[]{:S(2)}) collective-permute-start(bf16[4,128,1152]{2,1,0:T(8,128)(2,1)S(1)} %pad_maximum_fusion.6.refs_3_), channel_id=1, source_target_pairs={{0,6},{2,0},{4,2},{6,4},{1,7},{3,1},{5,3},{7,5},{8,14},{10,8},{12,... | collective-permute-start | bytes 3538952 | tf_op jit(solution)/shard_map/ppermute | solution.py:21
  165.0 6.4 %collective-permute-done.27.refs_2_ = bf16[4,128,1152]{2,1,0:T(8,128)(2,1)S(1)} collective-permute-done((bf16[4,128,1152]{2,1,0:T(8,128)(2,1)S(1)}, bf16[4,128,1152]{2,1,0:T(8,128)(2,1)S(1)}, u32[]{:S(2)}, u32[]{:S(2)}) %collective-permute-start.27) | collective-permute-done | bytes 1179680 | tf_op jit(solution)/shard_map/ppermute | solution.py:21
  172.4 1.9 collective-permute-start.33
  174.4 14.7 %collective-permute-done.31.refs_4_ = bf16[4,128,1152]{2,1,0:T(8,128)(2,1)S(1)} collective-permute-done((bf16[4,128,1152]{2,1,0:T(8,128)(2,1)S(1)}, bf16[4,128,1152]{2,1,0:T(8,128)(2,1)S(1)}, u32[]{:S(2)}, u32[]{:S(2)}) %collective-permute-start.31) | collective-permute-done | bytes 1179680 | tf_op jit(solution)/shard_map/ppermute | solution.py:21
  189.2 3.7 %collective-permute-start.35 = (bf16[4,64,1152]{2,1,0:T(8,128)(2,1)S(1)}, bf16[4,64,1152]{2,1,0:T(8,128)(2,1)S(1)}, u32[]{:S(2)}, u32[]{:S(2)}) collective-permute-start(bf16[4,64,1152]{2,1,0:T(8,128)(2,1)S(1)} %slice.180), channel_id=1, source_target_pairs={{0,6},{2,0},{4,2},{6,4},{1,7},{3,1},{5,3},{7,5},{8,14},{10,8},{12,... | collective-permute-start | bytes 1769480 | tf_op jit(solution)/shard_map/ppermute | solution.py:21
  192.9 15.0 %shard_map.96 = (f32[4,512,1152]{2,1,0:T(8,128)}, f32[768,512]{1,0:T(8,128)}, f32[1,1152]{1,0:T(1,128)}) custom-call(s32[4]{0:T(128)} %pad_add_fusion.where, bf16[768,512]{1,0:T(8,128)(2,1)} %copy-done.22, bf16[4,512,2304]{2,1,0:T(8,128)(2,1)} %bitcast.107, bf16[4,128,1152]{2,1,0:T(8,128)(2,1)} %copy-done.9, bf16[4,128,1152]{2,1,0:T(8,128)(2,1)} %copy-done.18, ...), custom_call_target="tpu_custom_call" | custom-call | flops 7247757312 | bytes 26214400 | tf_op jit(solution)/shard_map/pallas_call | solution.py:70
  209.3 13.3 %shard_map.97 = (f32[4,512,1152]{2,1,0:T(8,128)}, f32[512,512]{1,0:T(8,128)}, f32[512,512]{1,0:T(8,128)}, f32[1,1152]{1,0:T(1,128)}) custom-call(s32[4]{0:T(128)} %pad_add_fusion.where, bf16[256,512]{1,0:T(8,128)(2,1)} %pad_maximum_fusion.8.lat_ref, bf16[4,512,2304]{2,1,0:T(8,128)(2,1)} %bitcast.108, ...), custom_call_target="tpu_custom_call", output_to_operand_aliasing={{0}: (3, {})} | custom-call | flops 2415919104 | bytes 31457280 | tf_op jit(solution)/shard_map/pallas_call | solution.py:70
  223.9 2.5 %collective-permute-done.38.other_ref = f32[512,512]{1,0:T(8,128)S(1)} collective-permute-done((f32[512,512]{1,0:T(8,128)}, f32[512,512]{1,0:T(8,128)S(1)}, u32[]{:S(2)}, u32[]{:S(2)}) %collective-permute-start.38) | collective-permute-done | bytes 1048608 | tf_op jit(solution)/shard_map/ppermute | solution.py:31
  227.4 4.1 %shard_map.98 = (bf16[512,512]{1,0:T(8,128)(2,1)}, f32[1,512]{1,0:T(1,128)}) custom-call(s32[4]{0:T(128)} %pad_add_fusion.where, f32[512,512]{1,0:T(8,128)} %get-tuple-element.58.pre_ref, f32[512,512]{1,0:T(8,128)} %get-tuple-element.59.own_ref, f32[512,512]{1,0:T(8,128)} %copy-done.11), custom_call_target="tpu_custom_call" | custom-call | flops 5242880 | bytes 4194304 | tf_op jit(solution)/shard_map/pallas_call | solution.py:70
  232.0 1.4 collective-permute-done.37
  234.5 4.8 %shard_map.99.refs_0_ = f32[1152,512]{1,0:T(8,128)} custom-call(s32[4]{0:T(128)} %pad_add_fusion.where, bf16[512,1152]{1,0:T(8,128)(2,1)} %get-tuple-element.62.in_ref, bf16[512,512]{1,0:T(8,128)(2,1)} %get-tuple-element.61.grad_ref), custom_call_target="tpu_custom_call" | custom-call | flops 603979776 | bytes 4194304 | tf_op jit(solution)/shard_map/pallas_call | solution.py:70
  240.7 5.6 %shard_map.100 = f32[1152,512]{1,0:T(8,128)} custom-call(s32[4]{0:T(128)} %pad_add_fusion.where, bf16[512,1152]{1,0:T(8,128)(2,1)} %copy-done.5, bf16[512,512]{1,0:T(8,128)(2,1)} %copy-done.16, f32[1152,512]{1,0:T(8,128)} %shard_map.99.refs_0_), custom_call_target="tpu_custom_call", output_to_operand_aliasing={{}: (3, {})} | custom-call | flops 603979776 | bytes 4194304 | tf_op jit(solution)/shard_map/pallas_call | solution.py:70
  (147 shorter events, 37.1 us)
Async XLA Ops:
  7.4 14.0 %collective-permute-start = (bf16[512,512]{1,0:T(8,128)(2,1)}, bf16[512,512]{1,0:T(8,128)(2,1)S(1)}, u32[]{:S(2)}, u32[]{:S(2)}) collective-permute-start(bf16[512,512]{1,0:T(8,128)(2,1)} %get-tuple-element.34.lat_ref), channel_id=1, source_target_pairs={{0,1},{1,0},{2,3},{3,2},{4,5},{5,4},{6,7},{7,6},{8,9},{9,8},{10,11... | collective-permute-start | bytes 1572872 | tf_op jit(solution)/shard_map/ppermute | solution.py:31
  16.5 19.9 %collective-permute-start.4 = (bf16[4,64,1152]{2,1,0:T(8,128)(2,1)}, bf16[4,64,1152]{2,1,0:T(8,128)(2,1)S(1)}, u32[]{:S(2)}, u32[]{:S(2)}) collective-permute-start(bf16[4,64,1152]{2,1,0:T(8,128)(2,1)} %get-tuple-element.39), channel_id=1, source_target_pairs={{0,24},{8,0},{16,8},{24,16},{1,25},{9,1},{17,9},{25,17},{2,26},{10... | collective-permute-start | bytes 1769480 | tf_op jit(solution)/shard_map/ppermute | solution.py:21
  19.1 21.6 %collective-permute-start.2 = (bf16[4,64,1152]{2,1,0:T(8,128)(2,1)}, bf16[4,64,1152]{2,1,0:T(8,128)(2,1)S(1)}, u32[]{:S(2)}, u32[]{:S(2)}) collective-permute-start(bf16[4,64,1152]{2,1,0:T(8,128)(2,1)} %get-tuple-element.37), channel_id=1, source_target_pairs={{0,8},{8,16},{16,24},{24,0},{1,9},{9,17},{17,25},{25,1},{2,10},{10... | collective-permute-start | bytes 1769480 | tf_op jit(solution)/shard_map/ppermute | solution.py:21
  29.9 18.8 %collective-permute-start.9 = (bf16[4,64,1152]{2,1,0:T(8,128)(2,1)}, bf16[4,64,1152]{2,1,0:T(8,128)(2,1)}, u32[]{:S(2)}, u32[]{:S(2)}) collective-permute-start(bf16[4,64,1152]{2,1,0:T(8,128)(2,1)} %get-tuple-element.42), channel_id=1, source_target_pairs={{0,2},{2,4},{4,6},{6,0},{1,3},{3,5},{5,7},{7,1},{8,10},{10,12},{12... | collective-permute-start | bytes 1769480 | tf_op jit(solution)/shard_map/ppermute | solution.py:21
  31.6 10.4 %collective-permute-start.16 = (bf16[16,32,144]{2,1,0:T(8,128)(2,1)S(1)}, bf16[16,32,144]{2,1,0:T(8,128)(2,1)S(1)}, u32[]{:S(2)}, u32[]{:S(2)}) collective-permute-start(bf16[16,32,144]{2,1,0:T(8,128)(2,1)S(1)} %bitcast.121), channel_id=1, source_target_pairs={{0,1},{1,0},{2,3},{3,2},{4,5},{5,4},{6,7},{7,6},{8,9},{9,8},{10,11... | collective-permute-start | bytes 442376 | tf_op jit(solution)/shard_map/ppermute | solution.py:31
  34.4 17.3 %collective-permute-start.11 = (bf16[4,64,1152]{2,1,0:T(8,128)(2,1)}, bf16[4,64,1152]{2,1,0:T(8,128)(2,1)}, u32[]{:S(2)}, u32[]{:S(2)}) collective-permute-start(bf16[4,64,1152]{2,1,0:T(8,128)(2,1)} %get-tuple-element.44), channel_id=1, source_target_pairs={{0,6},{2,0},{4,2},{6,4},{1,7},{3,1},{5,3},{7,5},{8,14},{10,8},{12,... | collective-permute-start | bytes 1769480 | tf_op jit(solution)/shard_map/ppermute | solution.py:21
  37.8 30.4 %collective-permute-start.5 = (bf16[4,128,1152]{2,1,0:T(8,128)(2,1)}, bf16[4,128,1152]{2,1,0:T(8,128)(2,1)S(1)}, u32[]{:S(2)}, u32[]{:S(2)}) collective-permute-start(bf16[4,128,1152]{2,1,0:T(8,128)(2,1)} %pad_maximum_fusion.2), channel_id=1, source_target_pairs={{0,24},{8,0},{16,8},{24,16},{1,25},{9,1},{17,9},{25,17},{2,26},{10... | collective-permute-start | bytes 3538952 | tf_op jit(solution)/shard_map/ppermute | solution.py:21
  42.0 28.3 %collective-permute-start.3 = (bf16[4,128,1152]{2,1,0:T(8,128)(2,1)}, bf16[4,128,1152]{2,1,0:T(8,128)(2,1)}, u32[]{:S(2)}, u32[]{:S(2)}) collective-permute-start(bf16[4,128,1152]{2,1,0:T(8,128)(2,1)} %pad_maximum_fusion.1), channel_id=1, source_target_pairs={{0,8},{8,16},{16,24},{24,0},{1,9},{9,17},{17,25},{25,1},{2,10},{10... | collective-permute-start | bytes 3538952 | tf_op jit(solution)/shard_map/ppermute | solution.py:21
  43.3 73.4 %all-to-all-start = ((f32[2,16,32,144]{3,2,0,1:T(8,128)}), f32[2,16,32,144]{3,2,0,1:T(8,128)S(1)}, u32[]{:S(2)}, u32[]{:S(2)}) async-start(f32[2,16,32,144]{3,2,0,1:T(8,128)} %copy.34), calls=%async_computation | async-start | bytes 2097152 | tf_op jit(solution)/shard_map/all_to_all | solution.py:350
  50.3 20.0 %copy-start.3 = (f32[4,128,1152]{2,1,0:T(8,128)S(1)}, f32[4,128,1152]{2,1,0:T(8,128)}, u32[]{:S(2)}) copy-start(f32[4,128,1152]{2,1,0:T(8,128)} %get-tuple-element.35) | copy-start | bytes 7077892
  50.3 38.4 %collective-permute-start.10 = (bf16[4,128,1152]{2,1,0:T(8,128)(2,1)S(1)}, bf16[4,128,1152]{2,1,0:T(8,128)(2,1)S(1)}, u32[]{:S(2)}, u32[]{:S(2)}) collective-permute-start(bf16[4,128,1152]{2,1,0:T(8,128)(2,1)S(1)} %pad_maximum_fusion.3), channel_id=1, source_target_pairs={{0,2},{2,4},{4,6},{6,0},{1,3},{3,5},{5,7},{7,1},{8,10},{10,12},{12... | collective-permute-start | bytes 3538952 | tf_op jit(solution)/shard_map/ppermute | solution.py:21
  53.1 35.6 %collective-permute-start.12 = (bf16[4,128,1152]{2,1,0:T(8,128)(2,1)S(1)}, bf16[4,128,1152]{2,1,0:T(8,128)(2,1)S(1)}, u32[]{:S(2)}, u32[]{:S(2)}) collective-permute-start(bf16[4,128,1152]{2,1,0:T(8,128)(2,1)S(1)} %pad_maximum_fusion.4), channel_id=1, source_target_pairs={{0,6},{2,0},{4,2},{6,4},{1,7},{3,1},{5,3},{7,5},{8,14},{10,8},{12,... | collective-permute-start | bytes 3538952 | tf_op jit(solution)/shard_map/ppermute | solution.py:21
  70.4 18.4 %copy-start.2 = (f32[4,128,1152]{2,1,0:T(8,128)S(1)}, f32[4,128,1152]{2,1,0:T(8,128)}, u32[]{:S(2)}) copy-start(f32[4,128,1152]{2,1,0:T(8,128)} %get-tuple-element.40) | copy-start | bytes 7077892
  72.3 23.1 %collective-permute-start.6 = (bf16[4,32,1152]{2,1,0:T(8,128)(2,1)S(1)}, bf16[4,32,1152]{2,1,0:T(8,128)(2,1)S(1)}, u32[]{:S(2)}, u32[]{:S(2)}) collective-permute-start(bf16[4,32,1152]{2,1,0:T(8,128)(2,1)S(1)} %get-tuple-element.69), channel_id=1, source_target_pairs={{0,2},{2,4},{4,6},{6,0},{1,3},{3,5},{5,7},{7,1},{8,10},{10,12},{12... | collective-permute-start | bytes 884744 | tf_op jit(solution)/shard_map/ppermute | solution.py:21
  72.5 25.5 %collective-permute-start.8 = (bf16[4,32,1152]{2,1,0:T(8,128)(2,1)S(1)}, bf16[4,32,1152]{2,1,0:T(8,128)(2,1)S(1)}, u32[]{:S(2)}, u32[]{:S(2)}) collective-permute-start(bf16[4,32,1152]{2,1,0:T(8,128)(2,1)S(1)} %get-tuple-element.70), channel_id=1, source_target_pairs={{0,6},{2,0},{4,2},{6,4},{1,7},{3,1},{5,3},{7,5},{8,14},{10,8},{12,... | collective-permute-start | bytes 884744 | tf_op jit(solution)/shard_map/ppermute | solution.py:21
  75.0 26.0 %collective-permute-start.7 = (bf16[4,32,1152]{2,1,0:T(8,128)(2,1)S(1)}, bf16[4,32,1152]{2,1,0:T(8,128)(2,1)S(1)}, u32[]{:S(2)}, u32[]{:S(2)}) collective-permute-start(bf16[4,32,1152]{2,1,0:T(8,128)(2,1)S(1)} %get-tuple-element.71), channel_id=1, source_target_pairs={{0,4},{2,6},{4,0},{6,2},{1,5},{3,7},{5,1},{7,3},{8,12},{10,14},{12... | collective-permute-start | bytes 884744 | tf_op jit(solution)/shard_map/ppermute | solution.py:21
  89.2 11.9 %collective-permute-start.13 = (bf16[4,32,1152]{2,1,0:T(8,128)(2,1)S(1)}, bf16[4,32,1152]{2,1,0:T(8,128)(2,1)S(1)}, u32[]{:S(2)}, u32[]{:S(2)}) collective-permute-start(bf16[4,32,1152]{2,1,0:T(8,128)(2,1)S(1)} %get-tuple-element.66), channel_id=1, source_target_pairs={{0,8},{8,16},{16,24},{24,0},{1,9},{9,17},{17,25},{25,1},{2,10},{10... | collective-permute-start | bytes 884744 | tf_op jit(solution)/shard_map/ppermute | solution.py:21
  90.4 10.7 %collective-permute-start.15 = (bf16[4,32,1152]{2,1,0:T(8,128)(2,1)S(1)}, bf16[4,32,1152]{2,1,0:T(8,128)(2,1)S(1)}, u32[]{:S(2)}, u32[]{:S(2)}) collective-permute-start(bf16[4,32,1152]{2,1,0:T(8,128)(2,1)S(1)} %get-tuple-element.67), channel_id=1, source_target_pairs={{0,24},{8,0},{16,8},{24,16},{1,25},{9,1},{17,9},{25,17},{2,26},{10... | collective-permute-start | bytes 884744 | tf_op jit(solution)/shard_map/ppermute | solution.py:21
  95.4 10.6 %collective-permute-start.14 = (bf16[4,32,1152]{2,1,0:T(8,128)(2,1)S(1)}, bf16[4,32,1152]{2,1,0:T(8,128)(2,1)S(1)}, u32[]{:S(2)}, u32[]{:S(2)}) collective-permute-start(bf16[4,32,1152]{2,1,0:T(8,128)(2,1)S(1)} %get-tuple-element.68), channel_id=1, source_target_pairs={{0,16},{8,24},{16,0},{24,8},{1,17},{9,25},{17,1},{25,9},{2,18},{10... | collective-permute-start | bytes 884744 | tf_op jit(solution)/shard_map/ppermute | solution.py:21
  106.9 11.0 %collective-permute-start.17 = (bf16[2,32,1152]{2,1,0:T(8,128)(2,1)}, bf16[2,32,1152]{2,1,0:T(8,128)(2,1)}, u32[]{:S(2)}, u32[]{:S(2)}) collective-permute-start(bf16[2,32,1152]{2,1,0:T(8,128)(2,1)} %get-tuple-element.74), channel_id=1, source_target_pairs={{0,32},{32,64},{64,96},{1,33},{33,65},{65,97},{2,34},{34,66},{66,9... | collective-permute-start | bytes 442376 | tf_op jit(solution)/shard_map/ppermute | solution.py:27
  110.8 7.1 %collective-permute-start.19 = (bf16[2,32,1152]{2,1,0:T(8,128)(2,1)}, bf16[2,32,1152]{2,1,0:T(8,128)(2,1)}, u32[]{:S(2)}, u32[]{:S(2)}) collective-permute-start(bf16[2,32,1152]{2,1,0:T(8,128)(2,1)} %get-tuple-element.75), channel_id=1, source_target_pairs={{0,96},{1,97},{2,98},{3,99},{4,100},{5,101},{6,102},{7,103},{8,104... | collective-permute-start | bytes 442376 | tf_op jit(solution)/shard_map/ppermute | solution.py:27
  113.5 4.9 %collective-permute-start.18 = (bf16[2,32,1152]{2,1,0:T(8,128)(2,1)}, bf16[2,32,1152]{2,1,0:T(8,128)(2,1)}, u32[]{:S(2)}, u32[]{:S(2)}) collective-permute-start(bf16[2,32,1152]{2,1,0:T(8,128)(2,1)} %get-tuple-element.76), channel_id=1, source_target_pairs={{0,64},{32,96},{1,65},{33,97},{2,66},{34,98},{3,67},{35,99},{4,68}... | collective-permute-start | bytes 442376 | tf_op jit(solution)/shard_map/ppermute | solution.py:27
  118.0 12.6 %copy-start = (bf16[1,512,2304]{2,1,0:T(8,128)(2,1)S(1)}, bf16[1,512,2304]{2,1,0:T(8,128)(2,1)}, u32[]{:S(2)}) copy-start(bf16[1,512,2304]{2,1,0:T(8,128)(2,1)} %param.6) | copy-start | bytes 7077892
  120.5 7.3 %collective-permute-start.22 = (bf16[2,32,1152]{2,1,0:T(8,128)(2,1)}, bf16[2,32,1152]{2,1,0:T(8,128)(2,1)S(1)}, u32[]{:S(2)}, u32[]{:S(2)}) collective-permute-start(bf16[2,32,1152]{2,1,0:T(8,128)(2,1)} %fusion.18), channel_id=1, source_target_pairs={{96,0},{97,1},{98,2},{99,3},{100,4},{101,5},{102,6},{103,7},{104,8... | collective-permute-start | bytes 442376 | tf_op jit(solution)/shard_map/ppermute | solution.py:27
  121.8 7.6 %collective-permute-start.21 = (bf16[2,32,1152]{2,1,0:T(8,128)(2,1)}, bf16[2,32,1152]{2,1,0:T(8,128)(2,1)S(1)}, u32[]{:S(2)}, u32[]{:S(2)}) collective-permute-start(bf16[2,32,1152]{2,1,0:T(8,128)(2,1)} %fusion.18), channel_id=1, source_target_pairs={{64,0},{96,32},{65,1},{97,33},{66,2},{98,34},{67,3},{99,35},{68,4}... | collective-permute-start | bytes 442376 | tf_op jit(solution)/shard_map/ppermute | solution.py:27
  123.1 6.3 %collective-permute-start.20 = (bf16[2,32,1152]{2,1,0:T(8,128)(2,1)}, bf16[2,32,1152]{2,1,0:T(8,128)(2,1)S(1)}, u32[]{:S(2)}, u32[]{:S(2)}) collective-permute-start(bf16[2,32,1152]{2,1,0:T(8,128)(2,1)} %fusion.18), channel_id=1, source_target_pairs={{32,0},{64,32},{96,64},{33,1},{65,33},{97,65},{34,2},{66,34},{98,6... | collective-permute-start | bytes 442376 | tf_op jit(solution)/shard_map/ppermute | solution.py:27
  130.4 7.0 %collective-permute-start.25 = (bf16[4,32,1152]{2,1,0:T(8,128)(2,1)S(1)}, bf16[4,32,1152]{2,1,0:T(8,128)(2,1)}, u32[]{:S(2)}, u32[]{:S(2)}) collective-permute-start(bf16[4,32,1152]{2,1,0:T(8,128)(2,1)S(1)} %get-tuple-element.73), channel_id=1, source_target_pairs={{0,2},{2,4},{4,6},{6,0},{1,3},{3,5},{5,7},{7,1},{8,10},{10,12},{12... | collective-permute-start | bytes 884744 | tf_op jit(solution)/shard_map/ppermute | solution.py:21
  131.4 19.7 %collective-permute-start.30 = (bf16[4,32,1152]{2,1,0:T(8,128)(2,1)S(1)}, bf16[4,32,1152]{2,1,0:T(8,128)(2,1)S(1)}, u32[]{:S(2)}, u32[]{:S(2)}) collective-permute-start(bf16[4,32,1152]{2,1,0:T(8,128)(2,1)S(1)} %get-tuple-element.72), channel_id=1, source_target_pairs={{0,8},{8,16},{16,24},{24,0},{1,9},{9,17},{17,25},{25,1},{2,10},{10... | collective-permute-start | bytes 884744 | tf_op jit(solution)/shard_map/ppermute | solution.py:21
  132.6 18.4 %collective-permute-start.29 = (bf16[4,32,1152]{2,1,0:T(8,128)(2,1)S(1)}, bf16[4,32,1152]{2,1,0:T(8,128)(2,1)S(1)}, u32[]{:S(2)}, u32[]{:S(2)}) collective-permute-start(bf16[4,32,1152]{2,1,0:T(8,128)(2,1)S(1)} %get-tuple-element.72), channel_id=1, source_target_pairs={{0,16},{8,24},{16,0},{24,8},{1,17},{9,25},{17,1},{25,9},{2,18},{10... | collective-permute-start | bytes 884744 | tf_op jit(solution)/shard_map/ppermute | solution.py:21
  134.6 16.5 %collective-permute-start.28 = (bf16[4,32,1152]{2,1,0:T(8,128)(2,1)S(1)}, bf16[4,32,1152]{2,1,0:T(8,128)(2,1)}, u32[]{:S(2)}, u32[]{:S(2)}) collective-permute-start(bf16[4,32,1152]{2,1,0:T(8,128)(2,1)S(1)} %get-tuple-element.72), channel_id=1, source_target_pairs={{0,24},{8,0},{16,8},{24,16},{1,25},{9,1},{17,9},{25,17},{2,26},{10... | collective-permute-start | bytes 884744 | tf_op jit(solution)/shard_map/ppermute | solution.py:21
  135.1 10.6 %collective-permute-start.24 = (bf16[4,32,1152]{2,1,0:T(8,128)(2,1)S(1)}, bf16[4,32,1152]{2,1,0:T(8,128)(2,1)}, u32[]{:S(2)}, u32[]{:S(2)}) collective-permute-start(bf16[4,32,1152]{2,1,0:T(8,128)(2,1)S(1)} %get-tuple-element.73), channel_id=1, source_target_pairs={{0,4},{2,6},{4,0},{6,2},{1,5},{3,7},{5,1},{7,3},{8,12},{10,14},{12... | collective-permute-start | bytes 884744 | tf_op jit(solution)/shard_map/ppermute | solution.py:21
  137.4 9.7 %collective-permute-start.23 = (bf16[4,32,1152]{2,1,0:T(8,128)(2,1)S(1)}, bf16[4,32,1152]{2,1,0:T(8,128)(2,1)}, u32[]{:S(2)}, u32[]{:S(2)}) collective-permute-start(bf16[4,32,1152]{2,1,0:T(8,128)(2,1)S(1)} %get-tuple-element.73), channel_id=1, source_target_pairs={{0,6},{2,0},{4,2},{6,4},{1,7},{3,1},{5,3},{7,5},{8,14},{10,8},{12,... | collective-permute-start | bytes 884744 | tf_op jit(solution)/shard_map/ppermute | solution.py:21
  148.3 23.0 %collective-permute-start.27 = (bf16[4,128,1152]{2,1,0:T(8,128)(2,1)S(1)}, bf16[4,128,1152]{2,1,0:T(8,128)(2,1)S(1)}, u32[]{:S(2)}, u32[]{:S(2)}) collective-permute-start(bf16[4,128,1152]{2,1,0:T(8,128)(2,1)S(1)} %pad_maximum_fusion.5.refs_0_), channel_id=1, source_target_pairs={{0,8},{8,16},{16,24},{24,0},{1,9},{9,17},{17,25},{25,1},{2,10},{10... | collective-permute-start | bytes 3538952 | tf_op jit(solution)/shard_map/ppermute | solution.py:21
  148.9 23.5 %collective-permute-start.26 = (bf16[4,128,1152]{2,1,0:T(8,128)(2,1)S(1)}, bf16[4,128,1152]{2,1,0:T(8,128)(2,1)S(1)}, u32[]{:S(2)}, u32[]{:S(2)}) collective-permute-start(bf16[4,128,1152]{2,1,0:T(8,128)(2,1)S(1)} %pad_maximum_fusion.5.refs_0_), channel_id=1, source_target_pairs={{0,24},{8,0},{16,8},{24,16},{1,25},{9,1},{17,9},{25,17},{2,26},{10... | collective-permute-start | bytes 3538952 | tf_op jit(solution)/shard_map/ppermute | solution.py:21
  152.1 22.1 %collective-permute-start.32 = (bf16[4,128,1152]{2,1,0:T(8,128)(2,1)S(1)}, bf16[4,128,1152]{2,1,0:T(8,128)(2,1)S(1)}, u32[]{:S(2)}, u32[]{:S(2)}) collective-permute-start(bf16[4,128,1152]{2,1,0:T(8,128)(2,1)S(1)} %pad_maximum_fusion.6.refs_3_), channel_id=1, source_target_pairs={{0,2},{2,4},{4,6},{6,0},{1,3},{3,5},{5,7},{7,1},{8,10},{10,12},{12... | collective-permute-start | bytes 3538952 | tf_op jit(solution)/shard_map/ppermute | solution.py:21
  153.6 20.8 %collective-permute-start.1 = (bf16[512,1152]{1,0:T(8,128)(2,1)S(1)}, bf16[512,1152]{1,0:T(8,128)(2,1)S(1)}, u32[]{:S(2)}, u32[]{:S(2)}) collective-permute-start(bf16[512,1152]{1,0:T(8,128)(2,1)S(1)} %get-tuple-element.64), channel_id=1, source_target_pairs={{0,1},{1,0},{2,3},{3,2},{4,5},{5,4},{6,7},{7,6},{8,9},{9,8},{10,11... | collective-permute-start | bytes 3538952 | tf_op jit(solution)/shard_map/ppermute | solution.py:31
  160.9 28.2 %collective-permute-start.31 = (bf16[4,128,1152]{2,1,0:T(8,128)(2,1)S(1)}, bf16[4,128,1152]{2,1,0:T(8,128)(2,1)S(1)}, u32[]{:S(2)}, u32[]{:S(2)}) collective-permute-start(bf16[4,128,1152]{2,1,0:T(8,128)(2,1)S(1)} %pad_maximum_fusion.6.refs_3_), channel_id=1, source_target_pairs={{0,6},{2,0},{4,2},{6,4},{1,7},{3,1},{5,3},{7,5},{8,14},{10,8},{12,... | collective-permute-start | bytes 3538952 | tf_op jit(solution)/shard_map/ppermute | solution.py:21
  171.4 36.5 %collective-permute-start.34 = (bf16[4,64,1152]{2,1,0:T(8,128)(2,1)S(1)}, bf16[4,64,1152]{2,1,0:T(8,128)(2,1)S(1)}, u32[]{:S(2)}, u32[]{:S(2)}) collective-permute-start(bf16[4,64,1152]{2,1,0:T(8,128)(2,1)S(1)} %slice.179), channel_id=1, source_target_pairs={{0,8},{8,16},{16,24},{24,0},{1,9},{9,17},{17,25},{25,1},{2,10},{10... | collective-permute-start | bytes 1769480 | tf_op jit(solution)/shard_map/ppermute | solution.py:21
  172.4 16.7 %copy-start.18 = (bf16[4,128,1152]{2,1,0:T(8,128)(2,1)}, bf16[4,128,1152]{2,1,0:T(8,128)(2,1)S(1)}, u32[]{:S(2)}) copy-start(bf16[4,128,1152]{2,1,0:T(8,128)(2,1)S(1)} %collective-permute-done.26.refs_1_) | copy-start | bytes 3538948
  172.4 35.5 %collective-permute-start.33 = (bf16[4,64,1152]{2,1,0:T(8,128)(2,1)S(1)}, bf16[4,64,1152]{2,1,0:T(8,128)(2,1)S(1)}, u32[]{:S(2)}, u32[]{:S(2)}) collective-permute-start(bf16[4,64,1152]{2,1,0:T(8,128)(2,1)S(1)} %slice.178), channel_id=1, source_target_pairs={{0,24},{8,0},{16,8},{24,16},{1,25},{9,1},{17,9},{25,17},{2,26},{10... | collective-permute-start | bytes 1769480 | tf_op jit(solution)/shard_map/ppermute | solution.py:21
  174.3 18.6 %copy-start.19 = (bf16[4,128,1152]{2,1,0:T(8,128)(2,1)}, bf16[4,128,1152]{2,1,0:T(8,128)(2,1)S(1)}, u32[]{:S(2)}) copy-start(bf16[4,128,1152]{2,1,0:T(8,128)(2,1)S(1)} %collective-permute-done.32.refs_5_) | copy-start | bytes 3538948
  174.3 33.6 %collective-permute-start.36 = (bf16[4,64,1152]{2,1,0:T(8,128)(2,1)S(1)}, bf16[4,64,1152]{2,1,0:T(8,128)(2,1)S(1)}, u32[]{:S(2)}, u32[]{:S(2)}) collective-permute-start(bf16[4,64,1152]{2,1,0:T(8,128)(2,1)S(1)} %slice.181), channel_id=1, source_target_pairs={{0,2},{2,4},{4,6},{6,0},{1,3},{3,5},{5,7},{7,1},{8,10},{10,12},{12... | collective-permute-start | bytes 1769480 | tf_op jit(solution)/shard_map/ppermute | solution.py:21
  174.4 33.5 %copy-start.5 = (bf16[512,1152]{1,0:T(8,128)(2,1)}, bf16[512,1152]{1,0:T(8,128)(2,1)S(1)}, u32[]{:S(2)}) copy-start(bf16[512,1152]{1,0:T(8,128)(2,1)S(1)} %collective-permute-done.1.in_ref) | copy-start | bytes 3538948
  189.2 18.8 %collective-permute-start.35 = (bf16[4,64,1152]{2,1,0:T(8,128)(2,1)S(1)}, bf16[4,64,1152]{2,1,0:T(8,128)(2,1)S(1)}, u32[]{:S(2)}, u32[]{:S(2)}) collective-permute-start(bf16[4,64,1152]{2,1,0:T(8,128)(2,1)S(1)} %slice.180), channel_id=1, source_target_pairs={{0,6},{2,0},{4,2},{6,4},{1,7},{3,1},{5,3},{7,5},{8,14},{10,8},{12,... | collective-permute-start | bytes 1769480 | tf_op jit(solution)/shard_map/ppermute | solution.py:21
  222.7 3.7 %collective-permute-start.38 = (f32[512,512]{1,0:T(8,128)}, f32[512,512]{1,0:T(8,128)S(1)}, u32[]{:S(2)}, u32[]{:S(2)}) collective-permute-start(f32[512,512]{1,0:T(8,128)} %get-tuple-element.60), channel_id=1, source_target_pairs={{0,1},{1,0},{2,3},{3,2},{4,5},{5,4},{6,7},{7,6},{8,9},{9,8},{10,11... | collective-permute-start | bytes 3145736 | tf_op jit(solution)/shard_map/ppermute | solution.py:31
  231.5 8.4 %collective-permute-start.39 = (bf16[512,512]{1,0:T(8,128)(2,1)}, bf16[512,512]{1,0:T(8,128)(2,1)S(1)}, u32[]{:S(2)}, u32[]{:S(2)}) collective-permute-start(bf16[512,512]{1,0:T(8,128)(2,1)} %get-tuple-element.61.grad_ref), channel_id=1, source_target_pairs={{0,1},{1,0},{2,3},{3,2},{4,5},{5,4},{6,7},{7,6},{8,9},{9,8},{10,11... | collective-permute-start | bytes 1572872 | tf_op jit(solution)/shard_map/ppermute | solution.py:31
  231.9 1.5 collective-permute-start.37
  234.1 5.2 %collective-permute-start.40 = (f32[1,512]{1,0:T(1,128)}, f32[1,512]{1,0:T(1,128)S(1)}, u32[]{:S(2)}, u32[]{:S(2)}) collective-permute-start(f32[1,512]{1,0:T(1,128)} %get-tuple-element.63), channel_id=1, source_target_pairs={{0,1},{1,0},{2,3},{3,2},{4,5},{5,4},{6,7},{7,6},{8,9},{9,8},{10,11... | collective-permute-start | bytes 6152 | tf_op jit(solution)/shard_map/ppermute | solution.py:31
  (20 other events, 96.6 us)

commit v3 on v2

v3 whole, which is shorter than its diff:
```python
import functools
import math

import jax
import jax.numpy as jnp
from jax import lax
from jax.experimental import pallas as pl
from jax.experimental.pallas import tpu as pltpu
from jax.sharding import PartitionSpec as P

LAYER, LX, LZ, TOK = "layer", "lx", "lz", "tok"
BF16, F32 = jnp.bfloat16, jnp.float32
VMEM_MIB = 28


def smooth(values):
    return jax.nn.gelu(values, approximate=True)


def shift(value, axis, step):
    n = lax.axis_size(axis)
    return lax.ppermute(value, axis, [(i, (i + step) % n) for i in range(n)])


def send_up(value, step):
    n = lax.axis_size(LAYER)
    pairs = [(i, i + step) for i in range(n) if 0 <= i + step < n]
    return lax.ppermute(value, LAYER, pairs)


def swap(value):
    return lax.ppermute(value, TOK, [(0, 1), (1, 0)])


def turned(value, axis, by):
    n = value.shape[axis]
    return lax.dynamic_slice_in_dim(jnp.concatenate([value, value], axis), by, n, axis)


def total(values):
    return functools.reduce(jnp.add, [v.astype(F32) for v in values])


def spread(value, axis):
    return [value[0]] + [shift(value[k], axis, k) for k in range(1, len(value))]


def gathered(value, axis):
    n = lax.axis_size(axis)
    return [value] + [shift(value, axis, -k) for k in range(1, n)]


def call(kernel, where, inputs, in_specs, outs, out_specs, grid, scratch, flops, moved, aliases=None):
    return pl.pallas_call(
        kernel,
        out_shape=[jax.ShapeDtypeStruct(shape, dtype) for shape, dtype in outs],
        grid_spec=pltpu.PrefetchScalarGridSpec(
            num_scalar_prefetch=1,
            grid=(grid,),
            in_specs=in_specs,
            out_specs=out_specs,
            scratch_shapes=scratch,
        ),
        input_output_aliases=aliases or {},
        compiler_params=pltpu.CompilerParams(vmem_limit_bytes=VMEM_MIB * 2**20),
        cost_estimate=pl.CostEstimate(flops=flops, bytes_accessed=moved, transcendentals=0),
    )(where, *inputs)


def fixed(*shape):
    return pl.BlockSpec(shape, lambda k, w: (0,) * len(shape))


def each(*shape):
    return pl.BlockSpec(shape, lambda k, w: (k,) + (0,) * (len(shape) - 1))


def encode_kernel(where, in_ref, w_ref, bias_ref, pre_ref, lat_ref, turned_ref, acc_ref, *, ring):
    k = pl.program_id(0)

    @pl.when(k == 0)
    def _():
        acc_ref[...] = jnp.broadcast_to(bias_ref[...], acc_ref.shape)

    acc_ref[...] += jnp.dot(in_ref[...], w_ref[...], preferred_element_type=F32)

    @pl.when(k == pl.num_programs(0) - 1)
    def _():
        piece = acc_ref.shape[0] // (ring * ring)
        for i in range(ring):
            for j in range(ring):
                row, col = lax.rem(i + ring - where[2], ring), lax.rem(j + ring - where[3], ring)
                pre = acc_ref[(i * ring + j) * piece : (i * ring + j + 1) * piece, :]
                latent = smooth(pre).astype(BF16)
                to = pl.ds(pl.multiple_of((row * ring + col) * piece, piece), piece)
                pre_ref[to, :] = pre
                lat_ref[to, :] = latent
                turned_ref[pl.ds(pl.multiple_of((col * ring + row) * piece, piece), piece), :] = latent


def encode(where, inputs, weight, bias, ring, steps=3):
    rows, model = inputs.shape
    feats = weight.shape[1]
    return call(
        functools.partial(encode_kernel, ring=ring),
        where,
        (inputs, weight, bias),
        [
            pl.BlockSpec((rows, model // steps), lambda k, w: (0, k)),
            pl.BlockSpec((model // steps, feats), lambda k, w: (k, 0)),
            fixed(1, feats),
        ],
        [((rows, feats), F32), ((rows, feats), BF16), ((rows, feats), BF16)],
        [fixed(rows, feats)] * 3,
        steps,
        [pltpu.VMEM((rows, feats), F32)],
        2 * rows * model * feats,
        8 * 2**20,
    )


def far_kernel(where, own_ref, other_ref, w_ref, *out_refs):
    for lat_ref, refs in ((own_ref, out_refs[:2]), (other_ref, out_refs[2:])):
        n = lat_ref.shape[0] // 4
        out = jnp.dot(lat_ref[2 * n : 3 * n, :], w_ref[0], preferred_element_type=F32).astype(BF16)
        refs[0][0] = out[: n // 2]
        refs[1][0] = out[n // 2 :]


def near_kernel(where, own_ref, other_ref, w_ref, *out_refs):
    for lat_ref, refs in ((own_ref, out_refs[:3]), (other_ref, out_refs[3:])):
        n = lat_ref.shape[0] // 4
        out = jnp.dot(lat_ref[: 2 * n, :], w_ref[0], preferred_element_type=F32)
        refs[0][0] = out[:n]
        refs[1][0] = out[n:].astype(BF16)
        out = jnp.dot(lat_ref[3 * n :, :], w_ref[0], preferred_element_type=F32)
        refs[2][0] = out.astype(BF16)


def rebuild(kernel, where, own_lat, other_lat, weights, width):
    layers, feats, _ = weights.shape
    rows = own_lat.shape[0]
    n = rows // 4
    half = ((layers, n // 2, width), BF16)
    if kernel is far_kernel:
        outs, used = [half] * 4, 2 * n
    else:
        outs, used = [((layers, n, width), d) for d in (F32, BF16, BF16)] * 2, 6 * n
    return call(
        kernel,
        where,
        (own_lat, other_lat, weights),
        [
            fixed(rows, feats),
            fixed(rows, feats),
            pl.BlockSpec((1, feats, width), lambda k, w: (lax.rem(w[0] + k, layers), 0, 0)),
        ],
        outs,
        [each(1, *shape[1:]) for shape, _ in outs],
        layers,
        [],
        2 * layers * used * feats * width,
        8 * 2**20,
    )


def fold_kernel(where, *refs):
    for i in range(4):
        value, rows, out = refs[i], refs[4 + i], refs[8 + i]
        out[...] = (value[...].astype(F32) + rows[...].astype(F32)).astype(BF16)


def fold(where, values, rows, steps=2):
    layers, n, width = values[0].shape
    half = (layers // steps, n // 2, width)
    low, high = pl.BlockSpec(half, lambda k, w: (k, 0, 0)), pl.BlockSpec(half, lambda k, w: (k, 1, 0))
    return call(
        fold_kernel,
        where,
        (*values, *rows),
        [low, high, low, high] + [each(*half)] * 4,
        [(v.shape, BF16) for v in values],
        [low, high, low, high],
        steps,
        [],
        4 * values[0].size,
        12 * values[0].size,
        {1 + i: i for i in range(4)},
    )


def near_act_kernel(where, w_ref, *refs):
    *x_refs, act_ref, err_ref = refs
    k = pl.program_id(0)
    step = x_refs[0].shape[1]

    @pl.when(k == 0)
    def _():
        act_ref[...] = jnp.zeros_like(act_ref)

    @pl.when(where[0] + k < pl.num_programs(0))
    def _():
        for i, x_ref in enumerate(x_refs):
            err_ref[i * step : (i + 1) * step, :] = x_ref[0]
        for i in range(0, err_ref.shape[0], 256):
            act_ref[i : i + 256, :] += lax.dot_general(
                err_ref[i : i + 256, :], w_ref[0], (((1,), (1,)), ((), ())), preferred_element_type=F32
            )


def far_act_kernel(where, w_ref, near_ref, *refs, ring):
    *x_refs, own_ref, other_ref, err_ref, act_ref = refs
    k = pl.program_id(0)
    step = x_refs[0].shape[1]

    @pl.when(k == 0)
    def _():
        act_ref[...] = jnp.zeros_like(act_ref)

    @pl.when(where[0] + k < pl.num_programs(0))
    def _():
        for i, x_ref in enumerate(x_refs):
            err_ref[i * step : (i + 1) * step, :] = x_ref[0]
        act_ref[...] += lax.dot_general(
            err_ref[...], w_ref[0], (((1,), (1,)), ((), ())), preferred_element_type=F32
        )

    @pl.when(k == pl.num_programs(0) - 1)
    def _():
        n = act_ref.shape[0] // 2
        piece = n // ring
        for side in range(2):
            for i in range(ring):
                ref, at = {
                    0: (near_ref, 3 * n * side),
                    1: (near_ref, 3 * n * side + n),
                    2: (act_ref, n * side),
                    3: (near_ref, 3 * n * side + 2 * n),
                }[i]
                if side == 0:
                    own_ref[i * n : (i + 1) * n, :] = ref[at : at + n, :]
                else:
                    for j in range(ring):
                        to = (j * ring + i) * piece
                        other_ref[to : to + piece, :] = ref[at + j * piece : at + (j + 1) * piece, :]


def act_grads(where, weights, near, far, width, ring):
    layers, feats, _ = weights.shape
    n = near[0].shape[1]
    target = pl.BlockSpec((1, feats, width), lambda k, w: (lax.rem(w[0] + k, layers), 0, 0))
    [act] = call(
        near_act_kernel,
        where,
        (weights, *near),
        [target] + [each(1, n, width)] * 6,
        [((6 * n, feats), F32)],
        [fixed(6 * n, feats)],
        layers,
        [pltpu.VMEM((6 * n, width), BF16)],
        2 * layers * 6 * n * feats * width,
        14 * 2**20,
    )
    return call(
        functools.partial(far_act_kernel, ring=ring),
        where,
        (weights, act, *far),
        [target, fixed(6 * n, feats)] + [each(1, n // 2, width)] * 4,
        [((4 * n, feats), F32)] * 2,
        [fixed(4 * n, feats)] * 2,
        layers,
        [pltpu.VMEM((2 * n, width), BF16), pltpu.VMEM((2 * n, feats), F32)],
        2 * layers * 2 * n * feats * width,
        10 * 2**20,
    )


def dec_kernel(where, own_ref, other_ref, *refs):
    *x_refs, dec_ref, sum_ref, err_ref = refs
    live = where[0] + pl.program_id(0) < pl.num_programs(0)
    rows = own_ref.shape[0]

    @pl.when(live)
    def _():
        half = x_refs[-1].shape[1]
        starts = [0, 2, 6, 8, 10, 14, 4, 5, 12, 13]
        for x_ref, start in zip(x_refs, starts, strict=True):
            err_ref[start * half : start * half + x_ref.shape[1], :] = x_ref[0]
        dims = (((0,), (0,)), ((), ()))
        dec_ref[0] = lax.dot_general(
            own_ref[...], err_ref[:rows, :], dims, preferred_element_type=F32
        ) + lax.dot_general(other_ref[...], err_ref[rows:, :], dims, preferred_element_type=F32)

    @pl.when(jnp.logical_not(live))
    def _():
        dec_ref[0] = jnp.zeros_like(dec_ref[0])

    @pl.when(pl.program_id(0) == 0)
    def _():
        sum_ref[...] = jnp.sum(err_ref[...].astype(F32), axis=0, keepdims=True)


def dec_gradient(where, own_lat, other_lat, errs):
    rows, feats = own_lat.shape
    layers, _, width = errs[0].shape
    return call(
        dec_kernel,
        where,
        (own_lat, other_lat, *errs),
        [fixed(rows, feats)] * 2 + [each(1, e.shape[1], width) for e in errs],
        [((layers, feats, width), F32), ((1, width), F32)],
        [
            pl.BlockSpec((1, feats, width), lambda k, w: (lax.rem(w[0] + k, layers), 0, 0)),
            fixed(1, width),
        ],
        layers,
        [pltpu.VMEM((2 * rows, width), BF16)],
        4 * layers * rows * feats * width,
        20 * 2**20,
    )


def enc_kernel(where, in_ref, other_ref, grad_ref, other_grad_ref, out_ref):
    out_ref[...] = jnp.dot(in_ref[...], grad_ref[...], preferred_element_type=F32) + jnp.dot(
        other_ref[...], other_grad_ref[...], preferred_element_type=F32
    )


def enc_gradient(where, own_t, other_t, grad, other_grad, steps=6):
    width, rows = own_t.shape
    feats = grad.shape[1]
    tile = pl.BlockSpec((width // steps, rows), lambda k, w: (k, 0))
    return call(
        enc_kernel,
        where,
        (own_t, other_t, grad, other_grad),
        [tile, tile, fixed(rows, feats), fixed(rows, feats)],
        [((width, feats), F32)],
        [pl.BlockSpec((width // steps, feats), lambda k, w: (k, 0))],
        steps,
        [],
        4 * rows * width * feats,
        6 * 2**20,
    )[0]


def on_device(resid_in, resid_out, enc_weight, enc_bias, dec_weight, dec_bias):
    s, x, z, c = (lax.axis_index(a) for a in (LAYER, LX, LZ, TOK))
    ring = lax.axis_size(LX)
    layers, feats, model = dec_weight.shape[1:]
    tok = resid_in.shape[1]
    width = model // 2
    piece = tok // (ring * ring)
    scale = 1.0 / math.sqrt(tok * lax.axis_size(TOK))
    where = jnp.stack([s, c, x, z]).astype(jnp.int32)
    inputs = resid_in[0]
    weights = lax.dynamic_slice_in_dim(dec_weight[0], c * width, width, 2)

    def mine_first(rows):
        blocks = rows.reshape(ring, ring, piece, rows.shape[1])
        return turned(turned(blocks, 0, x), 1, z).reshape(rows.shape)

    pre, own_lat, crossed = encode(where, inputs, enc_weight[0], enc_bias, ring)
    own_out = resid_out[0].reshape(ring * ring, piece, -1)
    other_lat, other_out = lax.optimization_barrier((swap(crossed), swap(own_out)))

    far_a0, far_a1, far_b0, far_b1 = rebuild(far_kernel, where, own_lat, other_lat, weights, width)
    parts = [(far_a0, LX, 1), (far_a1, LX, -1), (far_b0, LZ, 1), (far_b1, LZ, -1)]
    got = [shift(*part) for part in parts]
    own_a, up_a, down_a, own_b, up_b, down_b = rebuild(
        near_kernel, where, own_lat, other_lat, weights, width
    )
    folded = fold(where, (up_a, down_a, up_b, down_b), got)
    got = [shift(value, *part[1:]) for value, part in zip(folded, parts, strict=True)]

    later, *_ = lax.optimization_barrier((inputs, *folded))
    ordered = mine_first(later)
    own_in = lax.dynamic_slice_in_dim(ordered, c * width, width, 1)
    to_other = lax.dynamic_slice_in_dim(ordered, (1 - c) * width, width, 1)
    own_in = own_in.T

    own_out, other_out, own_in, to_other = lax.optimization_barrier(
        (own_out, other_out, own_in, to_other)
    )
    base = dec_bias[0] - jnp.stack([own_out, other_out], 1).astype(F32)
    base = lax.all_to_all(base, (LX, LZ), 0, 0, tiled=True)
    base = lax.dynamic_slice_in_dim(base, c * (ring * ring // 2), ring * ring // 2, 0)
    base = base.transpose(1, 2, 0, 3).reshape(2, piece, width)

    a = total([own_a, *got[:2]]).reshape(layers, ring, piece, width)
    b = total([own_b, *got[2:]]).reshape(layers, ring, piece, width)
    a = spread([a[:, 0]] + [a[:, i].astype(BF16) for i in range(1, ring)], LZ)
    b = spread([b[:, 0]] + [b[:, i].astype(BF16) for i in range(1, ring)], LX)
    base, b[3] = lax.optimization_barrier((base, b[3]))
    a, b = total(a), total(b)
    pieces = jnp.stack([a, b], 1)
    rebuilt = pieces[0] + base
    for k in range(1, layers):
        rebuilt = rebuilt + send_up(pieces[k].astype(BF16), k).astype(F32)
    errors = (rebuilt * scale).astype(BF16)

    errors, to_other = lax.optimization_barrier((errors, to_other))
    other_in = swap(to_other).T
    errors = jnp.stack([errors] + [send_up(errors, -k) for k in range(1, layers)], 1)
    paths = [(LX, -1), (LX, 1), (LZ, -1), (LZ, 1)]
    own_a = jnp.concatenate(gathered(errors[0], LZ), 1)
    own_b = jnp.concatenate(gathered(errors[1], LX), 1)
    got = [shift(v, *path) for v, path in zip((own_a, own_a, own_b, own_b), paths, strict=True)]
    half = got[0].shape[1] // 2
    far = [
        shift(v[:, i % 2 * half : (i % 2 + 1) * half], *path)
        for i, (v, path) in enumerate(zip(got, paths, strict=True))
    ]
    own_in, other_in, *got = lax.optimization_barrier((own_in, other_in, *got))
    near = [own_a, *got[:2], own_b, *got[2:]]

    own_act, other_act = act_grads(where, weights, near, far, width, ring)
    dec_grad, sums = dec_gradient(where, own_lat, other_lat, [*near, *far])
    pre, sums = lax.optimization_barrier((pre, sums))
    act = own_act + swap(other_act)
    pre_grad = jax.vjp(smooth, pre)[1](act)[0].astype(BF16)
    own_sum = jnp.sum(pre_grad.astype(F32), axis=0, keepdims=True)
    enc_grad = enc_gradient(where, own_in, other_in, pre_grad, swap(pre_grad))
    enc_bias_grad = own_sum + swap(own_sum)
    both = turned(jnp.concatenate([sums, swap(sums)], 0), 0, c).reshape(1, model)
    size = dec_bias.shape[1]
    dec_bias_grad = lax.dynamic_slice_in_dim(both, (x * ring + z) * size, size, 1)
    return dec_grad[None], dec_bias_grad, enc_grad[None], enc_bias_grad


def solution(mesh):
    ring = math.isqrt(mesh.shape["latent"])
    shape = (mesh.shape["layer"], ring, ring, mesh.shape["tok"])
    fine = jax.sharding.Mesh(mesh.devices.reshape(shape), (LAYER, LX, LZ, TOK))
    latent = (LX, LZ)
    in_specs = (
        P(LAYER, TOK, None),
        P(LAYER, TOK, latent),
        P(LAYER, None, latent),
        P(LAYER, latent),
        P(LAYER, None, latent, None),
        P(LAYER, latent),
    )
    out_specs = (
        P(LAYER, None, latent, TOK),
        P(LAYER, latent),
        P(LAYER, TOK, latent),
        P(LAYER, latent),
    )
    return jax.shard_map(
        on_device, mesh=fine, in_specs=in_specs, out_specs=out_specs, check_vma=False
    )
```

time: 248 us -> 210 us (0.85)
  waiting for transfers between devices: 79.6 us -> 38.7 us
  starting transfers between devices: 68.5 us -> 93.9 us
  Pallas kernels: 64.3 us -> 39.8 us
  local copies, waits for them, and re-layouts: 15.4 us -> 23.3 us
  other arithmetic: 17.3 us -> 12.3 us
    ppermute x28, waiting for transfers between devices: 70.3 us -> 30 us  [shift(): return lax.ppermute(value, axis, [(i, (i + step) % n) for i in range(n)])]
    pallas_call x8, Pallas kernels: 64.3 us -> 39.8 us  [call(): pl.pallas_call(kernel, out_shape=[jax.ShapeDtypeStruct(shape, dtype) for...]
    ppermute x7, starting transfers between devices: 11.4 us -> 34.7 us  [swap(): return lax.ppermute(value, TOK, [(0, 1), (1, 0)])]
    unnamed x58 -> x55, local copies, waits for them, and re-layouts: 4.45 us -> 13 us
    concatenate x7 -> x2, other arithmetic: 5.59 us -> 0.18 us  [the longest x1 0.09 us: on_device(): own_a = jnp.concatenate(gathered(errors[0], LZ), 1)]
    slice x9 -> x4, local copies, waits for them, and re-layouts: 4.68 us -> 0.19 us  [on_device(): v[:, i % 2 * half:(i % 2 + 1) * half]]
    ppermute x28, starting transfers between devices: 38.1 us -> 42.3 us  [shift(): return lax.ppermute(value, axis, [(i, (i + step) % n) for i in range(n)])]
    convert_element_type x4 -> x0, other arithmetic: 3.03 us -> none  [the longest x2 1.65 us: ring_spread(): total([up[:, :half], from_below]).astype(BF16)]
  transfers between devices with their start and end apart: 42 -> 42, of which waited for: 16 -> 15; matrix products, arithmetic and copies ran while one was open for 10% -> 10% of each run, Pallas kernels for 14% -> 10%
where the time goes in v3:
time: 210 us; the launch traced here: 209 us
  starting transfers between devices  93.9 us (45%)
  Pallas kernels  39.8 us (19%)
  waiting for transfers between devices  38.7 us (18%)
  local copies, waits for them, and re-layouts  23.3 us (11%)
  other arithmetic  12.3 us (6%)
    ppermute x28, starting transfers between devices, shift(): return lax.ppermute(value, axis, [(i, (i + step) % n) for i in range(n)])  42.3 us
    pallas_call x8, Pallas kernels, call(): pl.pallas_call(kernel, out_shape=[jax.ShapeDtypeStruct(shape, dtype) for...  39.8 us
    ppermute x7, starting transfers between devices, swap(): return lax.ppermute(value, TOK, [(0, 1), (1, 0)])  34.7 us
    ppermute x28, waiting for transfers between devices, shift(): return lax.ppermute(value, axis, [(i, (i + step) % n) for i in range(n)])  30 us
    unnamed x55, local copies, waits for them, and re-layouts  13 us
    ppermute x6, starting transfers between devices, send_up(): return lax.ppermute(value, LAYER, pairs)  12.6 us
    ppermute x6, waiting for transfers between devices, send_up(): return lax.ppermute(value, LAYER, pairs)  6.85 us
    add x2, other arithmetic, total(): return functools.reduce(jnp.add, [v.astype(F32) for v in values])  4.68 us
  transfers between devices with their start and end apart: 42, of which 15 were waited for; matrix products, arithmetic and copies ran while one was open for 10% of the time, Pallas kernels for 10%

profile of v3, /device:TPU:1, one launch (start us, length us, event | category | flops | bytes accessed | tf_op | source)
XLA Modules:
  0.0 209.2 jit_solution(11599251473726753222)
XLA Ops:
  0.7 1.7 copy-done.2
  2.4 1.7 copy-done.5
  4.7 3.0 %shard_map.93 = (f32[512,512]{1,0:T(8,128)S(1)}, bf16[512,512]{1,0:T(8,128)(2,1)S(1)}, bf16[512,512]{1,0:T(8,128)(2,1)S(1)}) custom-call(s32[4]{0:T(128)S(1)} %pad_add_fusion.where, bf16[512,2304]{1,0:T(8,128)(2,1)S(1)} %bitcast.101, bf16[2304,512]{1,0:T(8,128)(2,1)S(1)} %bitcast.104, f32[1,512]{1,0:T(1,128)S(1)} %copy-done.14), custom_call_target="tpu_custom_call" | custom-call | flops 1207959552 | bytes 8388608 | tf_op jit(solution)/shard_map/pallas_call | solution.py:54
  7.7 1.5 collective-permute-start
  9.5 2.7 %dynamic-slice_bitcast_fusion.w_ref = bf16[4,512,1152]{2,1,0:T(8,128)(2,1)S(1)} fusion(bf16[1,4,512,2304]{3,2,1,0:T(8,128)(2,1)} %param.10, s32[]{:T(128)S(6)} %select_n.22), kind=kLoop, calls=%fused_computation.4 | loop fusion | bytes 9437188 | tf_op jit(solution)/shard_map/dynamic_slice | solution.py:357
  12.3 4.2 %shard_map.95 = (bf16[4,64,1152]{2,1,0:T(8,128)(2,1)}, bf16[4,64,1152]{2,1,0:T(8,128)(2,1)}, bf16[4,64,1152]{2,1,0:T(8,128)(2,1)}, bf16[4,64,1152]{2,1,0:T(8,128)(2,1)}) custom-call(s32[4]{0:T(128)S(1)} %pad_add_fusion.where, bf16[512,512]{1,0:T(8,128)(2,1)S(1)} %get-tuple-element.44.own_ref, bf16[512,512]{1,0:T(8,128)(2,1)S(1)} %collective-permute-done.other_ref, ...), custom_call_target="tpu_custom_call" | custom-call | flops 1207959552 | bytes 8388608 | tf_op jit(solution)/shard_map/pallas_call | solution.py:54
  19.2 1.7 collective-permute-start.4
  20.9 2.1 %collective-permute-start.5 = (bf16[4,64,1152]{2,1,0:T(8,128)(2,1)}, bf16[4,64,1152]{2,1,0:T(8,128)(2,1)}, u32[]{:S(2)}, u32[]{:S(2)}) collective-permute-start(bf16[4,64,1152]{2,1,0:T(8,128)(2,1)} %get-tuple-element.55), channel_id=1, source_target_pairs={{0,6},{2,0},{4,2},{6,4},{1,7},{3,1},{5,3},{7,5},{8,14},{10,8},{12,... | collective-permute-start | bytes 1769480 | tf_op jit(solution)/shard_map/ppermute | solution.py:22
  23.0 2.3 %copy-done.1 = bf16[4,512,1152]{2,1,0:T(8,128)(2,1)S(1)} copy-done((bf16[4,512,1152]{2,1,0:T(8,128)(2,1)S(1)}, bf16[4,512,1152]{2,1,0:T(8,128)(2,1)}, u32[]{:S(2)}) %copy-start.1) | copy-done | bytes 4718616
  27.5 6.3 %shard_map.94 = (f32[4,128,1152]{2,1,0:T(8,128)S(1)}, bf16[4,128,1152]{2,1,0:T(8,128)(2,1)}, bf16[4,128,1152]{2,1,0:T(8,128)(2,1)}, f32[4,128,1152]{2,1,0:T(8,12...) custom-call(s32[4]{0:T(128)S(1)} %pad_add_fusion.where, bf16[512,512]{1,0:T(8,128)(2,1)S(1)} %copy-done.9, ...), custom_call_target="tpu_custom_call" | custom-call | flops 3623878656 | bytes 8388608 | tf_op jit(solution)/shard_map/pallas_call | solution.py:54
  33.7 1.4 copy-done.4
  36.0 4.3 %shard_map.96 = (bf16[4,128,1152]{2,1,0:T(8,128)(2,1)}, bf16[4,128,1152]{2,1,0:T(8,128)(2,1)}, bf16[4,128,1152]{2,1,0:T(8,128)(2,1)}, bf16[4,128,1152]{2,1,0:T(8,128)(2,1)}) custom-call(s32[4]{0:T(128)S(1)} %pad_add_fusion.where, ...), custom_call_target="tpu_custom_call", output_to_operand_aliasing={{0}: (1, {}), {1}: (2, {}), {2}: (3, {}), {3}: (4, {})} | custom-call | flops 2359296 | bytes 7077888 | tf_op jit(solution)/shard_map/pallas_call | solution.py:54
  40.4 2.6 %collective-permute-start.7 = (bf16[4,128,1152]{2,1,0:T(8,128)(2,1)}, bf16[4,128,1152]{2,1,0:T(8,128)(2,1)}, u32[]{:S(2)}, u32[]{:S(2)}) collective-permute-start(bf16[4,128,1152]{2,1,0:T(8,128)(2,1)} %get-tuple-element.57), channel_id=1, source_target_pairs={{0,24},{8,0},{16,8},{24,16},{1,25},{9,1},{17,9},{25,17},{2,26},{10... | collective-permute-start | bytes 3538952 | tf_op jit(solution)/shard_map/ppermute | solution.py:22
  43.5 2.3 %collective-permute-start.12 = (bf16[4,128,1152]{2,1,0:T(8,128)(2,1)}, bf16[4,128,1152]{2,1,0:T(8,128)(2,1)}, u32[]{:S(2)}, u32[]{:S(2)}) collective-permute-start(bf16[4,128,1152]{2,1,0:T(8,128)(2,1)} %get-tuple-element.60), channel_id=1, source_target_pairs={{0,6},{2,0},{4,2},{6,4},{1,7},{3,1},{5,3},{7,5},{8,14},{10,8},{12,... | collective-permute-start | bytes 3538952 | tf_op jit(solution)/shard_map/ppermute | solution.py:22
  48.8 1.5 copy.45
  50.3 1.6 copy.44
  54.1 4.3 %all-to-all-start = ((f32[16,2,32,144]{3,2,1,0:T(8,128)}), f32[16,2,32,144]{3,2,1,0:T(8,128)}, u32[]{:S(2)}, u32[]{:S(2)}) async-start(f32[16,2,32,144]{3,2,1,0:T(8,128)} %copy.39), calls=%async_computation | async-start | bytes 2097152 | tf_op jit(solution)/shard_map/all_to_all | solution.py:386
  58.5 11.3 %collective-permute-done.11 = bf16[4,128,1152]{2,1,0:T(8,128)(2,1)} collective-permute-done((bf16[4,128,1152]{2,1,0:T(8,128)(2,1)}, bf16[4,128,1152]{2,1,0:T(8,128)(2,1)}, u32[]{:S(2)}, u32[]{:S(2)}) %collective-permute-start.11) | collective-permute-done | bytes 1179680 | tf_op jit(solution)/shard_map/ppermute | solution.py:22
  69.8 2.6 %convert_add_fusion = f32[4,128,1152]{2,1,0:T(8,128)S(1)} fusion(bf16[4,128,1152]{2,1,0:T(8,128)(2,1)} %collective-permute-done.12, f32[4,128,1152]{2,1,0:T(8,128)} %copy-done.4, bf16[4,128,1152]{2,1,0:T(8,128)(2,1)} %collective-permute-done.11), kind=kLoop, calls=%fused_computation.7 | loop fusion | flops 2359296 | bytes 7077888 | tf_op jit(solution)/shard_map/add | solution.py:41
  73.6 2.0 convert_add_fusion.1
  77.3 4.1 %collective-permute-start.10 = (bf16[4,32,1152]{2,1,0:T(8,128)(2,1)S(1)}, bf16[4,32,1152]{2,1,0:T(8,128)(2,1)}, u32[]{:S(2)}, u32[]{:S(2)}) collective-permute-start(bf16[4,32,1152]{2,1,0:T(8,128)(2,1)S(1)} %get-tuple-element.92), channel_id=1, source_target_pairs={{0,6},{2,0},{4,2},{6,4},{1,7},{3,1},{5,3},{7,5},{8,14},{10,8},{12,... | collective-permute-start | bytes 884744 | tf_op jit(solution)/shard_map/ppermute | solution.py:22
  86.7 2.6 %collective-permute-done.10 = bf16[4,32,1152]{2,1,0:T(8,128)(2,1)} collective-permute-done((bf16[4,32,1152]{2,1,0:T(8,128)(2,1)S(1)}, bf16[4,32,1152]{2,1,0:T(8,128)(2,1)}, u32[]{:S(2)}, u32[]{:S(2)}) %collective-permute-start.10) | collective-permute-done | bytes 294944 | tf_op jit(solution)/shard_map/ppermute | solution.py:22
  89.3 1.6 collective-permute-done.9
  90.9 1.5 fusion.17
  92.3 2.2 %collective-permute-done.13 = bf16[4,32,1152]{2,1,0:T(8,128)(2,1)S(1)} collective-permute-done((bf16[4,32,1152]{2,1,0:T(8,128)(2,1)S(1)}, bf16[4,32,1152]{2,1,0:T(8,128)(2,1)S(1)}, u32[]{:S(2)}, u32[]{:S(2)}) %collective-permute-start.13) | collective-permute-done | bytes 294944 | tf_op jit(solution)/shard_map/ppermute | solution.py:22
  96.0 3.5 %collective-permute-start.16 = (bf16[2,32,1152]{2,1,0:T(8,128)(2,1)S(1)}, bf16[2,32,1152]{2,1,0:T(8,128)(2,1)S(1)}, u32[]{:S(2)}, u32[]{:S(2)}) collective-permute-start(bf16[2,32,1152]{2,1,0:T(8,128)(2,1)S(1)} %get-tuple-element.96), channel_id=1, source_target_pairs={{0,32},{32,64},{64,96},{1,33},{33,65},{65,97},{2,34},{34,66},{66,9... | collective-permute-start | bytes 442376 | tf_op jit(solution)/shard_map/ppermute | solution.py:28
  99.5 2.8 %collective-permute-start.18 = (bf16[2,32,1152]{2,1,0:T(8,128)(2,1)S(1)}, bf16[2,32,1152]{2,1,0:T(8,128)(2,1)S(1)}, u32[]{:S(2)}, u32[]{:S(2)}) collective-permute-start(bf16[2,32,1152]{2,1,0:T(8,128)(2,1)S(1)} %get-tuple-element.97), channel_id=1, source_target_pairs={{0,96},{1,97},{2,98},{3,99},{4,100},{5,101},{6,102},{7,103},{8,104... | collective-permute-start | bytes 442376 | tf_op jit(solution)/shard_map/ppermute | solution.py:28
  102.3 2.5 %collective-permute-start.17 = (bf16[2,32,1152]{2,1,0:T(8,128)(2,1)S(1)}, bf16[2,32,1152]{2,1,0:T(8,128)(2,1)S(1)}, u32[]{:S(2)}, u32[]{:S(2)}) collective-permute-start(bf16[2,32,1152]{2,1,0:T(8,128)(2,1)S(1)} %get-tuple-element.98), channel_id=1, source_target_pairs={{0,64},{32,96},{1,65},{33,97},{2,66},{34,98},{3,67},{35,99},{4,68}... | collective-permute-start | bytes 442376 | tf_op jit(solution)/shard_map/ppermute | solution.py:28
  104.8 2.1 collective-permute-done.17
  110.8 3.2 %collective-permute-done.21 = bf16[2,32,1152]{2,1,0:T(8,128)(2,1)S(1)} collective-permute-done((bf16[2,32,1152]{2,1,0:T(8,128)(2,1)S(1)}, bf16[2,32,1152]{2,1,0:T(8,128)(2,1)S(1)}, u32[]{:S(2)}, u32[]{:S(2)}) %collective-permute-start.21) | collective-permute-done | bytes 147488 | tf_op jit(solution)/shard_map/ppermute | solution.py:28
  114.0 1.6 collective-permute-done.20
  117.4 2.0 collective-permute-start.22
  119.8 4.5 %collective-permute-start.29 = (bf16[4,32,1152]{2,1,0:T(8,128)(2,1)S(1)}, bf16[4,32,1152]{2,1,0:T(8,128)(2,1)S(1)}, u32[]{:S(2)}, u32[]{:S(2)}) collective-permute-start(bf16[4,32,1152]{2,1,0:T(8,128)(2,1)S(1)} %get-tuple-element.94), channel_id=1, source_target_pairs={{0,16},{8,24},{16,0},{24,8},{1,17},{9,25},{17,1},{25,9},{2,18},{10... | collective-permute-start | bytes 884744 | tf_op jit(solution)/shard_map/ppermute | solution.py:22
  124.3 1.5 collective-permute-done.24
  125.8 3.8 %collective-permute-start.28 = (bf16[4,32,1152]{2,1,0:T(8,128)(2,1)S(1)}, bf16[4,32,1152]{2,1,0:T(8,128)(2,1)S(1)}, u32[]{:S(2)}, u32[]{:S(2)}) collective-permute-start(bf16[4,32,1152]{2,1,0:T(8,128)(2,1)S(1)} %get-tuple-element.94), channel_id=1, source_target_pairs={{0,24},{8,0},{16,8},{24,16},{1,25},{9,1},{17,9},{25,17},{2,26},{10... | collective-permute-start | bytes 884744 | tf_op jit(solution)/shard_map/ppermute | solution.py:22
  129.8 2.7 %collective-permute-start.26 = (bf16[4,128,1152]{2,1,0:T(8,128)(2,1)S(1)}, bf16[4,128,1152]{2,1,0:T(8,128)(2,1)S(1)}, u32[]{:S(2)}, u32[]{:S(2)}) collective-permute-start(bf16[4,128,1152]{2,1,0:T(8,128)(2,1)S(1)} %pad_maximum_fusion.1.refs_0_), channel_id=1, source_target_pairs={{0,24},{8,0},{16,8},{24,16},{1,25},{9,1},{17,9},{25,17},{2,26},{10... | collective-permute-start | bytes 3538952 | tf_op jit(solution)/shard_map/ppermute | solution.py:22
  133.4 2.7 %collective-permute-start.31 = (bf16[4,128,1152]{2,1,0:T(8,128)(2,1)S(1)}, bf16[4,128,1152]{2,1,0:T(8,128)(2,1)S(1)}, u32[]{:S(2)}, u32[]{:S(2)}) collective-permute-start(bf16[4,128,1152]{2,1,0:T(8,128)(2,1)S(1)} %pad_maximum_fusion.2.refs_3_), channel_id=1, source_target_pairs={{0,6},{2,0},{4,2},{6,4},{1,7},{3,1},{5,3},{7,5},{8,14},{10,8},{12,... | collective-permute-start | bytes 3538952 | tf_op jit(solution)/shard_map/ppermute | solution.py:22
  136.1 19.9 %collective-permute-start.25 = (bf16[512,1152]{0,1:T(8,128)(2,1)S(1)}, bf16[512,1152]{0,1:T(8,128)(2,1)S(1)}, u32[]{:S(2)}, u32[]{:S(2)}) collective-permute-start(bf16[512,1152]{0,1:T(8,128)(2,1)S(1)} %copy-done.17), channel_id=1, source_target_pairs={{0,1},{1,0},{2,3},{3,2},{4,5},{5,4},{6,7},{7,6},{8,9},{9,8},{10,11... | collective-permute-start | bytes 3538952 | tf_op jit(solution)/shard_map/ppermute | solution.py:32
  156.2 2.7 %collective-permute-start.33 = (bf16[4,64,1152]{2,1,0:T(8,128)(2,1)S(1)}, bf16[4,64,1152]{2,1,0:T(8,128)(2,1)S(1)}, u32[]{:S(2)}, u32[]{:S(2)}) collective-permute-start(bf16[4,64,1152]{2,1,0:T(8,128)(2,1)S(1)} %slice.96), channel_id=1, source_target_pairs={{0,24},{8,0},{16,8},{24,16},{1,25},{9,1},{17,9},{25,17},{2,26},{10... | collective-permute-start | bytes 1769480 | tf_op jit(solution)/shard_map/ppermute | solution.py:22
  159.2 2.7 %collective-permute-start.35 = (bf16[4,64,1152]{2,1,0:T(8,128)(2,1)S(1)}, bf16[4,64,1152]{2,1,0:T(8,128)(2,1)S(1)}, u32[]{:S(2)}, u32[]{:S(2)}) collective-permute-start(bf16[4,64,1152]{2,1,0:T(8,128)(2,1)S(1)} %slice.98), channel_id=1, source_target_pairs={{0,6},{2,0},{4,2},{6,4},{1,7},{3,1},{5,3},{7,5},{8,14},{10,8},{12,... | collective-permute-start | bytes 1769480 | tf_op jit(solution)/shard_map/ppermute | solution.py:22
  161.9 5.6 %shard_map.98.near_ref = f32[768,512]{1,0:T(8,128)S(1)} custom-call(s32[4]{0:T(128)S(1)} %pad_add_fusion.where, bf16[4,512,1152]{2,1,0:T(8,128)(2,1)S(1)} %bitcast.100, bf16[4,128,1152]{2,1,0:T(8,128)(2,1)S(1)} %pad_maximum_fusion.1.refs_0_, bf16[4,128,1152]{2,1,0:T(8,128)(2,1)S(1)} %collective-permute-done.26.refs_1_, ...), custom_call_target="tpu_custom_call" | custom-call | flops 3623878656 | bytes 14680064 | tf_op jit(solution)/shard_map/pallas_call | solution.py:54
  167.6 5.1 %collective-permute-done.34.refs_7_.refs_1_ = bf16[4,64,1152]{2,1,0:T(8,128)(2,1)S(1)} collective-permute-done((bf16[4,64,1152]{2,1,0:T(8,128)(2,1)S(1)}, bf16[4,64,1152]{2,1,0:T(8,128)(2,1)S(1)}, u32[]{:S(2)}, u32[]{:S(2)}) %collective-permute-start.34) | collective-permute-done | bytes 589856 | tf_op jit(solution)/shard_map/ppermute | solution.py:22
  172.7 3.0 %collective-permute-done.36.refs_9_.refs_3_ = bf16[4,64,1152]{2,1,0:T(8,128)(2,1)S(1)} collective-permute-done((bf16[4,64,1152]{2,1,0:T(8,128)(2,1)S(1)}, bf16[4,64,1152]{2,1,0:T(8,128)(2,1)S(1)}, u32[]{:S(2)}, u32[]{:S(2)}) %collective-permute-start.36) | collective-permute-done | bytes 589856 | tf_op jit(solution)/shard_map/ppermute | solution.py:22
  175.7 3.0 %shard_map.99 = (f32[512,512]{1,0:T(8,128)S(1)}, f32[512,512]{1,0:T(8,128)S(1)}) custom-call(s32[4]{0:T(128)S(1)} %pad_add_fusion.where, bf16[4,512,1152]{2,1,0:T(8,128)(2,1)S(1)} %bitcast.100, f32[768,512]{1,0:T(8,128)S(1)} %shard_map.98.near_ref, bf16[4,64,1152]{2,1,0:T(8,128)(2,1)S(1)} %collective-permute-done.33.refs_6_.refs_0_, ...), custom_call_target="tpu_custom_call" | custom-call | flops 1207959552 | bytes 10485760 | tf_op jit(solution)/shard_map/pallas_call | solution.py:54
  178.8 12.3 %collective-permute-start.38 = (f32[512,512]{1,0:T(8,128)S(1)}, f32[512,512]{1,0:T(8,128)S(1)}, u32[]{:S(2)}, u32[]{:S(2)}) collective-permute-start(f32[512,512]{1,0:T(8,128)S(1)} %get-tuple-element.82), channel_id=1, source_target_pairs={{0,1},{1,0},{2,3},{3,2},{4,5},{5,4},{6,7},{7,6},{8,9},{9,8},{10,11... | collective-permute-start | bytes 3145736 | tf_op jit(solution)/shard_map/ppermute | solution.py:32
  191.1 9.1 %shard_map.97 = (f32[4,512,1152]{2,1,0:T(8,128)}, f32[1,1152]{1,0:T(1,128)S(1)}) custom-call(s32[4]{0:T(128)S(1)} %pad_add_fusion.where, bf16[512,512]{1,0:T(8,128)(2,1)S(1)} %copy-done.10, bf16[512,512]{1,0:T(8,128)(2,1)S(1)} %copy-done.13, bf16[4,128,1152]{2,1,0:T(8,128)(2,1)S(1)} %pad_maximum_fusion.1.refs_0_, ...), custom_call_target="tpu_custom_call" | custom-call | flops 4831838208 | bytes 20971520 | tf_op jit(solution)/shard_map/pallas_call | solution.py:54
  201.6 1.4 collective-permute-done.37
  204.9 4.3 %shard_map.100 = f32[1152,512]{1,0:T(8,128)} custom-call(s32[4]{0:T(128)S(1)} %pad_add_fusion.where, bf16[1152,512]{1,0:T(8,128)(2,1)S(1)} %bitcast.103, bf16[1152,512]{1,0:T(8,128)(2,1)S(1)} %bitcast.105, bf16[512,512]{1,0:T(8,128)(2,1)S(1)} %get-tuple-element.85.grad_ref, bf16[512,512]{1,0:T(8,128)(2,1)S(1)} %collective-permute-done.39.other_grad_ref), custom_call_target="tpu_custom_call" | custom-call | flops 1207959552 | bytes 6291456 | tf_op jit(solution)/shard_map/pallas_call | solution.py:54
  (132 shorter events, 32.9 us)
Async XLA Ops:
  7.7 4.5 %collective-permute-start = (bf16[512,512]{1,0:T(8,128)(2,1)S(1)}, bf16[512,512]{1,0:T(8,128)(2,1)S(1)}, u32[]{:S(2)}, u32[]{:S(2)}) collective-permute-start(bf16[512,512]{1,0:T(8,128)(2,1)S(1)} %get-tuple-element.45), channel_id=1, source_target_pairs={{0,1},{1,0},{2,3},{3,2},{4,5},{5,4},{6,7},{7,6},{8,9},{9,8},{10,11... | collective-permute-start | bytes 1572872 | tf_op jit(solution)/shard_map/ppermute | solution.py:32
  9.4 2.8 %collective-permute-start.1 = (bf16[16,32,144]{2,1,0:T(8,128)(2,1)S(1)}, bf16[16,32,144]{2,1,0:T(8,128)(2,1)S(1)}, u32[]{:S(2)}, u32[]{:S(2)}) collective-permute-start(bf16[16,32,144]{2,1,0:T(8,128)(2,1)S(1)} %bitcast.112), channel_id=1, source_target_pairs={{0,1},{1,0},{2,3},{3,2},{4,5},{5,4},{6,7},{7,6},{8,9},{9,8},{10,11... | collective-permute-start | bytes 442376 | tf_op jit(solution)/shard_map/ppermute | solution.py:32
  16.4 18.7 %collective-permute-start.2 = (bf16[4,64,1152]{2,1,0:T(8,128)(2,1)}, bf16[4,64,1152]{2,1,0:T(8,128)(2,1)}, u32[]{:S(2)}, u32[]{:S(2)}) collective-permute-start(bf16[4,64,1152]{2,1,0:T(8,128)(2,1)} %get-tuple-element.52), channel_id=1, source_target_pairs={{0,8},{8,16},{16,24},{24,0},{1,9},{9,17},{17,25},{25,1},{2,10},{10... | collective-permute-start | bytes 1769480 | tf_op jit(solution)/shard_map/ppermute | solution.py:22
  17.8 17.3 %collective-permute-start.3 = (bf16[4,64,1152]{2,1,0:T(8,128)(2,1)}, bf16[4,64,1152]{2,1,0:T(8,128)(2,1)}, u32[]{:S(2)}, u32[]{:S(2)}) collective-permute-start(bf16[4,64,1152]{2,1,0:T(8,128)(2,1)} %get-tuple-element.53), channel_id=1, source_target_pairs={{0,24},{8,0},{16,8},{24,16},{1,25},{9,1},{17,9},{25,17},{2,26},{10... | collective-permute-start | bytes 1769480 | tf_op jit(solution)/shard_map/ppermute | solution.py:22
  19.2 16.8 %collective-permute-start.4 = (bf16[4,64,1152]{2,1,0:T(8,128)(2,1)}, bf16[4,64,1152]{2,1,0:T(8,128)(2,1)}, u32[]{:S(2)}, u32[]{:S(2)}) collective-permute-start(bf16[4,64,1152]{2,1,0:T(8,128)(2,1)} %get-tuple-element.54), channel_id=1, source_target_pairs={{0,2},{2,4},{4,6},{6,0},{1,3},{3,5},{5,7},{7,1},{8,10},{10,12},{12... | collective-permute-start | bytes 1769480 | tf_op jit(solution)/shard_map/ppermute | solution.py:22
  20.9 15.1 %collective-permute-start.5 = (bf16[4,64,1152]{2,1,0:T(8,128)(2,1)}, bf16[4,64,1152]{2,1,0:T(8,128)(2,1)}, u32[]{:S(2)}, u32[]{:S(2)}) collective-permute-start(bf16[4,64,1152]{2,1,0:T(8,128)(2,1)} %get-tuple-element.55), channel_id=1, source_target_pairs={{0,6},{2,0},{4,2},{6,4},{1,7},{3,1},{5,3},{7,5},{8,14},{10,8},{12,... | collective-permute-start | bytes 1769480 | tf_op jit(solution)/shard_map/ppermute | solution.py:22
  40.3 33.3 %collective-permute-start.6 = (bf16[4,128,1152]{2,1,0:T(8,128)(2,1)}, bf16[4,128,1152]{2,1,0:T(8,128)(2,1)}, u32[]{:S(2)}, u32[]{:S(2)}) collective-permute-start(bf16[4,128,1152]{2,1,0:T(8,128)(2,1)} %get-tuple-element.56), channel_id=1, source_target_pairs={{0,8},{8,16},{16,24},{24,0},{1,9},{9,17},{17,25},{25,1},{2,10},{10... | collective-permute-start | bytes 3538952 | tf_op jit(solution)/shard_map/ppermute | solution.py:22
  40.4 33.2 %collective-permute-start.7 = (bf16[4,128,1152]{2,1,0:T(8,128)(2,1)}, bf16[4,128,1152]{2,1,0:T(8,128)(2,1)}, u32[]{:S(2)}, u32[]{:S(2)}) collective-permute-start(bf16[4,128,1152]{2,1,0:T(8,128)(2,1)} %get-tuple-element.57), channel_id=1, source_target_pairs={{0,24},{8,0},{16,8},{24,16},{1,25},{9,1},{17,9},{25,17},{2,26},{10... | collective-permute-start | bytes 3538952 | tf_op jit(solution)/shard_map/ppermute | solution.py:22
  43.1 26.8 %collective-permute-start.11 = (bf16[4,128,1152]{2,1,0:T(8,128)(2,1)}, bf16[4,128,1152]{2,1,0:T(8,128)(2,1)}, u32[]{:S(2)}, u32[]{:S(2)}) collective-permute-start(bf16[4,128,1152]{2,1,0:T(8,128)(2,1)} %get-tuple-element.59), channel_id=1, source_target_pairs={{0,2},{2,4},{4,6},{6,0},{1,3},{3,5},{5,7},{7,1},{8,10},{10,12},{12... | collective-permute-start | bytes 3538952 | tf_op jit(solution)/shard_map/ppermute | solution.py:22
  43.5 26.4 %collective-permute-start.12 = (bf16[4,128,1152]{2,1,0:T(8,128)(2,1)}, bf16[4,128,1152]{2,1,0:T(8,128)(2,1)}, u32[]{:S(2)}, u32[]{:S(2)}) collective-permute-start(bf16[4,128,1152]{2,1,0:T(8,128)(2,1)} %get-tuple-element.60), channel_id=1, source_target_pairs={{0,6},{2,0},{4,2},{6,4},{1,7},{3,1},{5,3},{7,5},{8,14},{10,8},{12,... | collective-permute-start | bytes 3538952 | tf_op jit(solution)/shard_map/ppermute | solution.py:22
  54.1 28.3 %all-to-all-start = ((f32[16,2,32,144]{3,2,1,0:T(8,128)}), f32[16,2,32,144]{3,2,1,0:T(8,128)}, u32[]{:S(2)}, u32[]{:S(2)}) async-start(f32[16,2,32,144]{3,2,1,0:T(8,128)} %copy.39), calls=%async_computation | async-start | bytes 2097152 | tf_op jit(solution)/shard_map/all_to_all | solution.py:386
  73.5 11.6 %collective-permute-start.15 = (bf16[4,32,1152]{2,1,0:T(8,128)(2,1)}, bf16[4,32,1152]{2,1,0:T(8,128)(2,1)}, u32[]{:S(2)}, u32[]{:S(2)}) collective-permute-start(bf16[4,32,1152]{2,1,0:T(8,128)(2,1)} %get-tuple-element.89), channel_id=1, source_target_pairs={{0,24},{8,0},{16,8},{24,16},{1,25},{9,1},{17,9},{25,17},{2,26},{10... | collective-permute-start | bytes 884744 | tf_op jit(solution)/shard_map/ppermute | solution.py:22
  77.2 9.5 %collective-permute-start.8 = (bf16[4,32,1152]{2,1,0:T(8,128)(2,1)S(1)}, bf16[4,32,1152]{2,1,0:T(8,128)(2,1)}, u32[]{:S(2)}, u32[]{:S(2)}) collective-permute-start(bf16[4,32,1152]{2,1,0:T(8,128)(2,1)S(1)} %get-tuple-element.91), channel_id=1, source_target_pairs={{0,2},{2,4},{4,6},{6,0},{1,3},{3,5},{5,7},{7,1},{8,10},{10,12},{12... | collective-permute-start | bytes 884744 | tf_op jit(solution)/shard_map/ppermute | solution.py:22
  77.3 12.0 %collective-permute-start.10 = (bf16[4,32,1152]{2,1,0:T(8,128)(2,1)S(1)}, bf16[4,32,1152]{2,1,0:T(8,128)(2,1)}, u32[]{:S(2)}, u32[]{:S(2)}) collective-permute-start(bf16[4,32,1152]{2,1,0:T(8,128)(2,1)S(1)} %get-tuple-element.92), channel_id=1, source_target_pairs={{0,6},{2,0},{4,2},{6,4},{1,7},{3,1},{5,3},{7,5},{8,14},{10,8},{12,... | collective-permute-start | bytes 884744 | tf_op jit(solution)/shard_map/ppermute | solution.py:22
  81.4 9.5 %collective-permute-start.9 = (bf16[4,32,1152]{2,1,0:T(8,128)(2,1)S(1)}, bf16[4,32,1152]{2,1,0:T(8,128)(2,1)}, u32[]{:S(2)}, u32[]{:S(2)}) collective-permute-start(bf16[4,32,1152]{2,1,0:T(8,128)(2,1)S(1)} %get-tuple-element.93), channel_id=1, source_target_pairs={{0,4},{2,6},{4,0},{6,2},{1,5},{3,7},{5,1},{7,3},{8,12},{10,14},{12... | collective-permute-start | bytes 884744 | tf_op jit(solution)/shard_map/ppermute | solution.py:22
  84.1 10.4 %collective-permute-start.13 = (bf16[4,32,1152]{2,1,0:T(8,128)(2,1)S(1)}, bf16[4,32,1152]{2,1,0:T(8,128)(2,1)S(1)}, u32[]{:S(2)}, u32[]{:S(2)}) collective-permute-start(bf16[4,32,1152]{2,1,0:T(8,128)(2,1)S(1)} %copy-done.20), channel_id=1, source_target_pairs={{0,8},{8,16},{16,24},{24,0},{1,9},{9,17},{17,25},{25,1},{2,10},{10... | collective-permute-start | bytes 884744 | tf_op jit(solution)/shard_map/ppermute | solution.py:22
  85.2 9.3 %collective-permute-start.14 = (bf16[4,32,1152]{2,1,0:T(8,128)(2,1)S(1)}, bf16[4,32,1152]{2,1,0:T(8,128)(2,1)S(1)}, u32[]{:S(2)}, u32[]{:S(2)}) collective-permute-start(bf16[4,32,1152]{2,1,0:T(8,128)(2,1)S(1)} %copy-done.19), channel_id=1, source_target_pairs={{0,16},{8,24},{16,0},{24,8},{1,17},{9,25},{17,1},{25,9},{2,18},{10... | collective-permute-start | bytes 884744 | tf_op jit(solution)/shard_map/ppermute | solution.py:22
  95.9 66.0 %slice-start = ((s8[4718592]{0:T(1024)(128)(4,1)}), s8[4194304]{0:T(1024)(128)(4,1)S(1)}, s32[]{:S(2)}) async-start(s8[4718592]{0:T(1024)(128)(4,1)} %bitcast.99), calls=%async_computation.1 | async-start | bytes 8388608
  96.0 8.8 %collective-permute-start.16 = (bf16[2,32,1152]{2,1,0:T(8,128)(2,1)S(1)}, bf16[2,32,1152]{2,1,0:T(8,128)(2,1)S(1)}, u32[]{:S(2)}, u32[]{:S(2)}) collective-permute-start(bf16[2,32,1152]{2,1,0:T(8,128)(2,1)S(1)} %get-tuple-element.96), channel_id=1, source_target_pairs={{0,32},{32,64},{64,96},{1,33},{33,65},{65,97},{2,34},{34,66},{66,9... | collective-permute-start | bytes 442376 | tf_op jit(solution)/shard_map/ppermute | solution.py:28
  99.5 5.3 %collective-permute-start.18 = (bf16[2,32,1152]{2,1,0:T(8,128)(2,1)S(1)}, bf16[2,32,1152]{2,1,0:T(8,128)(2,1)S(1)}, u32[]{:S(2)}, u32[]{:S(2)}) collective-permute-start(bf16[2,32,1152]{2,1,0:T(8,128)(2,1)S(1)} %get-tuple-element.97), channel_id=1, source_target_pairs={{0,96},{1,97},{2,98},{3,99},{4,100},{5,101},{6,102},{7,103},{8,104... | collective-permute-start | bytes 442376 | tf_op jit(solution)/shard_map/ppermute | solution.py:28
  102.3 4.6 %collective-permute-start.17 = (bf16[2,32,1152]{2,1,0:T(8,128)(2,1)S(1)}, bf16[2,32,1152]{2,1,0:T(8,128)(2,1)S(1)}, u32[]{:S(2)}, u32[]{:S(2)}) collective-permute-start(bf16[2,32,1152]{2,1,0:T(8,128)(2,1)S(1)} %get-tuple-element.98), channel_id=1, source_target_pairs={{0,64},{32,96},{1,65},{33,97},{2,66},{34,98},{3,67},{35,99},{4,68}... | collective-permute-start | bytes 442376 | tf_op jit(solution)/shard_map/ppermute | solution.py:28
  106.9 7.1 %collective-permute-start.21 = (bf16[2,32,1152]{2,1,0:T(8,128)(2,1)S(1)}, bf16[2,32,1152]{2,1,0:T(8,128)(2,1)S(1)}, u32[]{:S(2)}, u32[]{:S(2)}) collective-permute-start(bf16[2,32,1152]{2,1,0:T(8,128)(2,1)S(1)} %fusion.25), channel_id=1, source_target_pairs={{96,0},{97,1},{98,2},{99,3},{100,4},{101,5},{102,6},{103,7},{104,8... | collective-permute-start | bytes 442376 | tf_op jit(solution)/shard_map/ppermute | solution.py:28
  108.2 7.4 %collective-permute-start.20 = (bf16[2,32,1152]{2,1,0:T(8,128)(2,1)S(1)}, bf16[2,32,1152]{2,1,0:T(8,128)(2,1)S(1)}, u32[]{:S(2)}, u32[]{:S(2)}) collective-permute-start(bf16[2,32,1152]{2,1,0:T(8,128)(2,1)S(1)} %fusion.25), channel_id=1, source_target_pairs={{64,0},{96,32},{65,1},{97,33},{66,2},{98,34},{67,3},{99,35},{68,4}... | collective-permute-start | bytes 442376 | tf_op jit(solution)/shard_map/ppermute | solution.py:28
  109.5 6.1 %collective-permute-start.19 = (bf16[2,32,1152]{2,1,0:T(8,128)(2,1)S(1)}, bf16[2,32,1152]{2,1,0:T(8,128)(2,1)S(1)}, u32[]{:S(2)}, u32[]{:S(2)}) collective-permute-start(bf16[2,32,1152]{2,1,0:T(8,128)(2,1)S(1)} %fusion.25), channel_id=1, source_target_pairs={{32,0},{64,32},{96,64},{33,1},{65,33},{97,65},{34,2},{66,34},{98,6... | collective-permute-start | bytes 442376 | tf_op jit(solution)/shard_map/ppermute | solution.py:28
  115.8 10.0 %collective-permute-start.24 = (bf16[4,32,1152]{2,1,0:T(8,128)(2,1)S(1)}, bf16[4,32,1152]{2,1,0:T(8,128)(2,1)S(1)}, u32[]{:S(2)}, u32[]{:S(2)}) collective-permute-start(bf16[4,32,1152]{2,1,0:T(8,128)(2,1)S(1)} %get-tuple-element.95), channel_id=1, source_target_pairs={{0,2},{2,4},{4,6},{6,0},{1,3},{3,5},{5,7},{7,1},{8,10},{10,12},{12... | collective-permute-start | bytes 884744 | tf_op jit(solution)/shard_map/ppermute | solution.py:22
  116.3 13.3 %collective-permute-start.23 = (bf16[4,32,1152]{2,1,0:T(8,128)(2,1)S(1)}, bf16[4,32,1152]{2,1,0:T(8,128)(2,1)S(1)}, u32[]{:S(2)}, u32[]{:S(2)}) collective-permute-start(bf16[4,32,1152]{2,1,0:T(8,128)(2,1)S(1)} %get-tuple-element.95), channel_id=1, source_target_pairs={{0,4},{2,6},{4,0},{6,2},{1,5},{3,7},{5,1},{7,3},{8,12},{10,14},{12... | collective-permute-start | bytes 884744 | tf_op jit(solution)/shard_map/ppermute | solution.py:22
  117.4 12.2 %collective-permute-start.22 = (bf16[4,32,1152]{2,1,0:T(8,128)(2,1)S(1)}, bf16[4,32,1152]{2,1,0:T(8,128)(2,1)S(1)}, u32[]{:S(2)}, u32[]{:S(2)}) collective-permute-start(bf16[4,32,1152]{2,1,0:T(8,128)(2,1)S(1)} %get-tuple-element.95), channel_id=1, source_target_pairs={{0,6},{2,0},{4,2},{6,4},{1,7},{3,1},{5,3},{7,5},{8,14},{10,8},{12,... | collective-permute-start | bytes 884744 | tf_op jit(solution)/shard_map/ppermute | solution.py:22
  119.4 16.7 %copy-start.17 = (bf16[512,1152]{0,1:T(8,128)(2,1)S(1)}, bf16[512,1152]{0,1:T(8,128)(2,1)}, u32[]{:S(2)}) copy-start(bf16[512,1152]{0,1:T(8,128)(2,1)} %copy.45) | copy-start | bytes 3538948
  119.4 42.5 %slice-start.1 = ((s8[4718592]{0:T(1024)(128)(4,1)}), s8[524288]{0:T(1024)(128)(4,1)S(1)}, s32[]{:S(2)}) async-start(s8[4718592]{0:T(1024)(128)(4,1)} %bitcast.99), calls=%async_computation.2 | async-start | bytes 1048576
  119.4 13.0 %collective-permute-start.30 = (bf16[4,32,1152]{2,1,0:T(8,128)(2,1)S(1)}, bf16[4,32,1152]{2,1,0:T(8,128)(2,1)S(1)}, u32[]{:S(2)}, u32[]{:S(2)}) collective-permute-start(bf16[4,32,1152]{2,1,0:T(8,128)(2,1)S(1)} %get-tuple-element.94), channel_id=1, source_target_pairs={{0,8},{8,16},{16,24},{24,0},{1,9},{9,17},{17,25},{25,1},{2,10},{10... | collective-permute-start | bytes 884744 | tf_op jit(solution)/shard_map/ppermute | solution.py:22
  119.8 12.7 %collective-permute-start.29 = (bf16[4,32,1152]{2,1,0:T(8,128)(2,1)S(1)}, bf16[4,32,1152]{2,1,0:T(8,128)(2,1)S(1)}, u32[]{:S(2)}, u32[]{:S(2)}) collective-permute-start(bf16[4,32,1152]{2,1,0:T(8,128)(2,1)S(1)} %get-tuple-element.94), channel_id=1, source_target_pairs={{0,16},{8,24},{16,0},{24,8},{1,17},{9,25},{17,1},{25,9},{2,18},{10... | collective-permute-start | bytes 884744 | tf_op jit(solution)/shard_map/ppermute | solution.py:22
  125.8 7.4 %collective-permute-start.28 = (bf16[4,32,1152]{2,1,0:T(8,128)(2,1)S(1)}, bf16[4,32,1152]{2,1,0:T(8,128)(2,1)S(1)}, u32[]{:S(2)}, u32[]{:S(2)}) collective-permute-start(bf16[4,32,1152]{2,1,0:T(8,128)(2,1)S(1)} %get-tuple-element.94), channel_id=1, source_target_pairs={{0,24},{8,0},{16,8},{24,16},{1,25},{9,1},{17,9},{25,17},{2,26},{10... | collective-permute-start | bytes 884744 | tf_op jit(solution)/shard_map/ppermute | solution.py:22
  129.7 26.3 %collective-permute-start.27 = (bf16[4,128,1152]{2,1,0:T(8,128)(2,1)S(1)}, bf16[4,128,1152]{2,1,0:T(8,128)(2,1)S(1)}, u32[]{:S(2)}, u32[]{:S(2)}) collective-permute-start(bf16[4,128,1152]{2,1,0:T(8,128)(2,1)S(1)} %pad_maximum_fusion.1.refs_0_), channel_id=1, source_target_pairs={{0,8},{8,16},{16,24},{24,0},{1,9},{9,17},{17,25},{25,1},{2,10},{10... | collective-permute-start | bytes 3538952 | tf_op jit(solution)/shard_map/ppermute | solution.py:22
  129.8 26.4 %collective-permute-start.26 = (bf16[4,128,1152]{2,1,0:T(8,128)(2,1)S(1)}, bf16[4,128,1152]{2,1,0:T(8,128)(2,1)S(1)}, u32[]{:S(2)}, u32[]{:S(2)}) collective-permute-start(bf16[4,128,1152]{2,1,0:T(8,128)(2,1)S(1)} %pad_maximum_fusion.1.refs_0_), channel_id=1, source_target_pairs={{0,24},{8,0},{16,8},{24,16},{1,25},{9,1},{17,9},{25,17},{2,26},{10... | collective-permute-start | bytes 3538952 | tf_op jit(solution)/shard_map/ppermute | solution.py:22
  133.4 25.6 %collective-permute-start.32 = (bf16[4,128,1152]{2,1,0:T(8,128)(2,1)S(1)}, bf16[4,128,1152]{2,1,0:T(8,128)(2,1)S(1)}, u32[]{:S(2)}, u32[]{:S(2)}) collective-permute-start(bf16[4,128,1152]{2,1,0:T(8,128)(2,1)S(1)} %pad_maximum_fusion.2.refs_3_), channel_id=1, source_target_pairs={{0,2},{2,4},{4,6},{6,0},{1,3},{3,5},{5,7},{7,1},{8,10},{10,12},{12... | collective-permute-start | bytes 3538952 | tf_op jit(solution)/shard_map/ppermute | solution.py:22
  133.4 25.7 %collective-permute-start.31 = (bf16[4,128,1152]{2,1,0:T(8,128)(2,1)S(1)}, bf16[4,128,1152]{2,1,0:T(8,128)(2,1)S(1)}, u32[]{:S(2)}, u32[]{:S(2)}) collective-permute-start(bf16[4,128,1152]{2,1,0:T(8,128)(2,1)S(1)} %pad_maximum_fusion.2.refs_3_), channel_id=1, source_target_pairs={{0,6},{2,0},{4,2},{6,4},{1,7},{3,1},{5,3},{7,5},{8,14},{10,8},{12,... | collective-permute-start | bytes 3538952 | tf_op jit(solution)/shard_map/ppermute | solution.py:22
  136.1 25.8 %collective-permute-start.25 = (bf16[512,1152]{0,1:T(8,128)(2,1)S(1)}, bf16[512,1152]{0,1:T(8,128)(2,1)S(1)}, u32[]{:S(2)}, u32[]{:S(2)}) collective-permute-start(bf16[512,1152]{0,1:T(8,128)(2,1)S(1)} %copy-done.17), channel_id=1, source_target_pairs={{0,1},{1,0},{2,3},{3,2},{4,5},{5,4},{6,7},{7,6},{8,9},{9,8},{10,11... | collective-permute-start | bytes 3538952 | tf_op jit(solution)/shard_map/ppermute | solution.py:32
  156.1 16.6 %collective-permute-start.34 = (bf16[4,64,1152]{2,1,0:T(8,128)(2,1)S(1)}, bf16[4,64,1152]{2,1,0:T(8,128)(2,1)S(1)}, u32[]{:S(2)}, u32[]{:S(2)}) collective-permute-start(bf16[4,64,1152]{2,1,0:T(8,128)(2,1)S(1)} %slice.97), channel_id=1, source_target_pairs={{0,8},{8,16},{16,24},{24,0},{1,9},{9,17},{17,25},{25,1},{2,10},{10... | collective-permute-start | bytes 1769480 | tf_op jit(solution)/shard_map/ppermute | solution.py:22
  156.2 16.5 %collective-permute-start.33 = (bf16[4,64,1152]{2,1,0:T(8,128)(2,1)S(1)}, bf16[4,64,1152]{2,1,0:T(8,128)(2,1)S(1)}, u32[]{:S(2)}, u32[]{:S(2)}) collective-permute-start(bf16[4,64,1152]{2,1,0:T(8,128)(2,1)S(1)} %slice.96), channel_id=1, source_target_pairs={{0,24},{8,0},{16,8},{24,16},{1,25},{9,1},{17,9},{25,17},{2,26},{10... | collective-permute-start | bytes 1769480 | tf_op jit(solution)/shard_map/ppermute | solution.py:22
  159.0 16.7 %collective-permute-start.36 = (bf16[4,64,1152]{2,1,0:T(8,128)(2,1)S(1)}, bf16[4,64,1152]{2,1,0:T(8,128)(2,1)S(1)}, u32[]{:S(2)}, u32[]{:S(2)}) collective-permute-start(bf16[4,64,1152]{2,1,0:T(8,128)(2,1)S(1)} %slice.99), channel_id=1, source_target_pairs={{0,2},{2,4},{4,6},{6,0},{1,3},{3,5},{5,7},{7,1},{8,10},{10,12},{12... | collective-permute-start | bytes 1769480 | tf_op jit(solution)/shard_map/ppermute | solution.py:22
  159.2 16.5 %collective-permute-start.35 = (bf16[4,64,1152]{2,1,0:T(8,128)(2,1)S(1)}, bf16[4,64,1152]{2,1,0:T(8,128)(2,1)S(1)}, u32[]{:S(2)}, u32[]{:S(2)}) collective-permute-start(bf16[4,64,1152]{2,1,0:T(8,128)(2,1)S(1)} %slice.98), channel_id=1, source_target_pairs={{0,6},{2,0},{4,2},{6,4},{1,7},{3,1},{5,3},{7,5},{8,14},{10,8},{12,... | collective-permute-start | bytes 1769480 | tf_op jit(solution)/shard_map/ppermute | solution.py:22
  167.6 23.5 %copy-start.10 = (bf16[512,512]{1,0:T(8,128)(2,1)S(1)}, bf16[512,512]{1,0:T(8,128)(2,1)}, u32[]{:S(2)}) copy-start(bf16[512,512]{1,0:T(8,128)(2,1)} %copy-done.8) | copy-start | bytes 1572868
  167.6 23.5 %copy-start.13 = (bf16[512,512]{1,0:T(8,128)(2,1)S(1)}, bf16[512,512]{1,0:T(8,128)(2,1)}, u32[]{:S(2)}) copy-start(bf16[512,512]{1,0:T(8,128)(2,1)} %copy-done.11) | copy-start | bytes 1572868
  178.7 21.4 %copy-start.7 = (f32[512,512]{1,0:T(8,128)S(1)}, f32[512,512]{1,0:T(8,128)}, u32[]{:S(2)}) copy-start(f32[512,512]{1,0:T(8,128)} %copy-done.6) | copy-start | bytes 3145732
  178.8 21.4 %collective-permute-start.38 = (f32[512,512]{1,0:T(8,128)S(1)}, f32[512,512]{1,0:T(8,128)S(1)}, u32[]{:S(2)}, u32[]{:S(2)}) collective-permute-start(f32[512,512]{1,0:T(8,128)S(1)} %get-tuple-element.82), channel_id=1, source_target_pairs={{0,1},{1,0},{2,3},{3,2},{4,5},{5,4},{6,7},{7,6},{8,9},{9,8},{10,11... | collective-permute-start | bytes 3145736 | tf_op jit(solution)/shard_map/ppermute | solution.py:32
  201.0 3.9 %collective-permute-start.39 = (bf16[512,512]{1,0:T(8,128)(2,1)S(1)}, bf16[512,512]{1,0:T(8,128)(2,1)S(1)}, u32[]{:S(2)}, u32[]{:S(2)}) collective-permute-start(bf16[512,512]{1,0:T(8,128)(2,1)S(1)} %get-tuple-element.85.grad_ref), channel_id=1, source_target_pairs={{0,1},{1,0},{2,3},{3,2},{4,5},{5,4},{6,7},{7,6},{8,9},{9,8},{10,11... | collective-permute-start | bytes 1572872 | tf_op jit(solution)/shard_map/ppermute | solution.py:32
  201.1 1.9 collective-permute-start.37
  203.1 1.2 collective-permute-start.40
  (20 other events, 74.1 us)

commit v4 on v3

--- a/solution.py
+++ b/solution.py
@@ -10,7 +10,7 @@
 
 LAYER, LX, LZ, TOK = "layer", "lx", "lz", "tok"
 BF16, F32 = jnp.bfloat16, jnp.float32
-VMEM_MIB = 28
+VMEM_MIB, LARGE_MIB = 28, 56
 
 
 def smooth(values):
@@ -50,7 +50,7 @@
     return [value] + [shift(value, axis, -k) for k in range(1, n)]
 
 
-def call(kernel, where, inputs, in_specs, outs, out_specs, grid, scratch, flops, moved, aliases=None):
+def call(kernel, where, inputs, in_specs, outs, out_specs, grid, scratch, flops, moved, aliases=None, mib=VMEM_MIB):
     return pl.pallas_call(
         kernel,
         out_shape=[jax.ShapeDtypeStruct(shape, dtype) for shape, dtype in outs],
@@ -62,7 +62,7 @@
             scratch_shapes=scratch,
         ),
         input_output_aliases=aliases or {},
-        compiler_params=pltpu.CompilerParams(vmem_limit_bytes=VMEM_MIB * 2**20),
+        compiler_params=pltpu.CompilerParams(vmem_limit_bytes=mib * 2**20),
         cost_estimate=pl.CostEstimate(flops=flops, bytes_accessed=moved, transcendentals=0),
     )(where, *inputs)
 
@@ -161,6 +161,7 @@
         [],
         2 * layers * used * feats * width,
         8 * 2**20,
+        mib=VMEM_MIB if kernel is far_kernel else LARGE_MIB,
     )
 
 
@@ -361,8 +362,7 @@
         return turned(turned(blocks, 0, x), 1, z).reshape(rows.shape)
 
     pre, own_lat, crossed = encode(where, inputs, enc_weight[0], enc_bias, ring)
-    own_out = resid_out[0].reshape(ring * ring, piece, -1)
-    other_lat, other_out = lax.optimization_barrier((swap(crossed), swap(own_out)))
+    other_lat = swap(crossed)
 
     far_a0, far_a1, far_b0, far_b1 = rebuild(far_kernel, where, own_lat, other_lat, weights, width)
     parts = [(far_a0, LX, 1), (far_a1, LX, -1), (far_b0, LZ, 1), (far_b1, LZ, -1)]
@@ -370,6 +370,9 @@
     own_a, up_a, down_a, own_b, up_b, down_b = rebuild(
         near_kernel, where, own_lat, other_lat, weights, width
     )
+    out_in, own_a = lax.optimization_barrier((resid_out[0], own_a))
+    base = dec_bias[0] - out_in.astype(F32).reshape(ring * ring, piece, -1)
+    base = lax.all_to_all(base, (LX, LZ), 0, 0, tiled=True)
     folded = fold(where, (up_a, down_a, up_b, down_b), got)
     got = [shift(value, *part[1:]) for value, part in zip(folded, parts, strict=True)]
 
@@ -379,18 +382,21 @@
     to_other = lax.dynamic_slice_in_dim(ordered, (1 - c) * width, width, 1)
     own_in = own_in.T
 
-    own_out, other_out, own_in, to_other = lax.optimization_barrier(
-        (own_out, other_out, own_in, to_other)
-    )
-    base = dec_bias[0] - jnp.stack([own_out, other_out], 1).astype(F32)
-    base = lax.all_to_all(base, (LX, LZ), 0, 0, tiled=True)
-    base = lax.dynamic_slice_in_dim(base, c * (ring * ring // 2), ring * ring // 2, 0)
-    base = base.transpose(1, 2, 0, 3).reshape(2, piece, width)
-
-    a = total([own_a, *got[:2]]).reshape(layers, ring, piece, width)
-    b = total([own_b, *got[2:]]).reshape(layers, ring, piece, width)
-    a = spread([a[:, 0]] + [a[:, i].astype(BF16) for i in range(1, ring)], LZ)
-    b = spread([b[:, 0]] + [b[:, i].astype(BF16) for i in range(1, ring)], LX)
+    base, own_in, to_other = lax.optimization_barrier((base, own_in, to_other))
+    halves = base.reshape(2, ring * ring // 2, piece, -1)
+    own_base, other_base = (
+        lax.dynamic_index_in_dim(halves, core, 0, False).transpose(1, 0, 2).reshape(piece, width)
+        for core in (c, 1 - c)
+    )
+    base = jnp.stack([own_base, swap(other_base)])
+
+    def settled(own, below, above):
+        cuts = [slice(i * piece, (i + 1) * piece) for i in range(ring)]
+        sums = [total([v[:, cut] for v in (own, below, above)]) for cut in cuts]
+        return [sums[0]] + [v.astype(BF16) for v in sums[1:]]
+
+    a = spread(settled(own_a, *got[:2]), LZ)
+    b = spread(settled(own_b, *got[2:]), LX)
     base, b[3] = lax.optimization_barrier((base, b[3]))
     a, b = total(a), total(b)
     pieces = jnp.stack([a, b], 1)

time: 210 us -> 202 us (0.962)
  starting transfers between devices: 93.9 us -> 84.4 us
  local copies, waits for them, and re-layouts: 23.3 us -> 14.3 us
  waiting for transfers between devices: 38.7 us -> 45.9 us
    ppermute x28, waiting for transfers between devices: 30 us -> 37.2 us  [shift(): return lax.ppermute(value, axis, [(i, (i + step) % n) for i in range(n)])]
    unnamed x55 -> x45, local copies, waits for them, and re-layouts: 13 us -> 6.57 us
    ppermute x7, starting transfers between devices: 34.7 us -> 28.5 us  [swap(): return lax.ppermute(value, TOK, [(0, 1), (1, 0)])]
    convert_element_type x0 -> x2, other arithmetic: none -> 4.81 us  [settled(): return [sums[0]] + [v.astype(BF16) for v in sums[1:]]]
    add x2 -> x0, other arithmetic: 4.68 us -> none  [total(): return functools.reduce(jnp.add, [v.astype(F32) for v in values])]
    ppermute x28, starting transfers between devices: 42.3 us -> 39.1 us  [shift(): return lax.ppermute(value, axis, [(i, (i + step) % n) for i in range(n)])]
  transfers between devices with their start and end apart: 42 -> 42, of which waited for: 15 -> 15; matrix products, arithmetic and copies ran while one was open for 10% -> 10% of each run, Pallas kernels for 10% -> 14%
where the time goes in v4:
time: 202 us; the launch traced here: 201 us
  starting transfers between devices  84.4 us (42%)
  waiting for transfers between devices  45.9 us (23%)
  Pallas kernels  41.7 us (21%)
  local copies, waits for them, and re-layouts  14.3 us (7%)
  other arithmetic  13.5 us (7%)
    pallas_call x8, Pallas kernels, call(): pl.pallas_call(kernel, out_shape=[jax.ShapeDtypeStruct(shape, dtype) for...  41.7 us
    ppermute x28, starting transfers between devices, shift(): return lax.ppermute(value, axis, [(i, (i + step) % n) for i in range(n)])  39.1 us
    ppermute x28, waiting for transfers between devices, shift(): return lax.ppermute(value, axis, [(i, (i + step) % n) for i in range(n)])  37.2 us
    ppermute x7, starting transfers between devices, swap(): return lax.ppermute(value, TOK, [(0, 1), (1, 0)])  28.5 us
    ppermute x6, starting transfers between devices, send_up(): return lax.ppermute(value, LAYER, pairs)  12.5 us
    ppermute x6, waiting for transfers between devices, send_up(): return lax.ppermute(value, LAYER, pairs)  6.85 us
    unnamed x45, local copies, waits for them, and re-layouts  6.57 us
    convert_element_type x2, other arithmetic, settled(): return [sums[0]] + [v.astype(BF16) for v in sums[1:]]  4.81 us
  transfers between devices with their start and end apart: 42, of which 15 were waited for; matrix products, arithmetic and copies ran while one was open for 10% of the time, Pallas kernels for 14%

profile of v4, /device:TPU:1, one launch (start us, length us, event | category | flops | bytes accessed | tf_op | source)
XLA Modules:
  0.0 200.9 jit_solution(12084917008377575143)
XLA Ops:
  0.7 1.7 copy-done.1
  2.4 1.7 copy-done.3
  4.7 3.0 %shard_map.93 = (f32[512,512]{1,0:T(8,128)S(1)}, bf16[512,512]{1,0:T(8,128)(2,1)S(1)}, bf16[512,512]{1,0:T(8,128)(2,1)S(1)}) custom-call(s32[4]{0:T(128)S(1)} %pad_add_fusion.where, bf16[512,2304]{1,0:T(8,128)(2,1)S(1)} %bitcast.75, bf16[2304,512]{1,0:T(8,128)(2,1)S(1)} %bitcast.78, f32[1,512]{1,0:T(1,128)S(1)} %copy-done.13), custom_call_target="tpu_custom_call" | custom-call | flops 1207959552 | bytes 8388608 | tf_op jit(solution)/shard_map/pallas_call | solution.py:54
  8.7 1.4 collective-permute-start
  10.2 2.7 %dynamic-slice_bitcast_fusion.w_ref = bf16[4,512,1152]{2,1,0:T(8,128)(2,1)S(1)} fusion(bf16[1,4,512,2304]{3,2,1,0:T(8,128)(2,1)} %param.10, s32[]{:T(128)S(6)} %select_n.26), kind=kLoop, calls=%fused_computation.4 | loop fusion | bytes 9437188 | tf_op jit(solution)/shard_map/dynamic_slice | solution.py:358
  12.9 4.2 %shard_map.95 = (bf16[4,64,1152]{2,1,0:T(8,128)(2,1)}, bf16[4,64,1152]{2,1,0:T(8,128)(2,1)}, bf16[4,64,1152]{2,1,0:T(8,128)(2,1)}, bf16[4,64,1152]{2,1,0:T(8,128)(2,1)}) custom-call(s32[4]{0:T(128)S(1)} %pad_add_fusion.where, bf16[512,512]{1,0:T(8,128)(2,1)S(1)} %get-tuple-element.43.own_ref, bf16[512,512]{1,0:T(8,128)(2,1)S(1)} %collective-permute-done.other_ref, ...), custom_call_target="tpu_custom_call" | custom-call | flops 1207959552 | bytes 8388608 | tf_op jit(solution)/shard_map/pallas_call | solution.py:54
  19.9 1.7 collective-permute-start.3
  21.6 2.1 %collective-permute-start.4 = (bf16[4,64,1152]{2,1,0:T(8,128)(2,1)}, bf16[4,64,1152]{2,1,0:T(8,128)(2,1)S(1)}, u32[]{:S(2)}, u32[]{:S(2)}) collective-permute-start(bf16[4,64,1152]{2,1,0:T(8,128)(2,1)} %get-tuple-element.54), channel_id=1, source_target_pairs={{0,6},{2,0},{4,2},{6,4},{1,7},{3,1},{5,3},{7,5},{8,14},{10,8},{12,... | collective-permute-start | bytes 1769480 | tf_op jit(solution)/shard_map/ppermute | solution.py:22
  24.6 9.0 %shard_map.94 = (f32[4,128,1152]{2,1,0:T(8,128)}, bf16[4,128,1152]{2,1,0:T(8,128)(2,1)}, bf16[4,128,1152]{2,1,0:T(8,128)(2,1)}, f32[4,128,1152]{2,1,0:T(8,128)},...) custom-call(s32[4]{0:T(128)} %copy-done.11, bf16[512,512]{1,0:T(8,128)(2,1)} %copy-done.7, ...), custom_call_target="tpu_custom_call" | custom-call | flops 3623878656 | bytes 8388608 | tf_op jit(solution)/shard_map/pallas_call | solution.py:54
  34.4 4.2 %all-to-all-start = ((f32[16,32,144]{2,1,0:T(8,128)}), f32[16,32,144]{2,1,0:T(8,128)}, u32[]{:S(2)}, u32[]{:S(2)}) async-start(f32[16,32,144]{2,1,0:T(8,128)} %convert_subtract_fusion), calls=%async_computation | async-start | bytes 1048576 | tf_op jit(solution)/shard_map/all_to_all | solution.py:375
  38.8 3.5 %shard_map.96 = (bf16[4,128,1152]{2,1,0:T(8,128)(2,1)S(1)}, bf16[4,128,1152]{2,1,0:T(8,128)(2,1)}, bf16[4,128,1152]{2,1,0:T(8,128)(2,1)}, bf16[4,128,1152]{2,1,0:T(8,128)(2,1)}) custom-call(s32[4]{0:T(128)S(1)} %copy-done.12, bf16[4,128,1152]{2,1,0:T(8,128)(2,1)S(1)} %copy-done.4, ...), custom_call_target="tpu_custom_call", output_to_operand_aliasing={{0}: (1, {}), {1}: (2, {}), {2}: (3, {}), {3}: (4, {})} | custom-call | flops 2359296 | bytes 7077888 | tf_op jit(solution)/shard_map/pallas_call | solution.py:54
  43.4 1.5 collective-permute-start.6
  46.1 1.5 collective-permute-start.11
  49.6 1.5 copy.30
  53.8 2.5 %collective-permute-start.14 = (f32[32,1152]{1,0:T(8,128)}, f32[32,1152]{1,0:T(8,128)}, u32[]{:S(2)}, u32[]{:S(2)}) collective-permute-start(f32[32,1152]{1,0:T(8,128)} %reshape.39), channel_id=1, source_target_pairs={{0,1},{1,0},{2,3},{3,2},{4,5},{5,4},{6,7},{7,6},{8,9},{9,8},{10,11... | collective-permute-start | bytes 442376 | tf_op jit(solution)/shard_map/ppermute | solution.py:32
  56.3 17.1 %collective-permute-done.10 = bf16[4,128,1152]{2,1,0:T(8,128)(2,1)} collective-permute-done((bf16[4,128,1152]{2,1,0:T(8,128)(2,1)}, bf16[4,128,1152]{2,1,0:T(8,128)(2,1)}, u32[]{:S(2)}, u32[]{:S(2)}) %collective-permute-start.10) | collective-permute-done | bytes 1179680 | tf_op jit(solution)/shard_map/ppermute | solution.py:22
  73.4 2.4 %add_convert_fusion.2 = (bf16[4,32,1152]{2,1,0:T(8,128)(2,1)S(1)}, bf16[4,32,1152]{2,1,0:T(8,128)(2,1)S(1)}, bf16[4,32,1152]{2,1,0:T(8,128)(2,1)S(1)}) fusion(f32[4,128,1152]{2,1,0:T(8,128)} %get-tuple-element.57, bf16[4,128,1152]{2,1,0:T(8,128)(2,1)} %collective-permute-done.11, bf16[4,128,1152]{2,1,0:T(8,128)(2,1)} %collective-permute-done.10), kind=kLoop, calls=%fused_computation.27 | loop fusion | flops 2211840 | bytes 4423680 | tf_op jit(solution)/shard_map/convert_element_type | solution.py:396
  76.3 2.4 %add_convert_fusion.5 = (bf16[4,32,1152]{2,1,0:T(8,128)(2,1)}, bf16[4,32,1152]{2,1,0:T(8,128)(2,1)S(1)}, bf16[4,32,1152]{2,1,0:T(8,128)(2,1)S(1)}) fusion(f32[4,128,1152]{2,1,0:T(8,128)S(1)} %copy-done.14, bf16[4,128,1152]{2,1,0:T(8,128)(2,1)} %collective-permute-done.6, bf16[4,128,1152]{2,1,0:T(8,128)(2,1)} %collective-permute-done.5), kind=kLoop, calls=%fused_computation.31 | loop fusion | flops 2211840 | bytes 4423680 | tf_op jit(solution)/shard_map/convert_element_type | solution.py:396
  79.3 2.1 %collective-permute-start.9 = (bf16[4,32,1152]{2,1,0:T(8,128)(2,1)S(1)}, bf16[4,32,1152]{2,1,0:T(8,128)(2,1)}, u32[]{:S(2)}, u32[]{:S(2)}) collective-permute-start(bf16[4,32,1152]{2,1,0:T(8,128)(2,1)S(1)} %get-tuple-element.88), channel_id=1, source_target_pairs={{0,6},{2,0},{4,2},{6,4},{1,7},{3,1},{5,3},{7,5},{8,14},{10,8},{12,... | collective-permute-start | bytes 884744 | tf_op jit(solution)/shard_map/ppermute | solution.py:22
  84.7 2.8 %collective-permute-done.7 = bf16[4,32,1152]{2,1,0:T(8,128)(2,1)} collective-permute-done((bf16[4,32,1152]{2,1,0:T(8,128)(2,1)}, bf16[4,32,1152]{2,1,0:T(8,128)(2,1)}, u32[]{:S(2)}, u32[]{:S(2)}) %collective-permute-start.7) | collective-permute-done | bytes 294944 | tf_op jit(solution)/shard_map/ppermute | solution.py:22
  87.9 2.9 %collective-permute-done.8 = bf16[4,32,1152]{2,1,0:T(8,128)(2,1)} collective-permute-done((bf16[4,32,1152]{2,1,0:T(8,128)(2,1)S(1)}, bf16[4,32,1152]{2,1,0:T(8,128)(2,1)}, u32[]{:S(2)}, u32[]{:S(2)}) %collective-permute-start.8) | collective-permute-done | bytes 294944 | tf_op jit(solution)/shard_map/ppermute | solution.py:22
  90.8 1.7 add_bitcast_fusion.1
  92.5 1.7 collective-permute-done.12
  94.2 1.6 add_bitcast_fusion
  95.9 3.5 %collective-permute-start.16 = (bf16[2,32,1152]{2,1,0:T(8,128)(2,1)S(1)}, bf16[2,32,1152]{2,1,0:T(8,128)(2,1)S(1)}, u32[]{:S(2)}, u32[]{:S(2)}) collective-permute-start(bf16[2,32,1152]{2,1,0:T(8,128)(2,1)S(1)} %get-tuple-element.94), channel_id=1, source_target_pairs={{0,32},{32,64},{64,96},{1,33},{33,65},{65,97},{2,34},{34,66},{66,9... | collective-permute-start | bytes 442376 | tf_op jit(solution)/shard_map/ppermute | solution.py:28
  99.4 2.7 %collective-permute-start.18 = (bf16[2,32,1152]{2,1,0:T(8,128)(2,1)S(1)}, bf16[2,32,1152]{2,1,0:T(8,128)(2,1)S(1)}, u32[]{:S(2)}, u32[]{:S(2)}) collective-permute-start(bf16[2,32,1152]{2,1,0:T(8,128)(2,1)S(1)} %get-tuple-element.95), channel_id=1, source_target_pairs={{0,96},{1,97},{2,98},{3,99},{4,100},{5,101},{6,102},{7,103},{8,104... | collective-permute-start | bytes 442376 | tf_op jit(solution)/shard_map/ppermute | solution.py:28
  102.1 2.5 %collective-permute-start.17 = (bf16[2,32,1152]{2,1,0:T(8,128)(2,1)S(1)}, bf16[2,32,1152]{2,1,0:T(8,128)(2,1)S(1)}, u32[]{:S(2)}, u32[]{:S(2)}) collective-permute-start(bf16[2,32,1152]{2,1,0:T(8,128)(2,1)S(1)} %get-tuple-element.96), channel_id=1, source_target_pairs={{0,64},{32,96},{1,65},{33,97},{2,66},{34,98},{3,67},{35,99},{4,68}... | collective-permute-start | bytes 442376 | tf_op jit(solution)/shard_map/ppermute | solution.py:28
  104.6 2.1 %collective-permute-done.17 = bf16[2,32,1152]{2,1,0:T(8,128)(2,1)S(1)} collective-permute-done((bf16[2,32,1152]{2,1,0:T(8,128)(2,1)S(1)}, bf16[2,32,1152]{2,1,0:T(8,128)(2,1)S(1)}, u32[]{:S(2)}, u32[]{:S(2)}) %collective-permute-start.17) | collective-permute-done | bytes 147488 | tf_op jit(solution)/shard_map/ppermute | solution.py:28
  110.6 3.2 %collective-permute-done.21 = bf16[2,32,1152]{2,1,0:T(8,128)(2,1)S(1)} collective-permute-done((bf16[2,32,1152]{2,1,0:T(8,128)(2,1)S(1)}, bf16[2,32,1152]{2,1,0:T(8,128)(2,1)S(1)}, u32[]{:S(2)}, u32[]{:S(2)}) %collective-permute-start.21) | collective-permute-done | bytes 147488 | tf_op jit(solution)/shard_map/ppermute | solution.py:28
  113.8 1.6 collective-permute-done.20
  115.7 3.2 %collective-permute-start.23 = (bf16[4,32,1152]{2,1,0:T(8,128)(2,1)S(1)}, bf16[4,32,1152]{2,1,0:T(8,128)(2,1)S(1)}, u32[]{:S(2)}, u32[]{:S(2)}) collective-permute-start(bf16[4,32,1152]{2,1,0:T(8,128)(2,1)S(1)} %get-tuple-element.93), channel_id=1, source_target_pairs={{0,4},{2,6},{4,0},{6,2},{1,5},{3,7},{5,1},{7,3},{8,12},{10,14},{12... | collective-permute-start | bytes 884744 | tf_op jit(solution)/shard_map/ppermute | solution.py:22
  118.9 2.0 collective-permute-start.22
  120.9 3.6 %collective-permute-start.29 = (bf16[4,32,1152]{2,1,0:T(8,128)(2,1)S(1)}, bf16[4,32,1152]{2,1,0:T(8,128)(2,1)S(1)}, u32[]{:S(2)}, u32[]{:S(2)}) collective-permute-start(bf16[4,32,1152]{2,1,0:T(8,128)(2,1)S(1)} %get-tuple-element.92), channel_id=1, source_target_pairs={{0,16},{8,24},{16,0},{24,8},{1,17},{9,25},{17,1},{25,9},{2,18},{10... | collective-permute-start | bytes 884744 | tf_op jit(solution)/shard_map/ppermute | solution.py:22
  124.4 2.1 %collective-permute-start.28 = (bf16[4,32,1152]{2,1,0:T(8,128)(2,1)S(1)}, bf16[4,32,1152]{2,1,0:T(8,128)(2,1)S(1)}, u32[]{:S(2)}, u32[]{:S(2)}) collective-permute-start(bf16[4,32,1152]{2,1,0:T(8,128)(2,1)S(1)} %get-tuple-element.92), channel_id=1, source_target_pairs={{0,24},{8,0},{16,8},{24,16},{1,25},{9,1},{17,9},{25,17},{2,26},{10... | collective-permute-start | bytes 884744 | tf_op jit(solution)/shard_map/ppermute | solution.py:22
  126.6 1.5 collective-permute-start.27
  129.4 2.6 %collective-permute-done.29 = bf16[4,32,1152]{2,1,0:T(8,128)(2,1)S(1)} collective-permute-done((bf16[4,32,1152]{2,1,0:T(8,128)(2,1)S(1)}, bf16[4,32,1152]{2,1,0:T(8,128)(2,1)S(1)}, u32[]{:S(2)}, u32[]{:S(2)}) %collective-permute-start.29) | collective-permute-done | bytes 294944 | tf_op jit(solution)/shard_map/ppermute | solution.py:22
  132.2 2.7 %collective-permute-start.31 = (bf16[4,128,1152]{2,1,0:T(8,128)(2,1)S(1)}, bf16[4,128,1152]{2,1,0:T(8,128)(2,1)S(1)}, u32[]{:S(2)}, u32[]{:S(2)}) collective-permute-start(bf16[4,128,1152]{2,1,0:T(8,128)(2,1)S(1)} %pad_maximum_fusion.2.refs_3_), channel_id=1, source_target_pairs={{0,6},{2,0},{4,2},{6,4},{1,7},{3,1},{5,3},{7,5},{8,14},{10,8},{12,... | collective-permute-start | bytes 3538952 | tf_op jit(solution)/shard_map/ppermute | solution.py:22
  134.9 16.2 %collective-permute-start.25 = (bf16[512,1152]{0,1:T(8,128)(2,1)S(1)}, bf16[512,1152]{0,1:T(8,128)(2,1)S(1)}, u32[]{:S(2)}, u32[]{:S(2)}) collective-permute-start(bf16[512,1152]{0,1:T(8,128)(2,1)S(1)} %copy-done.15), channel_id=1, source_target_pairs={{0,1},{1,0},{2,3},{3,2},{4,5},{5,4},{6,7},{7,6},{8,9},{9,8},{10,11... | collective-permute-start | bytes 3538952 | tf_op jit(solution)/shard_map/ppermute | solution.py:32
  151.1 7.6 %collective-permute-done.27.refs_2_ = bf16[4,128,1152]{2,1,0:T(8,128)(2,1)S(1)} collective-permute-done((bf16[4,128,1152]{2,1,0:T(8,128)(2,1)S(1)}, bf16[4,128,1152]{2,1,0:T(8,128)(2,1)S(1)}, u32[]{:S(2)}, u32[]{:S(2)}) %collective-permute-start.27) | collective-permute-done | bytes 1179680 | tf_op jit(solution)/shard_map/ppermute | solution.py:22
  159.1 2.5 %collective-permute-start.33 = (bf16[4,64,1152]{2,1,0:T(8,128)(2,1)S(1)}, bf16[4,64,1152]{2,1,0:T(8,128)(2,1)S(1)}, u32[]{:S(2)}, u32[]{:S(2)}) collective-permute-start(bf16[4,64,1152]{2,1,0:T(8,128)(2,1)S(1)} %slice.162), channel_id=1, source_target_pairs={{0,24},{8,0},{16,8},{24,16},{1,25},{9,1},{17,9},{25,17},{2,26},{10... | collective-permute-start | bytes 1769480 | tf_op jit(solution)/shard_map/ppermute | solution.py:22
  161.8 2.7 %collective-permute-start.35 = (bf16[4,64,1152]{2,1,0:T(8,128)(2,1)S(1)}, bf16[4,64,1152]{2,1,0:T(8,128)(2,1)S(1)}, u32[]{:S(2)}, u32[]{:S(2)}) collective-permute-start(bf16[4,64,1152]{2,1,0:T(8,128)(2,1)S(1)} %slice.164), channel_id=1, source_target_pairs={{0,6},{2,0},{4,2},{6,4},{1,7},{3,1},{5,3},{7,5},{8,14},{10,8},{12,... | collective-permute-start | bytes 1769480 | tf_op jit(solution)/shard_map/ppermute | solution.py:22
  164.6 5.6 %shard_map.98.near_ref = f32[768,512]{1,0:T(8,128)S(1)} custom-call(s32[4]{0:T(128)S(1)} %copy-done.12, bf16[4,512,1152]{2,1,0:T(8,128)(2,1)S(1)} %bitcast.74, bf16[4,128,1152]{2,1,0:T(8,128)(2,1)S(1)} %pad_maximum_fusion.1.refs_0_, bf16[4,128,1152]{2,1,0:T(8,128)(2,1)S(1)} %collective-permute-done.26.refs_1_, ...), custom_call_target="tpu_custom_call" | custom-call | flops 3623878656 | bytes 14680064 | tf_op jit(solution)/shard_map/pallas_call | solution.py:54
  170.5 1.5 collective-permute-done.36.refs_9_.refs_3_
  172.2 3.0 %shard_map.99 = (f32[512,512]{1,0:T(8,128)S(1)}, f32[512,512]{1,0:T(8,128)S(1)}) custom-call(s32[4]{0:T(128)S(1)} %copy-done.12, bf16[4,512,1152]{2,1,0:T(8,128)(2,1)S(1)} %bitcast.74, f32[768,512]{1,0:T(8,128)S(1)} %shard_map.98.near_ref, bf16[4,64,1152]{2,1,0:T(8,128)(2,1)S(1)} %collective-permute-done.33.refs_6_.refs_0_, ...), custom_call_target="tpu_custom_call" | custom-call | flops 1207959552 | bytes 10485760 | tf_op jit(solution)/shard_map/pallas_call | solution.py:54
  175.3 7.6 %collective-permute-start.38 = (f32[512,512]{1,0:T(8,128)S(1)}, f32[512,512]{1,0:T(8,128)S(1)}, u32[]{:S(2)}, u32[]{:S(2)}) collective-permute-start(f32[512,512]{1,0:T(8,128)S(1)} %get-tuple-element.80), channel_id=1, source_target_pairs={{0,1},{1,0},{2,3},{3,2},{4,5},{5,4},{6,7},{7,6},{8,9},{9,8},{10,11... | collective-permute-start | bytes 3145736 | tf_op jit(solution)/shard_map/ppermute | solution.py:32
  182.9 9.1 %shard_map.97 = (f32[4,512,1152]{2,1,0:T(8,128)}, f32[1,1152]{1,0:T(1,128)S(1)}) custom-call(s32[4]{0:T(128)S(1)} %copy-done.12, bf16[512,512]{1,0:T(8,128)(2,1)S(1)} %copy-done.8, bf16[512,512]{1,0:T(8,128)(2,1)S(1)} %copy-done.10, bf16[4,128,1152]{2,1,0:T(8,128)(2,1)S(1)} %pad_maximum_fusion.1.refs_0_, ...), custom_call_target="tpu_custom_call" | custom-call | flops 4831838208 | bytes 20971520 | tf_op jit(solution)/shard_map/pallas_call | solution.py:54
  193.3 1.4 collective-permute-done.37
  196.6 4.3 %shard_map.100 = f32[1152,512]{1,0:T(8,128)} custom-call(s32[4]{0:T(128)S(1)} %copy-done.12, bf16[1152,512]{1,0:T(8,128)(2,1)S(1)} %bitcast.77, bf16[1152,512]{1,0:T(8,128)(2,1)S(1)} %bitcast.79, bf16[512,512]{1,0:T(8,128)(2,1)S(1)} %get-tuple-element.83.grad_ref, bf16[512,512]{1,0:T(8,128)(2,1)S(1)} %collective-permute-done.39.other_grad_ref), custom_call_target="tpu_custom_call" | custom-call | flops 1207959552 | bytes 6291456 | tf_op jit(solution)/shard_map/pallas_call | solution.py:54
  (122 shorter events, 28.3 us)
Async XLA Ops:
  0.7 12.2 %copy-start.11 = (s32[4]{0:T(128)}, s32[4]{0:T(128)S(1)}, u32[]{:S(2)}) copy-start(s32[4]{0:T(128)S(1)} %pad_add_fusion.where) | copy-start | bytes 52
  8.7 4.1 %collective-permute-start = (bf16[512,512]{1,0:T(8,128)(2,1)S(1)}, bf16[512,512]{1,0:T(8,128)(2,1)S(1)}, u32[]{:S(2)}, u32[]{:S(2)}) collective-permute-start(bf16[512,512]{1,0:T(8,128)(2,1)S(1)} %get-tuple-element.44), channel_id=1, source_target_pairs={{0,1},{1,0},{2,3},{3,2},{4,5},{5,4},{6,7},{7,6},{8,9},{9,8},{10,11... | collective-permute-start | bytes 1572872 | tf_op jit(solution)/shard_map/ppermute | solution.py:32
  17.1 21.5 %collective-permute-start.1 = (bf16[4,64,1152]{2,1,0:T(8,128)(2,1)}, bf16[4,64,1152]{2,1,0:T(8,128)(2,1)S(1)}, u32[]{:S(2)}, u32[]{:S(2)}) collective-permute-start(bf16[4,64,1152]{2,1,0:T(8,128)(2,1)} %get-tuple-element.51), channel_id=1, source_target_pairs={{0,8},{8,16},{16,24},{24,0},{1,9},{9,17},{17,25},{25,1},{2,10},{10... | collective-permute-start | bytes 1769480 | tf_op jit(solution)/shard_map/ppermute | solution.py:22
  18.5 20.2 %collective-permute-start.2 = (bf16[4,64,1152]{2,1,0:T(8,128)(2,1)}, bf16[4,64,1152]{2,1,0:T(8,128)(2,1)S(1)}, u32[]{:S(2)}, u32[]{:S(2)}) collective-permute-start(bf16[4,64,1152]{2,1,0:T(8,128)(2,1)} %get-tuple-element.52), channel_id=1, source_target_pairs={{0,24},{8,0},{16,8},{24,16},{1,25},{9,1},{17,9},{25,17},{2,26},{10... | collective-permute-start | bytes 1769480 | tf_op jit(solution)/shard_map/ppermute | solution.py:22
  19.9 18.8 %collective-permute-start.3 = (bf16[4,64,1152]{2,1,0:T(8,128)(2,1)}, bf16[4,64,1152]{2,1,0:T(8,128)(2,1)S(1)}, u32[]{:S(2)}, u32[]{:S(2)}) collective-permute-start(bf16[4,64,1152]{2,1,0:T(8,128)(2,1)} %get-tuple-element.53), channel_id=1, source_target_pairs={{0,2},{2,4},{4,6},{6,0},{1,3},{3,5},{5,7},{7,1},{8,10},{10,12},{12... | collective-permute-start | bytes 1769480 | tf_op jit(solution)/shard_map/ppermute | solution.py:22
  21.6 17.1 %collective-permute-start.4 = (bf16[4,64,1152]{2,1,0:T(8,128)(2,1)}, bf16[4,64,1152]{2,1,0:T(8,128)(2,1)S(1)}, u32[]{:S(2)}, u32[]{:S(2)}) collective-permute-start(bf16[4,64,1152]{2,1,0:T(8,128)(2,1)} %get-tuple-element.54), channel_id=1, source_target_pairs={{0,6},{2,0},{4,2},{6,4},{1,7},{3,1},{5,3},{7,5},{8,14},{10,8},{12,... | collective-permute-start | bytes 1769480 | tf_op jit(solution)/shard_map/ppermute | solution.py:22
  34.4 17.3 %all-to-all-start = ((f32[16,32,144]{2,1,0:T(8,128)}), f32[16,32,144]{2,1,0:T(8,128)}, u32[]{:S(2)}, u32[]{:S(2)}) async-start(f32[16,32,144]{2,1,0:T(8,128)} %convert_subtract_fusion), calls=%async_computation | async-start | bytes 1048576 | tf_op jit(solution)/shard_map/all_to_all | solution.py:375
  42.2 34.0 %collective-permute-start.5 = (bf16[4,128,1152]{2,1,0:T(8,128)(2,1)S(1)}, bf16[4,128,1152]{2,1,0:T(8,128)(2,1)}, u32[]{:S(2)}, u32[]{:S(2)}) collective-permute-start(bf16[4,128,1152]{2,1,0:T(8,128)(2,1)S(1)} %get-tuple-element.55), channel_id=1, source_target_pairs={{0,8},{8,16},{16,24},{24,0},{1,9},{9,17},{17,25},{25,1},{2,10},{10... | collective-permute-start | bytes 3538952 | tf_op jit(solution)/shard_map/ppermute | solution.py:22
  43.4 32.8 %collective-permute-start.6 = (bf16[4,128,1152]{2,1,0:T(8,128)(2,1)}, bf16[4,128,1152]{2,1,0:T(8,128)(2,1)}, u32[]{:S(2)}, u32[]{:S(2)}) collective-permute-start(bf16[4,128,1152]{2,1,0:T(8,128)(2,1)} %get-tuple-element.56), channel_id=1, source_target_pairs={{0,24},{8,0},{16,8},{24,16},{1,25},{9,1},{17,9},{25,17},{2,26},{10... | collective-permute-start | bytes 3538952 | tf_op jit(solution)/shard_map/ppermute | solution.py:22
  44.9 28.5 %collective-permute-start.10 = (bf16[4,128,1152]{2,1,0:T(8,128)(2,1)}, bf16[4,128,1152]{2,1,0:T(8,128)(2,1)}, u32[]{:S(2)}, u32[]{:S(2)}) collective-permute-start(bf16[4,128,1152]{2,1,0:T(8,128)(2,1)} %get-tuple-element.58), channel_id=1, source_target_pairs={{0,2},{2,4},{4,6},{6,0},{1,3},{3,5},{5,7},{7,1},{8,10},{10,12},{12... | collective-permute-start | bytes 3538952 | tf_op jit(solution)/shard_map/ppermute | solution.py:22
  46.1 27.3 %collective-permute-start.11 = (bf16[4,128,1152]{2,1,0:T(8,128)(2,1)}, bf16[4,128,1152]{2,1,0:T(8,128)(2,1)}, u32[]{:S(2)}, u32[]{:S(2)}) collective-permute-start(bf16[4,128,1152]{2,1,0:T(8,128)(2,1)} %get-tuple-element.59), channel_id=1, source_target_pairs={{0,6},{2,0},{4,2},{6,4},{1,7},{3,1},{5,3},{7,5},{8,14},{10,8},{12,... | collective-permute-start | bytes 3538952 | tf_op jit(solution)/shard_map/ppermute | solution.py:22
  53.8 28.5 %collective-permute-start.14 = (f32[32,1152]{1,0:T(8,128)}, f32[32,1152]{1,0:T(8,128)}, u32[]{:S(2)}, u32[]{:S(2)}) collective-permute-start(f32[32,1152]{1,0:T(8,128)} %reshape.39), channel_id=1, source_target_pairs={{0,1},{1,0},{2,3},{3,2},{4,5},{5,4},{6,7},{7,6},{8,9},{9,8},{10,11... | collective-permute-start | bytes 442376 | tf_op jit(solution)/shard_map/ppermute | solution.py:32
  75.8 8.1 %collective-permute-start.15 = (bf16[4,32,1152]{2,1,0:T(8,128)(2,1)S(1)}, bf16[4,32,1152]{2,1,0:T(8,128)(2,1)}, u32[]{:S(2)}, u32[]{:S(2)}) collective-permute-start(bf16[4,32,1152]{2,1,0:T(8,128)(2,1)S(1)} %get-tuple-element.85), channel_id=1, source_target_pairs={{0,24},{8,0},{16,8},{24,16},{1,25},{9,1},{17,9},{25,17},{2,26},{10... | collective-permute-start | bytes 884744 | tf_op jit(solution)/shard_map/ppermute | solution.py:22
  78.7 8.7 %collective-permute-start.7 = (bf16[4,32,1152]{2,1,0:T(8,128)(2,1)}, bf16[4,32,1152]{2,1,0:T(8,128)(2,1)}, u32[]{:S(2)}, u32[]{:S(2)}) collective-permute-start(bf16[4,32,1152]{2,1,0:T(8,128)(2,1)} %get-tuple-element.87), channel_id=1, source_target_pairs={{0,2},{2,4},{4,6},{6,0},{1,3},{3,5},{5,7},{7,1},{8,10},{10,12},{12... | collective-permute-start | bytes 884744 | tf_op jit(solution)/shard_map/ppermute | solution.py:22
  79.3 8.6 %collective-permute-start.9 = (bf16[4,32,1152]{2,1,0:T(8,128)(2,1)S(1)}, bf16[4,32,1152]{2,1,0:T(8,128)(2,1)}, u32[]{:S(2)}, u32[]{:S(2)}) collective-permute-start(bf16[4,32,1152]{2,1,0:T(8,128)(2,1)S(1)} %get-tuple-element.88), channel_id=1, source_target_pairs={{0,6},{2,0},{4,2},{6,4},{1,7},{3,1},{5,3},{7,5},{8,14},{10,8},{12,... | collective-permute-start | bytes 884744 | tf_op jit(solution)/shard_map/ppermute | solution.py:22
  81.4 9.4 %collective-permute-start.8 = (bf16[4,32,1152]{2,1,0:T(8,128)(2,1)S(1)}, bf16[4,32,1152]{2,1,0:T(8,128)(2,1)}, u32[]{:S(2)}, u32[]{:S(2)}) collective-permute-start(bf16[4,32,1152]{2,1,0:T(8,128)(2,1)S(1)} %get-tuple-element.89), channel_id=1, source_target_pairs={{0,4},{2,6},{4,0},{6,2},{1,5},{3,7},{5,1},{7,3},{8,12},{10,14},{12... | collective-permute-start | bytes 884744 | tf_op jit(solution)/shard_map/ppermute | solution.py:22
  83.2 11.0 %collective-permute-start.12 = (bf16[4,32,1152]{2,1,0:T(8,128)(2,1)S(1)}, bf16[4,32,1152]{2,1,0:T(8,128)(2,1)S(1)}, u32[]{:S(2)}, u32[]{:S(2)}) collective-permute-start(bf16[4,32,1152]{2,1,0:T(8,128)(2,1)S(1)} %get-tuple-element.84), channel_id=1, source_target_pairs={{0,8},{8,16},{16,24},{24,0},{1,9},{9,17},{17,25},{25,1},{2,10},{10... | collective-permute-start | bytes 884744 | tf_op jit(solution)/shard_map/ppermute | solution.py:22
  83.9 10.3 %collective-permute-start.13 = (bf16[4,32,1152]{2,1,0:T(8,128)(2,1)S(1)}, bf16[4,32,1152]{2,1,0:T(8,128)(2,1)S(1)}, u32[]{:S(2)}, u32[]{:S(2)}) collective-permute-start(bf16[4,32,1152]{2,1,0:T(8,128)(2,1)S(1)} %get-tuple-element.86), channel_id=1, source_target_pairs={{0,16},{8,24},{16,0},{24,8},{1,17},{9,25},{17,1},{25,9},{2,18},{10... | collective-permute-start | bytes 884744 | tf_op jit(solution)/shard_map/ppermute | solution.py:22
  95.8 68.7 %slice-start = ((s8[4718592]{0:T(1024)(128)(4,1)}), s8[4194304]{0:T(1024)(128)(4,1)S(1)}, s32[]{:S(2)}) async-start(s8[4718592]{0:T(1024)(128)(4,1)} %bitcast.73), calls=%async_computation.1 | async-start | bytes 8388608
  95.9 8.7 %collective-permute-start.16 = (bf16[2,32,1152]{2,1,0:T(8,128)(2,1)S(1)}, bf16[2,32,1152]{2,1,0:T(8,128)(2,1)S(1)}, u32[]{:S(2)}, u32[]{:S(2)}) collective-permute-start(bf16[2,32,1152]{2,1,0:T(8,128)(2,1)S(1)} %get-tuple-element.94), channel_id=1, source_target_pairs={{0,32},{32,64},{64,96},{1,33},{33,65},{65,97},{2,34},{34,66},{66,9... | collective-permute-start | bytes 442376 | tf_op jit(solution)/shard_map/ppermute | solution.py:28
  99.4 5.2 %collective-permute-start.18 = (bf16[2,32,1152]{2,1,0:T(8,128)(2,1)S(1)}, bf16[2,32,1152]{2,1,0:T(8,128)(2,1)S(1)}, u32[]{:S(2)}, u32[]{:S(2)}) collective-permute-start(bf16[2,32,1152]{2,1,0:T(8,128)(2,1)S(1)} %get-tuple-element.95), channel_id=1, source_target_pairs={{0,96},{1,97},{2,98},{3,99},{4,100},{5,101},{6,102},{7,103},{8,104... | collective-permute-start | bytes 442376 | tf_op jit(solution)/shard_map/ppermute | solution.py:28
  102.1 4.6 %collective-permute-start.17 = (bf16[2,32,1152]{2,1,0:T(8,128)(2,1)S(1)}, bf16[2,32,1152]{2,1,0:T(8,128)(2,1)S(1)}, u32[]{:S(2)}, u32[]{:S(2)}) collective-permute-start(bf16[2,32,1152]{2,1,0:T(8,128)(2,1)S(1)} %get-tuple-element.96), channel_id=1, source_target_pairs={{0,64},{32,96},{1,65},{33,97},{2,66},{34,98},{3,67},{35,99},{4,68}... | collective-permute-start | bytes 442376 | tf_op jit(solution)/shard_map/ppermute | solution.py:28
  106.7 7.1 %collective-permute-start.21 = (bf16[2,32,1152]{2,1,0:T(8,128)(2,1)S(1)}, bf16[2,32,1152]{2,1,0:T(8,128)(2,1)S(1)}, u32[]{:S(2)}, u32[]{:S(2)}) collective-permute-start(bf16[2,32,1152]{2,1,0:T(8,128)(2,1)S(1)} %fusion.17), channel_id=1, source_target_pairs={{96,0},{97,1},{98,2},{99,3},{100,4},{101,5},{102,6},{103,7},{104,8... | collective-permute-start | bytes 442376 | tf_op jit(solution)/shard_map/ppermute | solution.py:28
  108.0 7.4 %collective-permute-start.20 = (bf16[2,32,1152]{2,1,0:T(8,128)(2,1)S(1)}, bf16[2,32,1152]{2,1,0:T(8,128)(2,1)S(1)}, u32[]{:S(2)}, u32[]{:S(2)}) collective-permute-start(bf16[2,32,1152]{2,1,0:T(8,128)(2,1)S(1)} %fusion.17), channel_id=1, source_target_pairs={{64,0},{96,32},{65,1},{97,33},{66,2},{98,34},{67,3},{99,35},{68,4}... | collective-permute-start | bytes 442376 | tf_op jit(solution)/shard_map/ppermute | solution.py:28
  109.3 6.1 %collective-permute-start.19 = (bf16[2,32,1152]{2,1,0:T(8,128)(2,1)S(1)}, bf16[2,32,1152]{2,1,0:T(8,128)(2,1)S(1)}, u32[]{:S(2)}, u32[]{:S(2)}) collective-permute-start(bf16[2,32,1152]{2,1,0:T(8,128)(2,1)S(1)} %fusion.17), channel_id=1, source_target_pairs={{32,0},{64,32},{96,64},{33,1},{65,33},{97,65},{34,2},{66,34},{98,6... | collective-permute-start | bytes 442376 | tf_op jit(solution)/shard_map/ppermute | solution.py:28
  115.6 8.9 %collective-permute-start.24 = (bf16[4,32,1152]{2,1,0:T(8,128)(2,1)S(1)}, bf16[4,32,1152]{2,1,0:T(8,128)(2,1)S(1)}, u32[]{:S(2)}, u32[]{:S(2)}) collective-permute-start(bf16[4,32,1152]{2,1,0:T(8,128)(2,1)S(1)} %get-tuple-element.93), channel_id=1, source_target_pairs={{0,2},{2,4},{4,6},{6,0},{1,3},{3,5},{5,7},{7,1},{8,10},{10,12},{12... | collective-permute-start | bytes 884744 | tf_op jit(solution)/shard_map/ppermute | solution.py:22
  115.7 10.9 %collective-permute-start.23 = (bf16[4,32,1152]{2,1,0:T(8,128)(2,1)S(1)}, bf16[4,32,1152]{2,1,0:T(8,128)(2,1)S(1)}, u32[]{:S(2)}, u32[]{:S(2)}) collective-permute-start(bf16[4,32,1152]{2,1,0:T(8,128)(2,1)S(1)} %get-tuple-element.93), channel_id=1, source_target_pairs={{0,4},{2,6},{4,0},{6,2},{1,5},{3,7},{5,1},{7,3},{8,12},{10,14},{12... | collective-permute-start | bytes 884744 | tf_op jit(solution)/shard_map/ppermute | solution.py:22
  118.9 7.6 %collective-permute-start.22 = (bf16[4,32,1152]{2,1,0:T(8,128)(2,1)S(1)}, bf16[4,32,1152]{2,1,0:T(8,128)(2,1)S(1)}, u32[]{:S(2)}, u32[]{:S(2)}) collective-permute-start(bf16[4,32,1152]{2,1,0:T(8,128)(2,1)S(1)} %get-tuple-element.93), channel_id=1, source_target_pairs={{0,6},{2,0},{4,2},{6,4},{1,7},{3,1},{5,3},{7,5},{8,14},{10,8},{12,... | collective-permute-start | bytes 884744 | tf_op jit(solution)/shard_map/ppermute | solution.py:22
  120.9 43.7 %slice-start.1 = ((s8[4718592]{0:T(1024)(128)(4,1)}), s8[524288]{0:T(1024)(128)(4,1)S(1)}, s32[]{:S(2)}) async-start(s8[4718592]{0:T(1024)(128)(4,1)} %bitcast.73), calls=%async_computation.2 | async-start | bytes 1048576
  120.9 8.5 %collective-permute-start.30 = (bf16[4,32,1152]{2,1,0:T(8,128)(2,1)S(1)}, bf16[4,32,1152]{2,1,0:T(8,128)(2,1)S(1)}, u32[]{:S(2)}, u32[]{:S(2)}) collective-permute-start(bf16[4,32,1152]{2,1,0:T(8,128)(2,1)S(1)} %get-tuple-element.92), channel_id=1, source_target_pairs={{0,8},{8,16},{16,24},{24,0},{1,9},{9,17},{17,25},{25,1},{2,10},{10... | collective-permute-start | bytes 884744 | tf_op jit(solution)/shard_map/ppermute | solution.py:22
  120.9 11.1 %collective-permute-start.29 = (bf16[4,32,1152]{2,1,0:T(8,128)(2,1)S(1)}, bf16[4,32,1152]{2,1,0:T(8,128)(2,1)S(1)}, u32[]{:S(2)}, u32[]{:S(2)}) collective-permute-start(bf16[4,32,1152]{2,1,0:T(8,128)(2,1)S(1)} %get-tuple-element.92), channel_id=1, source_target_pairs={{0,16},{8,24},{16,0},{24,8},{1,17},{9,25},{17,1},{25,9},{2,18},{10... | collective-permute-start | bytes 884744 | tf_op jit(solution)/shard_map/ppermute | solution.py:22
  124.4 7.6 %collective-permute-start.28 = (bf16[4,32,1152]{2,1,0:T(8,128)(2,1)S(1)}, bf16[4,32,1152]{2,1,0:T(8,128)(2,1)S(1)}, u32[]{:S(2)}, u32[]{:S(2)}) collective-permute-start(bf16[4,32,1152]{2,1,0:T(8,128)(2,1)S(1)} %get-tuple-element.92), channel_id=1, source_target_pairs={{0,24},{8,0},{16,8},{24,16},{1,25},{9,1},{17,9},{25,17},{2,26},{10... | collective-permute-start | bytes 884744 | tf_op jit(solution)/shard_map/ppermute | solution.py:22
  126.6 32.1 %collective-permute-start.27 = (bf16[4,128,1152]{2,1,0:T(8,128)(2,1)S(1)}, bf16[4,128,1152]{2,1,0:T(8,128)(2,1)S(1)}, u32[]{:S(2)}, u32[]{:S(2)}) collective-permute-start(bf16[4,128,1152]{2,1,0:T(8,128)(2,1)S(1)} %pad_maximum_fusion.1.refs_0_), channel_id=1, source_target_pairs={{0,8},{8,16},{16,24},{24,0},{1,9},{9,17},{17,25},{25,1},{2,10},{10... | collective-permute-start | bytes 3538952 | tf_op jit(solution)/shard_map/ppermute | solution.py:22
  128.1 30.9 %collective-permute-start.26 = (bf16[4,128,1152]{2,1,0:T(8,128)(2,1)S(1)}, bf16[4,128,1152]{2,1,0:T(8,128)(2,1)S(1)}, u32[]{:S(2)}, u32[]{:S(2)}) collective-permute-start(bf16[4,128,1152]{2,1,0:T(8,128)(2,1)S(1)} %pad_maximum_fusion.1.refs_0_), channel_id=1, source_target_pairs={{0,24},{8,0},{16,8},{24,16},{1,25},{9,1},{17,9},{25,17},{2,26},{10... | collective-permute-start | bytes 3538952 | tf_op jit(solution)/shard_map/ppermute | solution.py:22
  132.1 29.5 %collective-permute-start.32 = (bf16[4,128,1152]{2,1,0:T(8,128)(2,1)S(1)}, bf16[4,128,1152]{2,1,0:T(8,128)(2,1)S(1)}, u32[]{:S(2)}, u32[]{:S(2)}) collective-permute-start(bf16[4,128,1152]{2,1,0:T(8,128)(2,1)S(1)} %pad_maximum_fusion.2.refs_3_), channel_id=1, source_target_pairs={{0,2},{2,4},{4,6},{6,0},{1,3},{3,5},{5,7},{7,1},{8,10},{10,12},{12... | collective-permute-start | bytes 3538952 | tf_op jit(solution)/shard_map/ppermute | solution.py:22
  132.2 29.6 %collective-permute-start.31 = (bf16[4,128,1152]{2,1,0:T(8,128)(2,1)S(1)}, bf16[4,128,1152]{2,1,0:T(8,128)(2,1)S(1)}, u32[]{:S(2)}, u32[]{:S(2)}) collective-permute-start(bf16[4,128,1152]{2,1,0:T(8,128)(2,1)S(1)} %pad_maximum_fusion.2.refs_3_), channel_id=1, source_target_pairs={{0,6},{2,0},{4,2},{6,4},{1,7},{3,1},{5,3},{7,5},{8,14},{10,8},{12,... | collective-permute-start | bytes 3538952 | tf_op jit(solution)/shard_map/ppermute | solution.py:22
  134.9 29.7 %collective-permute-start.25 = (bf16[512,1152]{0,1:T(8,128)(2,1)S(1)}, bf16[512,1152]{0,1:T(8,128)(2,1)S(1)}, u32[]{:S(2)}, u32[]{:S(2)}) collective-permute-start(bf16[512,1152]{0,1:T(8,128)(2,1)S(1)} %copy-done.15), channel_id=1, source_target_pairs={{0,1},{1,0},{2,3},{3,2},{4,5},{5,4},{6,7},{7,6},{8,9},{9,8},{10,11... | collective-permute-start | bytes 3538952 | tf_op jit(solution)/shard_map/ppermute | solution.py:32
  158.7 11.7 %collective-permute-start.34 = (bf16[4,64,1152]{2,1,0:T(8,128)(2,1)S(1)}, bf16[4,64,1152]{2,1,0:T(8,128)(2,1)S(1)}, u32[]{:S(2)}, u32[]{:S(2)}) collective-permute-start(bf16[4,64,1152]{2,1,0:T(8,128)(2,1)S(1)} %slice.163), channel_id=1, source_target_pairs={{0,8},{8,16},{16,24},{24,0},{1,9},{9,17},{17,25},{25,1},{2,10},{10... | collective-permute-start | bytes 1769480 | tf_op jit(solution)/shard_map/ppermute | solution.py:22
  159.1 11.3 %collective-permute-start.33 = (bf16[4,64,1152]{2,1,0:T(8,128)(2,1)S(1)}, bf16[4,64,1152]{2,1,0:T(8,128)(2,1)S(1)}, u32[]{:S(2)}, u32[]{:S(2)}) collective-permute-start(bf16[4,64,1152]{2,1,0:T(8,128)(2,1)S(1)} %slice.162), channel_id=1, source_target_pairs={{0,24},{8,0},{16,8},{24,16},{1,25},{9,1},{17,9},{25,17},{2,26},{10... | collective-permute-start | bytes 1769480 | tf_op jit(solution)/shard_map/ppermute | solution.py:22
  161.7 10.3 %collective-permute-start.36 = (bf16[4,64,1152]{2,1,0:T(8,128)(2,1)S(1)}, bf16[4,64,1152]{2,1,0:T(8,128)(2,1)S(1)}, u32[]{:S(2)}, u32[]{:S(2)}) collective-permute-start(bf16[4,64,1152]{2,1,0:T(8,128)(2,1)S(1)} %slice.165), channel_id=1, source_target_pairs={{0,2},{2,4},{4,6},{6,0},{1,3},{3,5},{5,7},{7,1},{8,10},{10,12},{12... | collective-permute-start | bytes 1769480 | tf_op jit(solution)/shard_map/ppermute | solution.py:22
  161.8 10.4 %collective-permute-start.35 = (bf16[4,64,1152]{2,1,0:T(8,128)(2,1)S(1)}, bf16[4,64,1152]{2,1,0:T(8,128)(2,1)S(1)}, u32[]{:S(2)}, u32[]{:S(2)}) collective-permute-start(bf16[4,64,1152]{2,1,0:T(8,128)(2,1)S(1)} %slice.164), channel_id=1, source_target_pairs={{0,6},{2,0},{4,2},{6,4},{1,7},{3,1},{5,3},{7,5},{8,14},{10,8},{12,... | collective-permute-start | bytes 1769480 | tf_op jit(solution)/shard_map/ppermute | solution.py:22
  170.2 12.6 %copy-start.8 = (bf16[512,512]{1,0:T(8,128)(2,1)S(1)}, bf16[512,512]{1,0:T(8,128)(2,1)}, u32[]{:S(2)}) copy-start(bf16[512,512]{1,0:T(8,128)(2,1)} %copy-done.7) | copy-start | bytes 1572868
  170.2 12.6 %copy-start.10 = (bf16[512,512]{1,0:T(8,128)(2,1)S(1)}, bf16[512,512]{1,0:T(8,128)(2,1)}, u32[]{:S(2)}) copy-start(bf16[512,512]{1,0:T(8,128)(2,1)} %copy-done.9) | copy-start | bytes 1572868
  175.3 16.7 %copy-start.6 = (f32[512,512]{1,0:T(8,128)S(1)}, f32[512,512]{1,0:T(8,128)}, u32[]{:S(2)}) copy-start(f32[512,512]{1,0:T(8,128)} %copy-done.5) | copy-start | bytes 3145732
  175.3 16.7 %collective-permute-start.38 = (f32[512,512]{1,0:T(8,128)S(1)}, f32[512,512]{1,0:T(8,128)S(1)}, u32[]{:S(2)}, u32[]{:S(2)}) collective-permute-start(f32[512,512]{1,0:T(8,128)S(1)} %get-tuple-element.80), channel_id=1, source_target_pairs={{0,1},{1,0},{2,3},{3,2},{4,5},{5,4},{6,7},{7,6},{8,9},{9,8},{10,11... | collective-permute-start | bytes 3145736 | tf_op jit(solution)/shard_map/ppermute | solution.py:32
  192.8 3.9 %collective-permute-start.39 = (bf16[512,512]{1,0:T(8,128)(2,1)S(1)}, bf16[512,512]{1,0:T(8,128)(2,1)S(1)}, u32[]{:S(2)}, u32[]{:S(2)}) collective-permute-start(bf16[512,512]{1,0:T(8,128)(2,1)S(1)} %get-tuple-element.83.grad_ref), channel_id=1, source_target_pairs={{0,1},{1,0},{2,3},{3,2},{4,5},{5,4},{6,7},{7,6},{8,9},{9,8},{10,11... | collective-permute-start | bytes 1572872 | tf_op jit(solution)/shard_map/ppermute | solution.py:32
  192.9 1.9 collective-permute-start.37
  194.8 1.2 collective-permute-start.40
  (15 other events, 76.9 us)

commit v5 on v4

--- a/solution.py
+++ b/solution.py
@@ -116,6 +116,7 @@
         [pltpu.VMEM((rows, feats), F32)],
         2 * rows * model * feats,
         8 * 2**20,
+        mib=LARGE_MIB,
     )
 
 

time: 202 us -> 201 us (level)
  local copies, waits for them, and re-layouts: 14.3 us -> 9.34 us
  Pallas kernels: 41.7 us -> 45 us
  waiting for transfers between devices: 45.9 us -> 48.4 us
  starting transfers between devices: 84.4 us -> 82.3 us
    unnamed x45 -> x37, local copies, waits for them, and re-layouts: 6.57 us -> 1.54 us
    pallas_call x8, Pallas kernels: 41.7 us -> 45 us  [call(): pl.pallas_call(kernel, out_shape=[jax.ShapeDtypeStruct(shape, dtype) for...]
    ppermute x28, waiting for transfers between devices: 37.2 us -> 39.4 us  [shift(): return lax.ppermute(value, axis, [(i, (i + step) % n) for i in range(n)])]
  transfers between devices with their start and end apart: 42 -> 42, of which waited for: 15 -> 17; matrix products, arithmetic and copies ran while one was open for 10% -> 10% of each run, Pallas kernels for 14% -> 14%
where the time goes in v5:
time: 201 us; the launch traced here: 200 us
  starting transfers between devices  82.3 us (41%)
  waiting for transfers between devices  48.4 us (24%)
  Pallas kernels  45 us (22%)
  other arithmetic  14 us (7%)
  local copies, waits for them, and re-layouts  9.34 us (5%)
    pallas_call x8, Pallas kernels, call(): pl.pallas_call(kernel, out_shape=[jax.ShapeDtypeStruct(shape, dtype) for...  45 us
    ppermute x28, waiting for transfers between devices, shift(): return lax.ppermute(value, axis, [(i, (i + step) % n) for i in range(n)])  39.4 us
    ppermute x28, starting transfers between devices, shift(): return lax.ppermute(value, axis, [(i, (i + step) % n) for i in range(n)])  38.7 us
    ppermute x7, starting transfers between devices, swap(): return lax.ppermute(value, TOK, [(0, 1), (1, 0)])  26.7 us
    ppermute x6, starting transfers between devices, send_up(): return lax.ppermute(value, LAYER, pairs)  12.6 us
    ppermute x6, waiting for transfers between devices, send_up(): return lax.ppermute(value, LAYER, pairs)  7.16 us
    convert_element_type x2, other arithmetic, settled(): return [sums[0]] + [v.astype(BF16) for v in sums[1:]]  4.79 us
    all_to_all x1, starting transfers between devices, on_device(): base = lax.all_to_all(base, (LX, LZ), 0, 0, tiled=True)  4.25 us
  transfers between devices with their start and end apart: 42, of which 17 were waited for; matrix products, arithmetic and copies ran while one was open for 10% of the time, Pallas kernels for 14%

profile of v5, /device:TPU:1, one launch (start us, length us, event | category | flops | bytes accessed | tf_op | source)
XLA Modules:
  0.0 200.2 jit_solution(7978818776306195102)
XLA Ops:
  1.2 6.4 %shard_map.93 = (f32[512,512]{1,0:T(8,128)}, bf16[512,512]{1,0:T(8,128)(2,1)}, bf16[512,512]{1,0:T(8,128)(2,1)}) custom-call(s32[4]{0:T(128)} %pad_add_fusion.where, bf16[512,2304]{1,0:T(8,128)(2,1)} %bitcast.78, bf16[2304,512]{1,0:T(8,128)(2,1)} %bitcast.80, f32[1,512]{1,0:T(1,128)} %bias_ref.1), custom_call_target="tpu_custom_call" | custom-call | flops 1207959552 | bytes 8388608 | tf_op jit(solution)/shard_map/pallas_call | solution.py:54
  7.6 1.4 collective-permute-start
  9.1 2.8 %dynamic-slice_bitcast_fusion.w_ref = bf16[4,512,1152]{2,1,0:T(8,128)(2,1)S(1)} fusion(bf16[1,4,512,2304]{3,2,1,0:T(8,128)(2,1)} %param.10, s32[]{:T(128)S(6)} %select_n.26), kind=kLoop, calls=%fused_computation.4 | loop fusion | bytes 9437188 | tf_op jit(solution)/shard_map/dynamic_slice | solution.py:359
  11.9 4.1 %shard_map.95 = (bf16[4,64,1152]{2,1,0:T(8,128)(2,1)}, bf16[4,64,1152]{2,1,0:T(8,128)(2,1)}, bf16[4,64,1152]{2,1,0:T(8,128)(2,1)}, bf16[4,64,1152]{2,1,0:T(8,128)(2,1)}) custom-call(s32[4]{0:T(128)S(1)} %copy-done.6, bf16[512,512]{1,0:T(8,128)(2,1)S(1)} %copy-done.2, bf16[512,512]{1,0:T(8,128)(2,1)S(1)} %collective-permute-done.other_ref, ...), custom_call_target="tpu_custom_call" | custom-call | flops 1207959552 | bytes 8388608 | tf_op jit(solution)/shard_map/pallas_call | solution.py:54
  17.4 1.4 collective-permute-start.2
  18.7 1.7 collective-permute-start.3
  20.5 2.1 %collective-permute-start.4 = (bf16[4,64,1152]{2,1,0:T(8,128)(2,1)}, bf16[4,64,1152]{2,1,0:T(8,128)(2,1)S(1)}, u32[]{:S(2)}, u32[]{:S(2)}) collective-permute-start(bf16[4,64,1152]{2,1,0:T(8,128)(2,1)} %get-tuple-element.54), channel_id=1, source_target_pairs={{0,6},{2,0},{4,2},{6,4},{1,7},{3,1},{5,3},{7,5},{8,14},{10,8},{12,... | collective-permute-start | bytes 1769480 | tf_op jit(solution)/shard_map/ppermute | solution.py:22
  23.4 9.0 %shard_map.94 = (f32[4,128,1152]{2,1,0:T(8,128)}, bf16[4,128,1152]{2,1,0:T(8,128)(2,1)}, bf16[4,128,1152]{2,1,0:T(8,128)(2,1)}, f32[4,128,1152]{2,1,0:T(8,128)},...) custom-call(s32[4]{0:T(128)} %pad_add_fusion.where, bf16[512,512]{1,0:T(8,128)(2,1)} %get-tuple-element.43.own_ref, ...), custom_call_target="tpu_custom_call" | custom-call | flops 3623878656 | bytes 8388608 | tf_op jit(solution)/shard_map/pallas_call | solution.py:54
  33.3 4.2 %all-to-all-start = ((f32[16,32,144]{2,1,0:T(8,128)}), f32[16,32,144]{2,1,0:T(8,128)}, u32[]{:S(2)}, u32[]{:S(2)}) async-start(f32[16,32,144]{2,1,0:T(8,128)} %convert_subtract_fusion), calls=%async_computation | async-start | bytes 1048576 | tf_op jit(solution)/shard_map/all_to_all | solution.py:376
  37.7 3.5 %shard_map.96 = (bf16[4,128,1152]{2,1,0:T(8,128)(2,1)S(1)}, bf16[4,128,1152]{2,1,0:T(8,128)(2,1)}, bf16[4,128,1152]{2,1,0:T(8,128)(2,1)}, bf16[4,128,1152]{2,1,0:T(8,128)(2,1)}) custom-call(s32[4]{0:T(128)S(1)} %copy-done.7, bf16[4,128,1152]{2,1,0:T(8,128)(2,1)S(1)} %copy-done.1, ...), custom_call_target="tpu_custom_call", output_to_operand_aliasing={{0}: (1, {}), {1}: (2, {}), {2}: (3, {}), {3}: (4, {})} | custom-call | flops 2359296 | bytes 7077888 | tf_op jit(solution)/shard_map/pallas_call | solution.py:54
  42.4 1.4 collective-permute-start.6
  45.1 1.4 collective-permute-start.11
  48.5 1.5 copy.30
  52.7 2.3 %collective-permute-start.14 = (f32[32,1152]{1,0:T(8,128)}, f32[32,1152]{1,0:T(8,128)}, u32[]{:S(2)}, u32[]{:S(2)}) collective-permute-start(f32[32,1152]{1,0:T(8,128)} %reshape.39), channel_id=1, source_target_pairs={{0,1},{1,0},{2,3},{3,2},{4,5},{5,4},{6,7},{7,6},{8,9},{9,8},{10,11... | collective-permute-start | bytes 442376 | tf_op jit(solution)/shard_map/ppermute | solution.py:32
  55.0 17.4 %collective-permute-done.10 = bf16[4,128,1152]{2,1,0:T(8,128)(2,1)} collective-permute-done((bf16[4,128,1152]{2,1,0:T(8,128)(2,1)}, bf16[4,128,1152]{2,1,0:T(8,128)(2,1)}, u32[]{:S(2)}, u32[]{:S(2)}) %collective-permute-start.10) | collective-permute-done | bytes 1179680 | tf_op jit(solution)/shard_map/ppermute | solution.py:22
  72.4 2.4 %add_convert_fusion.2 = (bf16[4,32,1152]{2,1,0:T(8,128)(2,1)S(1)}, bf16[4,32,1152]{2,1,0:T(8,128)(2,1)S(1)}, bf16[4,32,1152]{2,1,0:T(8,128)(2,1)S(1)}) fusion(f32[4,128,1152]{2,1,0:T(8,128)} %get-tuple-element.57, bf16[4,128,1152]{2,1,0:T(8,128)(2,1)} %collective-permute-done.11, bf16[4,128,1152]{2,1,0:T(8,128)(2,1)} %collective-permute-done.10), kind=kLoop, calls=%fused_computation.27 | loop fusion | flops 2211840 | bytes 4423680 | tf_op jit(solution)/shard_map/convert_element_type | solution.py:397
  75.3 2.4 %add_convert_fusion.5 = (bf16[4,32,1152]{2,1,0:T(8,128)(2,1)}, bf16[4,32,1152]{2,1,0:T(8,128)(2,1)S(1)}, bf16[4,32,1152]{2,1,0:T(8,128)(2,1)S(1)}) fusion(f32[4,128,1152]{2,1,0:T(8,128)S(1)} %copy-done.9, bf16[4,128,1152]{2,1,0:T(8,128)(2,1)} %collective-permute-done.6, bf16[4,128,1152]{2,1,0:T(8,128)(2,1)} %collective-permute-done.5), kind=kLoop, calls=%fused_computation.31 | loop fusion | flops 2211840 | bytes 4423680 | tf_op jit(solution)/shard_map/convert_element_type | solution.py:397
  78.3 2.1 %collective-permute-start.9 = (bf16[4,32,1152]{2,1,0:T(8,128)(2,1)S(1)}, bf16[4,32,1152]{2,1,0:T(8,128)(2,1)}, u32[]{:S(2)}, u32[]{:S(2)}) collective-permute-start(bf16[4,32,1152]{2,1,0:T(8,128)(2,1)S(1)} %get-tuple-element.88), channel_id=1, source_target_pairs={{0,6},{2,0},{4,2},{6,4},{1,7},{3,1},{5,3},{7,5},{8,14},{10,8},{12,... | collective-permute-start | bytes 884744 | tf_op jit(solution)/shard_map/ppermute | solution.py:22
  83.7 2.3 %collective-permute-done.7 = bf16[4,32,1152]{2,1,0:T(8,128)(2,1)} collective-permute-done((bf16[4,32,1152]{2,1,0:T(8,128)(2,1)}, bf16[4,32,1152]{2,1,0:T(8,128)(2,1)}, u32[]{:S(2)}, u32[]{:S(2)}) %collective-permute-start.7) | collective-permute-done | bytes 294944 | tf_op jit(solution)/shard_map/ppermute | solution.py:22
  86.8 3.2 %collective-permute-done.8 = bf16[4,32,1152]{2,1,0:T(8,128)(2,1)} collective-permute-done((bf16[4,32,1152]{2,1,0:T(8,128)(2,1)S(1)}, bf16[4,32,1152]{2,1,0:T(8,128)(2,1)}, u32[]{:S(2)}, u32[]{:S(2)}) %collective-permute-start.8) | collective-permute-done | bytes 294944 | tf_op jit(solution)/shard_map/ppermute | solution.py:22
  90.0 1.7 add_bitcast_fusion.1
  91.7 1.5 collective-permute-done.12
  93.2 1.6 add_bitcast_fusion
  94.9 3.5 %collective-permute-start.16 = (bf16[2,32,1152]{2,1,0:T(8,128)(2,1)S(1)}, bf16[2,32,1152]{2,1,0:T(8,128)(2,1)S(1)}, u32[]{:S(2)}, u32[]{:S(2)}) collective-permute-start(bf16[2,32,1152]{2,1,0:T(8,128)(2,1)S(1)} %get-tuple-element.94), channel_id=1, source_target_pairs={{0,32},{32,64},{64,96},{1,33},{33,65},{65,97},{2,34},{34,66},{66,9... | collective-permute-start | bytes 442376 | tf_op jit(solution)/shard_map/ppermute | solution.py:28
  98.4 2.8 %collective-permute-start.18 = (bf16[2,32,1152]{2,1,0:T(8,128)(2,1)S(1)}, bf16[2,32,1152]{2,1,0:T(8,128)(2,1)S(1)}, u32[]{:S(2)}, u32[]{:S(2)}) collective-permute-start(bf16[2,32,1152]{2,1,0:T(8,128)(2,1)S(1)} %get-tuple-element.95), channel_id=1, source_target_pairs={{0,96},{1,97},{2,98},{3,99},{4,100},{5,101},{6,102},{7,103},{8,104... | collective-permute-start | bytes 442376 | tf_op jit(solution)/shard_map/ppermute | solution.py:28
  101.2 2.5 %collective-permute-start.17 = (bf16[2,32,1152]{2,1,0:T(8,128)(2,1)S(1)}, bf16[2,32,1152]{2,1,0:T(8,128)(2,1)S(1)}, u32[]{:S(2)}, u32[]{:S(2)}) collective-permute-start(bf16[2,32,1152]{2,1,0:T(8,128)(2,1)S(1)} %get-tuple-element.96), channel_id=1, source_target_pairs={{0,64},{32,96},{1,65},{33,97},{2,66},{34,98},{3,67},{35,99},{4,68}... | collective-permute-start | bytes 442376 | tf_op jit(solution)/shard_map/ppermute | solution.py:28
  103.7 2.4 %collective-permute-done.17 = bf16[2,32,1152]{2,1,0:T(8,128)(2,1)S(1)} collective-permute-done((bf16[2,32,1152]{2,1,0:T(8,128)(2,1)S(1)}, bf16[2,32,1152]{2,1,0:T(8,128)(2,1)S(1)}, u32[]{:S(2)}, u32[]{:S(2)}) %collective-permute-start.17) | collective-permute-done | bytes 147488 | tf_op jit(solution)/shard_map/ppermute | solution.py:28
  110.0 3.2 %collective-permute-done.21 = bf16[2,32,1152]{2,1,0:T(8,128)(2,1)S(1)} collective-permute-done((bf16[2,32,1152]{2,1,0:T(8,128)(2,1)S(1)}, bf16[2,32,1152]{2,1,0:T(8,128)(2,1)S(1)}, u32[]{:S(2)}, u32[]{:S(2)}) %collective-permute-start.21) | collective-permute-done | bytes 147488 | tf_op jit(solution)/shard_map/ppermute | solution.py:28
  113.2 1.6 collective-permute-done.20
  115.1 3.3 %collective-permute-start.23 = (bf16[4,32,1152]{2,1,0:T(8,128)(2,1)S(1)}, bf16[4,32,1152]{2,1,0:T(8,128)(2,1)S(1)}, u32[]{:S(2)}, u32[]{:S(2)}) collective-permute-start(bf16[4,32,1152]{2,1,0:T(8,128)(2,1)S(1)} %get-tuple-element.93), channel_id=1, source_target_pairs={{0,4},{2,6},{4,0},{6,2},{1,5},{3,7},{5,1},{7,3},{8,12},{10,14},{12... | collective-permute-start | bytes 884744 | tf_op jit(solution)/shard_map/ppermute | solution.py:22
  118.4 2.0 collective-permute-start.22
  120.4 3.0 %collective-permute-start.29 = (bf16[4,32,1152]{2,1,0:T(8,128)(2,1)S(1)}, bf16[4,32,1152]{2,1,0:T(8,128)(2,1)S(1)}, u32[]{:S(2)}, u32[]{:S(2)}) collective-permute-start(bf16[4,32,1152]{2,1,0:T(8,128)(2,1)S(1)} %get-tuple-element.92), channel_id=1, source_target_pairs={{0,16},{8,24},{16,0},{24,8},{1,17},{9,25},{17,1},{25,9},{2,18},{10... | collective-permute-start | bytes 884744 | tf_op jit(solution)/shard_map/ppermute | solution.py:22
  123.4 2.1 %collective-permute-start.28 = (bf16[4,32,1152]{2,1,0:T(8,128)(2,1)S(1)}, bf16[4,32,1152]{2,1,0:T(8,128)(2,1)S(1)}, u32[]{:S(2)}, u32[]{:S(2)}) collective-permute-start(bf16[4,32,1152]{2,1,0:T(8,128)(2,1)S(1)} %get-tuple-element.92), channel_id=1, source_target_pairs={{0,24},{8,0},{16,8},{24,16},{1,25},{9,1},{17,9},{25,17},{2,26},{10... | collective-permute-start | bytes 884744 | tf_op jit(solution)/shard_map/ppermute | solution.py:22
  125.7 1.5 collective-permute-start.27
  128.4 2.5 %collective-permute-done.29 = bf16[4,32,1152]{2,1,0:T(8,128)(2,1)S(1)} collective-permute-done((bf16[4,32,1152]{2,1,0:T(8,128)(2,1)S(1)}, bf16[4,32,1152]{2,1,0:T(8,128)(2,1)S(1)}, u32[]{:S(2)}, u32[]{:S(2)}) %collective-permute-start.29) | collective-permute-done | bytes 294944 | tf_op jit(solution)/shard_map/ppermute | solution.py:22
  131.4 2.7 %collective-permute-start.31 = (bf16[4,128,1152]{2,1,0:T(8,128)(2,1)S(1)}, bf16[4,128,1152]{2,1,0:T(8,128)(2,1)S(1)}, u32[]{:S(2)}, u32[]{:S(2)}) collective-permute-start(bf16[4,128,1152]{2,1,0:T(8,128)(2,1)S(1)} %pad_maximum_fusion.2.refs_3_), channel_id=1, source_target_pairs={{0,6},{2,0},{4,2},{6,4},{1,7},{3,1},{5,3},{7,5},{8,14},{10,8},{12,... | collective-permute-start | bytes 3538952 | tf_op jit(solution)/shard_map/ppermute | solution.py:22
  134.0 16.1 %collective-permute-start.25 = (bf16[512,1152]{0,1:T(8,128)(2,1)S(1)}, bf16[512,1152]{0,1:T(8,128)(2,1)S(1)}, u32[]{:S(2)}, u32[]{:S(2)}) collective-permute-start(bf16[512,1152]{0,1:T(8,128)(2,1)S(1)} %copy-done.10), channel_id=1, source_target_pairs={{0,1},{1,0},{2,3},{3,2},{4,5},{5,4},{6,7},{7,6},{8,9},{9,8},{10,11... | collective-permute-start | bytes 3538952 | tf_op jit(solution)/shard_map/ppermute | solution.py:32
  150.1 7.3 %collective-permute-done.27.refs_2_ = bf16[4,128,1152]{2,1,0:T(8,128)(2,1)S(1)} collective-permute-done((bf16[4,128,1152]{2,1,0:T(8,128)(2,1)S(1)}, bf16[4,128,1152]{2,1,0:T(8,128)(2,1)S(1)}, u32[]{:S(2)}, u32[]{:S(2)}) %collective-permute-start.27) | collective-permute-done | bytes 1179680 | tf_op jit(solution)/shard_map/ppermute | solution.py:22
  157.9 2.4 %collective-permute-start.33 = (bf16[4,64,1152]{2,1,0:T(8,128)(2,1)S(1)}, bf16[4,64,1152]{2,1,0:T(8,128)(2,1)S(1)}, u32[]{:S(2)}, u32[]{:S(2)}) collective-permute-start(bf16[4,64,1152]{2,1,0:T(8,128)(2,1)S(1)} %slice.162), channel_id=1, source_target_pairs={{0,24},{8,0},{16,8},{24,16},{1,25},{9,1},{17,9},{25,17},{2,26},{10... | collective-permute-start | bytes 1769480 | tf_op jit(solution)/shard_map/ppermute | solution.py:22
  161.7 1.6 collective-permute-start.35
  163.3 5.7 %shard_map.98.near_ref = f32[768,512]{1,0:T(8,128)S(1)} custom-call(s32[4]{0:T(128)S(1)} %copy-done.7, bf16[4,512,1152]{2,1,0:T(8,128)(2,1)S(1)} %bitcast.74, bf16[4,128,1152]{2,1,0:T(8,128)(2,1)S(1)} %pad_maximum_fusion.1.refs_0_, bf16[4,128,1152]{2,1,0:T(8,128)(2,1)S(1)} %collective-permute-done.26.refs_1_, ...), custom_call_target="tpu_custom_call" | custom-call | flops 3623878656 | bytes 14680064 | tf_op jit(solution)/shard_map/pallas_call | solution.py:54
  169.2 1.5 collective-permute-done.36.refs_9_.refs_3_
  170.7 2.3 %collective-permute-done.35.refs_8_.refs_2_ = bf16[4,64,1152]{2,1,0:T(8,128)(2,1)S(1)} collective-permute-done((bf16[4,64,1152]{2,1,0:T(8,128)(2,1)S(1)}, bf16[4,64,1152]{2,1,0:T(8,128)(2,1)S(1)}, u32[]{:S(2)}, u32[]{:S(2)}) %collective-permute-start.35) | collective-permute-done | bytes 589856 | tf_op jit(solution)/shard_map/ppermute | solution.py:22
  173.0 3.0 %shard_map.99 = (f32[512,512]{1,0:T(8,128)S(1)}, f32[512,512]{1,0:T(8,128)S(1)}) custom-call(s32[4]{0:T(128)S(1)} %copy-done.7, bf16[4,512,1152]{2,1,0:T(8,128)(2,1)S(1)} %bitcast.74, f32[768,512]{1,0:T(8,128)S(1)} %shard_map.98.near_ref, bf16[4,64,1152]{2,1,0:T(8,128)(2,1)S(1)} %collective-permute-done.33.refs_6_.refs_0_, ...), custom_call_target="tpu_custom_call" | custom-call | flops 1207959552 | bytes 10485760 | tf_op jit(solution)/shard_map/pallas_call | solution.py:54
  176.1 6.0 %collective-permute-start.38 = (f32[512,512]{1,0:T(8,128)S(1)}, f32[512,512]{1,0:T(8,128)S(1)}, u32[]{:S(2)}, u32[]{:S(2)}) collective-permute-start(f32[512,512]{1,0:T(8,128)S(1)} %get-tuple-element.80), channel_id=1, source_target_pairs={{0,1},{1,0},{2,3},{3,2},{4,5},{5,4},{6,7},{7,6},{8,9},{9,8},{10,11... | collective-permute-start | bytes 3145736 | tf_op jit(solution)/shard_map/ppermute | solution.py:32
  182.1 9.1 %shard_map.97 = (f32[4,512,1152]{2,1,0:T(8,128)}, f32[1,1152]{1,0:T(1,128)S(1)}) custom-call(s32[4]{0:T(128)S(1)} %copy-done.7, bf16[512,512]{1,0:T(8,128)(2,1)S(1)} %copy-done.3, bf16[512,512]{1,0:T(8,128)(2,1)S(1)} %copy-done.5, bf16[4,128,1152]{2,1,0:T(8,128)(2,1)S(1)} %pad_maximum_fusion.1.refs_0_, ...), custom_call_target="tpu_custom_call" | custom-call | flops 4831838208 | bytes 20971520 | tf_op jit(solution)/shard_map/pallas_call | solution.py:54
  192.6 1.4 collective-permute-done.37
  195.9 4.3 %shard_map.100 = f32[1152,512]{1,0:T(8,128)} custom-call(s32[4]{0:T(128)S(1)} %copy-done.7, bf16[1152,512]{1,0:T(8,128)(2,1)S(1)} %bitcast.75, bf16[1152,512]{1,0:T(8,128)(2,1)S(1)} %bitcast.76, bf16[512,512]{1,0:T(8,128)(2,1)S(1)} %get-tuple-element.83.grad_ref, bf16[512,512]{1,0:T(8,128)(2,1)S(1)} %collective-permute-done.39.other_grad_ref), custom_call_target="tpu_custom_call" | custom-call | flops 1207959552 | bytes 6291456 | tf_op jit(solution)/shard_map/pallas_call | solution.py:54
  (114 shorter events, 27.5 us)
Async XLA Ops:
  7.6 4.2 %collective-permute-start = (bf16[512,512]{1,0:T(8,128)(2,1)}, bf16[512,512]{1,0:T(8,128)(2,1)S(1)}, u32[]{:S(2)}, u32[]{:S(2)}) collective-permute-start(bf16[512,512]{1,0:T(8,128)(2,1)} %get-tuple-element.44), channel_id=1, source_target_pairs={{0,1},{1,0},{2,3},{3,2},{4,5},{5,4},{6,7},{7,6},{8,9},{9,8},{10,11... | collective-permute-start | bytes 1572872 | tf_op jit(solution)/shard_map/ppermute | solution.py:32
  11.9 10.7 %copy-start.13 = (bf16[1,512,144]{1,2,0:T(8,128)(2,1)S(1)}, bf16[1,512,144]{1,2,0:T(8,128)(2,1)}, u32[]{:S(2)}) copy-start(bf16[1,512,144]{1,2,0:T(8,128)(2,1)} %param.7) | copy-start | bytes 442372
  16.0 21.6 %collective-permute-start.1 = (bf16[4,64,1152]{2,1,0:T(8,128)(2,1)}, bf16[4,64,1152]{2,1,0:T(8,128)(2,1)S(1)}, u32[]{:S(2)}, u32[]{:S(2)}) collective-permute-start(bf16[4,64,1152]{2,1,0:T(8,128)(2,1)} %get-tuple-element.51), channel_id=1, source_target_pairs={{0,8},{8,16},{16,24},{24,0},{1,9},{9,17},{17,25},{25,1},{2,10},{10... | collective-permute-start | bytes 1769480 | tf_op jit(solution)/shard_map/ppermute | solution.py:22
  17.4 20.2 %collective-permute-start.2 = (bf16[4,64,1152]{2,1,0:T(8,128)(2,1)}, bf16[4,64,1152]{2,1,0:T(8,128)(2,1)S(1)}, u32[]{:S(2)}, u32[]{:S(2)}) collective-permute-start(bf16[4,64,1152]{2,1,0:T(8,128)(2,1)} %get-tuple-element.52), channel_id=1, source_target_pairs={{0,24},{8,0},{16,8},{24,16},{1,25},{9,1},{17,9},{25,17},{2,26},{10... | collective-permute-start | bytes 1769480 | tf_op jit(solution)/shard_map/ppermute | solution.py:22
  18.7 18.9 %collective-permute-start.3 = (bf16[4,64,1152]{2,1,0:T(8,128)(2,1)}, bf16[4,64,1152]{2,1,0:T(8,128)(2,1)S(1)}, u32[]{:S(2)}, u32[]{:S(2)}) collective-permute-start(bf16[4,64,1152]{2,1,0:T(8,128)(2,1)} %get-tuple-element.53), channel_id=1, source_target_pairs={{0,2},{2,4},{4,6},{6,0},{1,3},{3,5},{5,7},{7,1},{8,10},{10,12},{12... | collective-permute-start | bytes 1769480 | tf_op jit(solution)/shard_map/ppermute | solution.py:22
  20.5 17.1 %collective-permute-start.4 = (bf16[4,64,1152]{2,1,0:T(8,128)(2,1)}, bf16[4,64,1152]{2,1,0:T(8,128)(2,1)S(1)}, u32[]{:S(2)}, u32[]{:S(2)}) collective-permute-start(bf16[4,64,1152]{2,1,0:T(8,128)(2,1)} %get-tuple-element.54), channel_id=1, source_target_pairs={{0,6},{2,0},{4,2},{6,4},{1,7},{3,1},{5,3},{7,5},{8,14},{10,8},{12,... | collective-permute-start | bytes 1769480 | tf_op jit(solution)/shard_map/ppermute | solution.py:22
  33.3 17.3 %all-to-all-start = ((f32[16,32,144]{2,1,0:T(8,128)}), f32[16,32,144]{2,1,0:T(8,128)}, u32[]{:S(2)}, u32[]{:S(2)}) async-start(f32[16,32,144]{2,1,0:T(8,128)} %convert_subtract_fusion), calls=%async_computation | async-start | bytes 1048576 | tf_op jit(solution)/shard_map/all_to_all | solution.py:376
  41.1 34.2 %collective-permute-start.5 = (bf16[4,128,1152]{2,1,0:T(8,128)(2,1)S(1)}, bf16[4,128,1152]{2,1,0:T(8,128)(2,1)}, u32[]{:S(2)}, u32[]{:S(2)}) collective-permute-start(bf16[4,128,1152]{2,1,0:T(8,128)(2,1)S(1)} %get-tuple-element.55), channel_id=1, source_target_pairs={{0,8},{8,16},{16,24},{24,0},{1,9},{9,17},{17,25},{25,1},{2,10},{10... | collective-permute-start | bytes 3538952 | tf_op jit(solution)/shard_map/ppermute | solution.py:22
  42.4 33.0 %collective-permute-start.6 = (bf16[4,128,1152]{2,1,0:T(8,128)(2,1)}, bf16[4,128,1152]{2,1,0:T(8,128)(2,1)}, u32[]{:S(2)}, u32[]{:S(2)}) collective-permute-start(bf16[4,128,1152]{2,1,0:T(8,128)(2,1)} %get-tuple-element.56), channel_id=1, source_target_pairs={{0,24},{8,0},{16,8},{24,16},{1,25},{9,1},{17,9},{25,17},{2,26},{10... | collective-permute-start | bytes 3538952 | tf_op jit(solution)/shard_map/ppermute | solution.py:22
  43.8 28.6 %collective-permute-start.10 = (bf16[4,128,1152]{2,1,0:T(8,128)(2,1)}, bf16[4,128,1152]{2,1,0:T(8,128)(2,1)}, u32[]{:S(2)}, u32[]{:S(2)}) collective-permute-start(bf16[4,128,1152]{2,1,0:T(8,128)(2,1)} %get-tuple-element.58), channel_id=1, source_target_pairs={{0,2},{2,4},{4,6},{6,0},{1,3},{3,5},{5,7},{7,1},{8,10},{10,12},{12... | collective-permute-start | bytes 3538952 | tf_op jit(solution)/shard_map/ppermute | solution.py:22
  45.1 27.4 %collective-permute-start.11 = (bf16[4,128,1152]{2,1,0:T(8,128)(2,1)}, bf16[4,128,1152]{2,1,0:T(8,128)(2,1)}, u32[]{:S(2)}, u32[]{:S(2)}) collective-permute-start(bf16[4,128,1152]{2,1,0:T(8,128)(2,1)} %get-tuple-element.59), channel_id=1, source_target_pairs={{0,6},{2,0},{4,2},{6,4},{1,7},{3,1},{5,3},{7,5},{8,14},{10,8},{12,... | collective-permute-start | bytes 3538952 | tf_op jit(solution)/shard_map/ppermute | solution.py:22
  52.7 28.6 %collective-permute-start.14 = (f32[32,1152]{1,0:T(8,128)}, f32[32,1152]{1,0:T(8,128)}, u32[]{:S(2)}, u32[]{:S(2)}) collective-permute-start(f32[32,1152]{1,0:T(8,128)} %reshape.39), channel_id=1, source_target_pairs={{0,1},{1,0},{2,3},{3,2},{4,5},{5,4},{6,7},{7,6},{8,9},{9,8},{10,11... | collective-permute-start | bytes 442376 | tf_op jit(solution)/shard_map/ppermute | solution.py:32
  74.8 8.2 %collective-permute-start.15 = (bf16[4,32,1152]{2,1,0:T(8,128)(2,1)S(1)}, bf16[4,32,1152]{2,1,0:T(8,128)(2,1)}, u32[]{:S(2)}, u32[]{:S(2)}) collective-permute-start(bf16[4,32,1152]{2,1,0:T(8,128)(2,1)S(1)} %get-tuple-element.85), channel_id=1, source_target_pairs={{0,24},{8,0},{16,8},{24,16},{1,25},{9,1},{17,9},{25,17},{2,26},{10... | collective-permute-start | bytes 884744 | tf_op jit(solution)/shard_map/ppermute | solution.py:22
  77.8 8.2 %collective-permute-start.7 = (bf16[4,32,1152]{2,1,0:T(8,128)(2,1)}, bf16[4,32,1152]{2,1,0:T(8,128)(2,1)}, u32[]{:S(2)}, u32[]{:S(2)}) collective-permute-start(bf16[4,32,1152]{2,1,0:T(8,128)(2,1)} %get-tuple-element.87), channel_id=1, source_target_pairs={{0,2},{2,4},{4,6},{6,0},{1,3},{3,5},{5,7},{7,1},{8,10},{10,12},{12... | collective-permute-start | bytes 884744 | tf_op jit(solution)/shard_map/ppermute | solution.py:22
  78.3 8.5 %collective-permute-start.9 = (bf16[4,32,1152]{2,1,0:T(8,128)(2,1)S(1)}, bf16[4,32,1152]{2,1,0:T(8,128)(2,1)}, u32[]{:S(2)}, u32[]{:S(2)}) collective-permute-start(bf16[4,32,1152]{2,1,0:T(8,128)(2,1)S(1)} %get-tuple-element.88), channel_id=1, source_target_pairs={{0,6},{2,0},{4,2},{6,4},{1,7},{3,1},{5,3},{7,5},{8,14},{10,8},{12,... | collective-permute-start | bytes 884744 | tf_op jit(solution)/shard_map/ppermute | solution.py:22
  80.4 9.6 %collective-permute-start.8 = (bf16[4,32,1152]{2,1,0:T(8,128)(2,1)S(1)}, bf16[4,32,1152]{2,1,0:T(8,128)(2,1)}, u32[]{:S(2)}, u32[]{:S(2)}) collective-permute-start(bf16[4,32,1152]{2,1,0:T(8,128)(2,1)S(1)} %get-tuple-element.89), channel_id=1, source_target_pairs={{0,4},{2,6},{4,0},{6,2},{1,5},{3,7},{5,1},{7,3},{8,12},{10,14},{12... | collective-permute-start | bytes 884744 | tf_op jit(solution)/shard_map/ppermute | solution.py:22
  82.2 11.0 %collective-permute-start.12 = (bf16[4,32,1152]{2,1,0:T(8,128)(2,1)S(1)}, bf16[4,32,1152]{2,1,0:T(8,128)(2,1)S(1)}, u32[]{:S(2)}, u32[]{:S(2)}) collective-permute-start(bf16[4,32,1152]{2,1,0:T(8,128)(2,1)S(1)} %get-tuple-element.84), channel_id=1, source_target_pairs={{0,8},{8,16},{16,24},{24,0},{1,9},{9,17},{17,25},{25,1},{2,10},{10... | collective-permute-start | bytes 884744 | tf_op jit(solution)/shard_map/ppermute | solution.py:22
  83.0 10.2 %collective-permute-start.13 = (bf16[4,32,1152]{2,1,0:T(8,128)(2,1)S(1)}, bf16[4,32,1152]{2,1,0:T(8,128)(2,1)S(1)}, u32[]{:S(2)}, u32[]{:S(2)}) collective-permute-start(bf16[4,32,1152]{2,1,0:T(8,128)(2,1)S(1)} %get-tuple-element.86), channel_id=1, source_target_pairs={{0,16},{8,24},{16,0},{24,8},{1,17},{9,25},{17,1},{25,9},{2,18},{10... | collective-permute-start | bytes 884744 | tf_op jit(solution)/shard_map/ppermute | solution.py:22
  94.9 68.4 %slice-start = ((s8[4718592]{0:T(1024)(128)(4,1)}), s8[4194304]{0:T(1024)(128)(4,1)S(1)}, s32[]{:S(2)}) async-start(s8[4718592]{0:T(1024)(128)(4,1)} %bitcast.73), calls=%async_computation.1 | async-start | bytes 8388608
  94.9 8.7 %collective-permute-start.16 = (bf16[2,32,1152]{2,1,0:T(8,128)(2,1)S(1)}, bf16[2,32,1152]{2,1,0:T(8,128)(2,1)S(1)}, u32[]{:S(2)}, u32[]{:S(2)}) collective-permute-start(bf16[2,32,1152]{2,1,0:T(8,128)(2,1)S(1)} %get-tuple-element.94), channel_id=1, source_target_pairs={{0,32},{32,64},{64,96},{1,33},{33,65},{65,97},{2,34},{34,66},{66,9... | collective-permute-start | bytes 442376 | tf_op jit(solution)/shard_map/ppermute | solution.py:28
  98.4 5.3 %collective-permute-start.18 = (bf16[2,32,1152]{2,1,0:T(8,128)(2,1)S(1)}, bf16[2,32,1152]{2,1,0:T(8,128)(2,1)S(1)}, u32[]{:S(2)}, u32[]{:S(2)}) collective-permute-start(bf16[2,32,1152]{2,1,0:T(8,128)(2,1)S(1)} %get-tuple-element.95), channel_id=1, source_target_pairs={{0,96},{1,97},{2,98},{3,99},{4,100},{5,101},{6,102},{7,103},{8,104... | collective-permute-start | bytes 442376 | tf_op jit(solution)/shard_map/ppermute | solution.py:28
  101.2 4.9 %collective-permute-start.17 = (bf16[2,32,1152]{2,1,0:T(8,128)(2,1)S(1)}, bf16[2,32,1152]{2,1,0:T(8,128)(2,1)S(1)}, u32[]{:S(2)}, u32[]{:S(2)}) collective-permute-start(bf16[2,32,1152]{2,1,0:T(8,128)(2,1)S(1)} %get-tuple-element.96), channel_id=1, source_target_pairs={{0,64},{32,96},{1,65},{33,97},{2,66},{34,98},{3,67},{35,99},{4,68}... | collective-permute-start | bytes 442376 | tf_op jit(solution)/shard_map/ppermute | solution.py:28
  106.1 7.1 %collective-permute-start.21 = (bf16[2,32,1152]{2,1,0:T(8,128)(2,1)S(1)}, bf16[2,32,1152]{2,1,0:T(8,128)(2,1)S(1)}, u32[]{:S(2)}, u32[]{:S(2)}) collective-permute-start(bf16[2,32,1152]{2,1,0:T(8,128)(2,1)S(1)} %fusion.17), channel_id=1, source_target_pairs={{96,0},{97,1},{98,2},{99,3},{100,4},{101,5},{102,6},{103,7},{104,8... | collective-permute-start | bytes 442376 | tf_op jit(solution)/shard_map/ppermute | solution.py:28
  107.4 7.4 %collective-permute-start.20 = (bf16[2,32,1152]{2,1,0:T(8,128)(2,1)S(1)}, bf16[2,32,1152]{2,1,0:T(8,128)(2,1)S(1)}, u32[]{:S(2)}, u32[]{:S(2)}) collective-permute-start(bf16[2,32,1152]{2,1,0:T(8,128)(2,1)S(1)} %fusion.17), channel_id=1, source_target_pairs={{64,0},{96,32},{65,1},{97,33},{66,2},{98,34},{67,3},{99,35},{68,4}... | collective-permute-start | bytes 442376 | tf_op jit(solution)/shard_map/ppermute | solution.py:28
  108.7 6.1 %collective-permute-start.19 = (bf16[2,32,1152]{2,1,0:T(8,128)(2,1)S(1)}, bf16[2,32,1152]{2,1,0:T(8,128)(2,1)S(1)}, u32[]{:S(2)}, u32[]{:S(2)}) collective-permute-start(bf16[2,32,1152]{2,1,0:T(8,128)(2,1)S(1)} %fusion.17), channel_id=1, source_target_pairs={{32,0},{64,32},{96,64},{33,1},{65,33},{97,65},{34,2},{66,34},{98,6... | collective-permute-start | bytes 442376 | tf_op jit(solution)/shard_map/ppermute | solution.py:28
  115.0 8.4 %collective-permute-start.24 = (bf16[4,32,1152]{2,1,0:T(8,128)(2,1)S(1)}, bf16[4,32,1152]{2,1,0:T(8,128)(2,1)S(1)}, u32[]{:S(2)}, u32[]{:S(2)}) collective-permute-start(bf16[4,32,1152]{2,1,0:T(8,128)(2,1)S(1)} %get-tuple-element.93), channel_id=1, source_target_pairs={{0,2},{2,4},{4,6},{6,0},{1,3},{3,5},{5,7},{7,1},{8,10},{10,12},{12... | collective-permute-start | bytes 884744 | tf_op jit(solution)/shard_map/ppermute | solution.py:22
  115.1 10.5 %collective-permute-start.23 = (bf16[4,32,1152]{2,1,0:T(8,128)(2,1)S(1)}, bf16[4,32,1152]{2,1,0:T(8,128)(2,1)S(1)}, u32[]{:S(2)}, u32[]{:S(2)}) collective-permute-start(bf16[4,32,1152]{2,1,0:T(8,128)(2,1)S(1)} %get-tuple-element.93), channel_id=1, source_target_pairs={{0,4},{2,6},{4,0},{6,2},{1,5},{3,7},{5,1},{7,3},{8,12},{10,14},{12... | collective-permute-start | bytes 884744 | tf_op jit(solution)/shard_map/ppermute | solution.py:22
  118.4 7.2 %collective-permute-start.22 = (bf16[4,32,1152]{2,1,0:T(8,128)(2,1)S(1)}, bf16[4,32,1152]{2,1,0:T(8,128)(2,1)S(1)}, u32[]{:S(2)}, u32[]{:S(2)}) collective-permute-start(bf16[4,32,1152]{2,1,0:T(8,128)(2,1)S(1)} %get-tuple-element.93), channel_id=1, source_target_pairs={{0,6},{2,0},{4,2},{6,4},{1,7},{3,1},{5,3},{7,5},{8,14},{10,8},{12,... | collective-permute-start | bytes 884744 | tf_op jit(solution)/shard_map/ppermute | solution.py:22
  120.4 43.0 %slice-start.1 = ((s8[4718592]{0:T(1024)(128)(4,1)}), s8[524288]{0:T(1024)(128)(4,1)S(1)}, s32[]{:S(2)}) async-start(s8[4718592]{0:T(1024)(128)(4,1)} %bitcast.73), calls=%async_computation.2 | async-start | bytes 1048576
  120.4 8.1 %collective-permute-start.30 = (bf16[4,32,1152]{2,1,0:T(8,128)(2,1)S(1)}, bf16[4,32,1152]{2,1,0:T(8,128)(2,1)S(1)}, u32[]{:S(2)}, u32[]{:S(2)}) collective-permute-start(bf16[4,32,1152]{2,1,0:T(8,128)(2,1)S(1)} %get-tuple-element.92), channel_id=1, source_target_pairs={{0,8},{8,16},{16,24},{24,0},{1,9},{9,17},{17,25},{25,1},{2,10},{10... | collective-permute-start | bytes 884744 | tf_op jit(solution)/shard_map/ppermute | solution.py:22
  120.4 10.6 %collective-permute-start.29 = (bf16[4,32,1152]{2,1,0:T(8,128)(2,1)S(1)}, bf16[4,32,1152]{2,1,0:T(8,128)(2,1)S(1)}, u32[]{:S(2)}, u32[]{:S(2)}) collective-permute-start(bf16[4,32,1152]{2,1,0:T(8,128)(2,1)S(1)} %get-tuple-element.92), channel_id=1, source_target_pairs={{0,16},{8,24},{16,0},{24,8},{1,17},{9,25},{17,1},{25,9},{2,18},{10... | collective-permute-start | bytes 884744 | tf_op jit(solution)/shard_map/ppermute | solution.py:22
  123.4 7.8 %collective-permute-start.28 = (bf16[4,32,1152]{2,1,0:T(8,128)(2,1)S(1)}, bf16[4,32,1152]{2,1,0:T(8,128)(2,1)S(1)}, u32[]{:S(2)}, u32[]{:S(2)}) collective-permute-start(bf16[4,32,1152]{2,1,0:T(8,128)(2,1)S(1)} %get-tuple-element.92), channel_id=1, source_target_pairs={{0,24},{8,0},{16,8},{24,16},{1,25},{9,1},{17,9},{25,17},{2,26},{10... | collective-permute-start | bytes 884744 | tf_op jit(solution)/shard_map/ppermute | solution.py:22
  125.7 31.8 %collective-permute-start.27 = (bf16[4,128,1152]{2,1,0:T(8,128)(2,1)S(1)}, bf16[4,128,1152]{2,1,0:T(8,128)(2,1)S(1)}, u32[]{:S(2)}, u32[]{:S(2)}) collective-permute-start(bf16[4,128,1152]{2,1,0:T(8,128)(2,1)S(1)} %pad_maximum_fusion.1.refs_0_), channel_id=1, source_target_pairs={{0,8},{8,16},{16,24},{24,0},{1,9},{9,17},{17,25},{25,1},{2,10},{10... | collective-permute-start | bytes 3538952 | tf_op jit(solution)/shard_map/ppermute | solution.py:22
  127.2 30.7 %collective-permute-start.26 = (bf16[4,128,1152]{2,1,0:T(8,128)(2,1)S(1)}, bf16[4,128,1152]{2,1,0:T(8,128)(2,1)S(1)}, u32[]{:S(2)}, u32[]{:S(2)}) collective-permute-start(bf16[4,128,1152]{2,1,0:T(8,128)(2,1)S(1)} %pad_maximum_fusion.1.refs_0_), channel_id=1, source_target_pairs={{0,24},{8,0},{16,8},{24,16},{1,25},{9,1},{17,9},{25,17},{2,26},{10... | collective-permute-start | bytes 3538952 | tf_op jit(solution)/shard_map/ppermute | solution.py:22
  131.3 29.1 %collective-permute-start.32 = (bf16[4,128,1152]{2,1,0:T(8,128)(2,1)S(1)}, bf16[4,128,1152]{2,1,0:T(8,128)(2,1)S(1)}, u32[]{:S(2)}, u32[]{:S(2)}) collective-permute-start(bf16[4,128,1152]{2,1,0:T(8,128)(2,1)S(1)} %pad_maximum_fusion.2.refs_3_), channel_id=1, source_target_pairs={{0,2},{2,4},{4,6},{6,0},{1,3},{3,5},{5,7},{7,1},{8,10},{10,12},{12... | collective-permute-start | bytes 3538952 | tf_op jit(solution)/shard_map/ppermute | solution.py:22
  131.4 30.3 %collective-permute-start.31 = (bf16[4,128,1152]{2,1,0:T(8,128)(2,1)S(1)}, bf16[4,128,1152]{2,1,0:T(8,128)(2,1)S(1)}, u32[]{:S(2)}, u32[]{:S(2)}) collective-permute-start(bf16[4,128,1152]{2,1,0:T(8,128)(2,1)S(1)} %pad_maximum_fusion.2.refs_3_), channel_id=1, source_target_pairs={{0,6},{2,0},{4,2},{6,4},{1,7},{3,1},{5,3},{7,5},{8,14},{10,8},{12,... | collective-permute-start | bytes 3538952 | tf_op jit(solution)/shard_map/ppermute | solution.py:22
  134.0 29.3 %collective-permute-start.25 = (bf16[512,1152]{0,1:T(8,128)(2,1)S(1)}, bf16[512,1152]{0,1:T(8,128)(2,1)S(1)}, u32[]{:S(2)}, u32[]{:S(2)}) collective-permute-start(bf16[512,1152]{0,1:T(8,128)(2,1)S(1)} %copy-done.10), channel_id=1, source_target_pairs={{0,1},{1,0},{2,3},{3,2},{4,5},{5,4},{6,7},{7,6},{8,9},{9,8},{10,11... | collective-permute-start | bytes 3538952 | tf_op jit(solution)/shard_map/ppermute | solution.py:32
  157.5 11.7 %collective-permute-start.34 = (bf16[4,64,1152]{2,1,0:T(8,128)(2,1)S(1)}, bf16[4,64,1152]{2,1,0:T(8,128)(2,1)S(1)}, u32[]{:S(2)}, u32[]{:S(2)}) collective-permute-start(bf16[4,64,1152]{2,1,0:T(8,128)(2,1)S(1)} %slice.163), channel_id=1, source_target_pairs={{0,8},{8,16},{16,24},{24,0},{1,9},{9,17},{17,25},{25,1},{2,10},{10... | collective-permute-start | bytes 1769480 | tf_op jit(solution)/shard_map/ppermute | solution.py:22
  157.9 11.3 %collective-permute-start.33 = (bf16[4,64,1152]{2,1,0:T(8,128)(2,1)S(1)}, bf16[4,64,1152]{2,1,0:T(8,128)(2,1)S(1)}, u32[]{:S(2)}, u32[]{:S(2)}) collective-permute-start(bf16[4,64,1152]{2,1,0:T(8,128)(2,1)S(1)} %slice.162), channel_id=1, source_target_pairs={{0,24},{8,0},{16,8},{24,16},{1,25},{9,1},{17,9},{25,17},{2,26},{10... | collective-permute-start | bytes 1769480 | tf_op jit(solution)/shard_map/ppermute | solution.py:22
  160.4 10.3 %collective-permute-start.36 = (bf16[4,64,1152]{2,1,0:T(8,128)(2,1)S(1)}, bf16[4,64,1152]{2,1,0:T(8,128)(2,1)S(1)}, u32[]{:S(2)}, u32[]{:S(2)}) collective-permute-start(bf16[4,64,1152]{2,1,0:T(8,128)(2,1)S(1)} %slice.165), channel_id=1, source_target_pairs={{0,2},{2,4},{4,6},{6,0},{1,3},{3,5},{5,7},{7,1},{8,10},{10,12},{12... | collective-permute-start | bytes 1769480 | tf_op jit(solution)/shard_map/ppermute | solution.py:22
  161.7 11.4 %collective-permute-start.35 = (bf16[4,64,1152]{2,1,0:T(8,128)(2,1)S(1)}, bf16[4,64,1152]{2,1,0:T(8,128)(2,1)S(1)}, u32[]{:S(2)}, u32[]{:S(2)}) collective-permute-start(bf16[4,64,1152]{2,1,0:T(8,128)(2,1)S(1)} %slice.164), channel_id=1, source_target_pairs={{0,6},{2,0},{4,2},{6,4},{1,7},{3,1},{5,3},{7,5},{8,14},{10,8},{12,... | collective-permute-start | bytes 1769480 | tf_op jit(solution)/shard_map/ppermute | solution.py:22
  169.0 13.1 %copy-start.3 = (bf16[512,512]{1,0:T(8,128)(2,1)S(1)}, bf16[512,512]{1,0:T(8,128)(2,1)}, u32[]{:S(2)}) copy-start(bf16[512,512]{1,0:T(8,128)(2,1)} %get-tuple-element.43.own_ref) | copy-start | bytes 1572868
  169.0 13.1 %copy-start.5 = (bf16[512,512]{1,0:T(8,128)(2,1)S(1)}, bf16[512,512]{1,0:T(8,128)(2,1)}, u32[]{:S(2)}) copy-start(bf16[512,512]{1,0:T(8,128)(2,1)} %copy-done.4) | copy-start | bytes 1572868
  176.1 15.1 %copy-start.11 = (f32[512,512]{1,0:T(8,128)S(1)}, f32[512,512]{1,0:T(8,128)}, u32[]{:S(2)}) copy-start(f32[512,512]{1,0:T(8,128)} %get-tuple-element.81) | copy-start | bytes 3145732
  176.1 15.1 %collective-permute-start.38 = (f32[512,512]{1,0:T(8,128)S(1)}, f32[512,512]{1,0:T(8,128)S(1)}, u32[]{:S(2)}, u32[]{:S(2)}) collective-permute-start(f32[512,512]{1,0:T(8,128)S(1)} %get-tuple-element.80), channel_id=1, source_target_pairs={{0,1},{1,0},{2,3},{3,2},{4,5},{5,4},{6,7},{7,6},{8,9},{9,8},{10,11... | collective-permute-start | bytes 3145736 | tf_op jit(solution)/shard_map/ppermute | solution.py:32
  192.0 3.9 %collective-permute-start.39 = (bf16[512,512]{1,0:T(8,128)(2,1)S(1)}, bf16[512,512]{1,0:T(8,128)(2,1)S(1)}, u32[]{:S(2)}, u32[]{:S(2)}) collective-permute-start(bf16[512,512]{1,0:T(8,128)(2,1)S(1)} %get-tuple-element.83.grad_ref), channel_id=1, source_target_pairs={{0,1},{1,0},{2,3},{3,2},{4,5},{5,4},{6,7},{7,6},{8,9},{9,8},{10,11... | collective-permute-start | bytes 1572872 | tf_op jit(solution)/shard_map/ppermute | solution.py:32
  192.1 1.9 collective-permute-start.37
  194.1 1.2 collective-permute-start.40
  (11 other events, 62.5 us)

commit v6 on v5

--- a/solution.py
+++ b/solution.py
@@ -192,7 +192,7 @@
 
 
 def near_act_kernel(where, w_ref, *refs):
-    *x_refs, act_ref, err_ref = refs
+    *x_refs, act_ref, sum_ref, err_ref = refs
     k = pl.program_id(0)
     step = x_refs[0].shape[1]
 
@@ -209,9 +209,13 @@
                 err_ref[i : i + 256, :], w_ref[0], (((1,), (1,)), ((), ())), preferred_element_type=F32
             )
 
-
-def far_act_kernel(where, w_ref, near_ref, *refs, ring):
-    *x_refs, own_ref, other_ref, err_ref, act_ref = refs
+    @pl.when(k == 0)
+    def _():
+        sum_ref[...] = jnp.sum(err_ref[...].astype(F32), axis=0, keepdims=True)
+
+
+def far_act_kernel(where, w_ref, near_ref, near_sum_ref, *refs, ring):
+    *x_refs, own_ref, other_ref, sum_ref, err_ref, act_ref = refs
     k = pl.program_id(0)
     step = x_refs[0].shape[1]
 
@@ -226,6 +230,10 @@
         act_ref[...] += lax.dot_general(
             err_ref[...], w_ref[0], (((1,), (1,)), ((), ())), preferred_element_type=F32
         )
+
+    @pl.when(k == 0)
+    def _():
+        sum_ref[...] = near_sum_ref[...] + jnp.sum(err_ref[...].astype(F32), axis=0, keepdims=True)
 
     @pl.when(k == pl.num_programs(0) - 1)
     def _():
@@ -251,13 +259,13 @@
     layers, feats, _ = weights.shape
     n = near[0].shape[1]
     target = pl.BlockSpec((1, feats, width), lambda k, w: (lax.rem(w[0] + k, layers), 0, 0))
-    [act] = call(
+    act, sums = call(
         near_act_kernel,
         where,
         (weights, *near),
         [target] + [each(1, n, width)] * 6,
-        [((6 * n, feats), F32)],
-        [fixed(6 * n, feats)],
+        [((6 * n, feats), F32), ((1, width), F32)],
+        [fixed(6 * n, feats), fixed(1, width)],
         layers,
         [pltpu.VMEM((6 * n, width), BF16)],
         2 * layers * 6 * n * feats * width,
@@ -266,10 +274,10 @@
     return call(
         functools.partial(far_act_kernel, ring=ring),
         where,
-        (weights, act, *far),
-        [target, fixed(6 * n, feats)] + [each(1, n // 2, width)] * 4,
-        [((4 * n, feats), F32)] * 2,
-        [fixed(4 * n, feats)] * 2,
+        (weights, act, sums, *far),
+        [target, fixed(6 * n, feats), fixed(1, width)] + [each(1, n // 2, width)] * 4,
+        [((4 * n, feats), F32)] * 2 + [((1, width), F32)],
+        [fixed(4 * n, feats)] * 2 + [fixed(1, width)],
         layers,
         [pltpu.VMEM((2 * n, width), BF16), pltpu.VMEM((2 * n, feats), F32)],
         2 * layers * 2 * n * feats * width,
@@ -278,7 +286,7 @@
 
 
 def dec_kernel(where, own_ref, other_ref, *refs):
-    *x_refs, dec_ref, sum_ref, err_ref = refs
+    *x_refs, dec_ref, mark_ref, err_ref = refs
     live = where[0] + pl.program_id(0) < pl.num_programs(0)
     rows = own_ref.shape[0]
 
@@ -299,7 +307,7 @@
 
     @pl.when(pl.program_id(0) == 0)
     def _():
-        sum_ref[...] = jnp.sum(err_ref[...].astype(F32), axis=0, keepdims=True)
+        mark_ref[...] = jnp.zeros_like(mark_ref)
 
 
 def dec_gradient(where, own_lat, other_lat, errs):
@@ -421,15 +429,16 @@
     own_in, other_in, *got = lax.optimization_barrier((own_in, other_in, *got))
     near = [own_a, *got[:2], own_b, *got[2:]]
 
-    own_act, other_act = act_grads(where, weights, near, far, width, ring)
-    dec_grad, sums = dec_gradient(where, own_lat, other_lat, [*near, *far])
-    pre, sums = lax.optimization_barrier((pre, sums))
+    own_act, other_act, sums = act_grads(where, weights, near, far, width, ring)
+    dec_grad, mark = dec_gradient(where, own_lat, other_lat, [*near, *far])
+    other_sums = swap(sums)
+    pre, mark, other_sums = lax.optimization_barrier((pre, mark, other_sums))
     act = own_act + swap(other_act)
     pre_grad = jax.vjp(smooth, pre)[1](act)[0].astype(BF16)
     own_sum = jnp.sum(pre_grad.astype(F32), axis=0, keepdims=True)
     enc_grad = enc_gradient(where, own_in, other_in, pre_grad, swap(pre_grad))
     enc_bias_grad = own_sum + swap(own_sum)
-    both = turned(jnp.concatenate([sums, swap(sums)], 0), 0, c).reshape(1, model)
+    both = turned(jnp.concatenate([sums, other_sums], 0), 0, c).reshape(1, model)
     size = dec_bias.shape[1]
     dec_bias_grad = lax.dynamic_slice_in_dim(both, (x * ring + z) * size, size, 1)
     return dec_grad[None], dec_bias_grad, enc_grad[None], enc_bias_grad

time: 201 us -> 222 us (1.10)
  waiting for transfers between devices: 48.4 us -> 71.6 us
  starting transfers between devices: 82.3 us -> 70.5 us
  local copies, waits for them, and re-layouts: 9.34 us -> 16.8 us
    ppermute x28, waiting for transfers between devices: 39.4 us -> 55.2 us  [shift(): return lax.ppermute(value, axis, [(i, (i + step) % n) for i in range(n)])]
    ppermute x7, starting transfers between devices: 26.7 us -> 17.8 us  [swap(): return lax.ppermute(value, TOK, [(0, 1), (1, 0)])]
    unnamed x37 -> x73, local copies, waits for them, and re-layouts: 1.54 us -> 8.61 us
    ppermute x6, waiting for transfers between devices: 7.16 us -> 12.7 us  [send_up(): return lax.ppermute(value, LAYER, pairs)]
    ppermute x28, starting transfers between devices: 38.7 us -> 35.3 us  [shift(): return lax.ppermute(value, axis, [(i, (i + step) % n) for i in range(n)])]
  transfers between devices with their start and end apart: 42 -> 42, of which waited for: 17 -> 24; matrix products, arithmetic and copies ran while one was open for 10% -> 9% of each run, Pallas kernels for 14% -> 12%
where the time goes in v6:
time: 222 us; the launch traced here: 221 us
  waiting for transfers between devices  71.6 us (32%)
  starting transfers between devices  70.5 us (32%)
  Pallas kernels  46.3 us (21%)
  local copies, waits for them, and re-layouts  16.8 us (8%)
  other arithmetic  14.7 us (7%)
    ppermute x28, waiting for transfers between devices, shift(): return lax.ppermute(value, axis, [(i, (i + step) % n) for i in range(n)])  55.2 us
    pallas_call x8, Pallas kernels, call(): pl.pallas_call(kernel, out_shape=[jax.ShapeDtypeStruct(shape, dtype) for...  46.3 us
    ppermute x28, starting transfers between devices, shift(): return lax.ppermute(value, axis, [(i, (i + step) % n) for i in range(n)])  35.3 us
    ppermute x7, starting transfers between devices, swap(): return lax.ppermute(value, TOK, [(0, 1), (1, 0)])  17.8 us
    ppermute x6, starting transfers between devices, send_up(): return lax.ppermute(value, LAYER, pairs)  13.2 us
    ppermute x6, waiting for transfers between devices, send_up(): return lax.ppermute(value, LAYER, pairs)  12.7 us
    unnamed x73, local copies, waits for them, and re-layouts  8.61 us
  transfers between devices with their start and end apart: 42, of which 24 were waited for; matrix products, arithmetic and copies ran while one was open for 9% of the time, Pallas kernels for 12%

profile of v6, /device:TPU:1, one launch (start us, length us, event | category | flops | bytes accessed | tf_op | source)
XLA Modules:
  0.0 221.2 jit_solution(13513055417059961731)
XLA Ops:
  1.2 6.4 %shard_map.93 = (f32[512,512]{1,0:T(8,128)}, bf16[512,512]{1,0:T(8,128)(2,1)}, bf16[512,512]{1,0:T(8,128)(2,1)}) custom-call(s32[4]{0:T(128)} %pad_add_fusion.where, bf16[512,2304]{1,0:T(8,128)(2,1)} %bitcast.78, bf16[2304,512]{1,0:T(8,128)(2,1)} %bitcast.80, f32[1,512]{1,0:T(1,128)} %bias_ref.1), custom_call_target="tpu_custom_call" | custom-call | flops 1207959552 | bytes 8388608 | tf_op jit(solution)/shard_map/pallas_call | solution.py:54
  7.6 1.4 collective-permute-start
  9.0 2.8 %dynamic-slice_bitcast_fusion.w_ref = bf16[4,512,1152]{2,1,0:T(8,128)(2,1)S(1)} fusion(bf16[1,4,512,2304]{3,2,1,0:T(8,128)(2,1)} %param.10, s32[]{:T(128)S(6)} %select_n.26), kind=kLoop, calls=%fused_computation.4 | loop fusion | bytes 9437188 | tf_op jit(solution)/shard_map/dynamic_slice | solution.py:367
  11.9 4.2 %shard_map.95 = (bf16[4,64,1152]{2,1,0:T(8,128)(2,1)}, bf16[4,64,1152]{2,1,0:T(8,128)(2,1)}, bf16[4,64,1152]{2,1,0:T(8,128)(2,1)}, bf16[4,64,1152]{2,1,0:T(8,128)(2,1)}) custom-call(s32[4]{0:T(128)S(1)} %copy-done.25, bf16[512,512]{1,0:T(8,128)(2,1)S(1)} %copy-done.13, bf16[512,512]{1,0:T(8,128)(2,1)S(1)} %collective-permute-done.other_ref, ...), custom_call_target="tpu_custom_call" | custom-call | flops 1207959552 | bytes 8388608 | tf_op jit(solution)/shard_map/pallas_call | solution.py:54
  18.9 1.7 collective-permute-start.3
  20.6 2.1 collective-permute-start.4
  23.6 9.0 %shard_map.94 = (f32[4,128,1152]{2,1,0:T(8,128)}, bf16[4,128,1152]{2,1,0:T(8,128)(2,1)}, bf16[4,128,1152]{2,1,0:T(8,128)(2,1)}, f32[4,128,1152]{2,1,0:T(8,128)},...) custom-call(s32[4]{0:T(128)} %pad_add_fusion.where, bf16[512,512]{1,0:T(8,128)(2,1)} %get-tuple-element.45.own_ref, ...), custom_call_target="tpu_custom_call" | custom-call | flops 3623878656 | bytes 8388608 | tf_op jit(solution)/shard_map/pallas_call | solution.py:54
  33.5 4.2 %all-to-all-start = ((f32[16,32,144]{2,1,0:T(8,128)}), f32[16,32,144]{2,1,0:T(8,128)}, u32[]{:S(2)}, u32[]{:S(2)}) async-start(f32[16,32,144]{2,1,0:T(8,128)} %convert_subtract_fusion), calls=%async_computation | async-start | bytes 1048576 | tf_op jit(solution)/shard_map/all_to_all | solution.py:384
  37.8 3.5 %shard_map.96 = (bf16[4,128,1152]{2,1,0:T(8,128)(2,1)S(1)}, bf16[4,128,1152]{2,1,0:T(8,128)(2,1)}, bf16[4,128,1152]{2,1,0:T(8,128)(2,1)}, bf16[4,128,1152]{2,1,0:T(8,128)(2,1)}) custom-call(s32[4]{0:T(128)S(1)} %copy-done.26, bf16[4,128,1152]{2,1,0:T(8,128)(2,1)S(1)} %copy-done.1, ...), custom_call_target="tpu_custom_call", output_to_operand_aliasing={{0}: (1, {}), {1}: (2, {}), {2}: (3, {}), {3}: (4, {})} | custom-call | flops 2359296 | bytes 7077888 | tf_op jit(solution)/shard_map/pallas_call | solution.py:54
  42.5 1.5 collective-permute-start.11
  45.2 1.5 collective-permute-start.6
  48.4 1.4 constant_dynamic-slice_fusion.3
  49.7 1.6 copy.29
  51.3 1.5 copy.30
  54.2 2.4 %collective-permute-start.14 = (f32[32,1152]{1,0:T(8,128)S(1)}, f32[32,1152]{1,0:T(8,128)S(1)}, u32[]{:S(2)}, u32[]{:S(2)}) collective-permute-start(f32[32,1152]{1,0:T(8,128)S(1)} %reshape.39), channel_id=1, source_target_pairs={{0,1},{1,0},{2,3},{3,2},{4,5},{5,4},{6,7},{7,6},{8,9},{9,8},{10,11... | collective-permute-start | bytes 442376 | tf_op jit(solution)/shard_map/ppermute | solution.py:32
  57.6 15.6 %collective-permute-done.10 = bf16[4,128,1152]{2,1,0:T(8,128)(2,1)} collective-permute-done((bf16[4,128,1152]{2,1,0:T(8,128)(2,1)}, bf16[4,128,1152]{2,1,0:T(8,128)(2,1)}, u32[]{:S(2)}, u32[]{:S(2)}) %collective-permute-start.10) | collective-permute-done | bytes 1179680 | tf_op jit(solution)/shard_map/ppermute | solution.py:22
  73.2 2.4 %add_convert_fusion.2 = (bf16[4,32,1152]{2,1,0:T(8,128)(2,1)S(1)}, bf16[4,32,1152]{2,1,0:T(8,128)(2,1)S(1)}, bf16[4,32,1152]{2,1,0:T(8,128)(2,1)S(1)}) fusion(f32[4,128,1152]{2,1,0:T(8,128)} %get-tuple-element.59, bf16[4,128,1152]{2,1,0:T(8,128)(2,1)} %collective-permute-done.11, bf16[4,128,1152]{2,1,0:T(8,128)(2,1)} %collective-permute-done.10), kind=kLoop, calls=%fused_computation.27 | loop fusion | flops 2211840 | bytes 4423680 | tf_op jit(solution)/shard_map/convert_element_type | solution.py:405
  75.6 1.6 collective-permute-start.15
  77.2 2.1 collective-permute-start.13
  79.3 1.8 add_convert_fusion.5
  83.2 1.7 collective-permute-start.9
  86.1 5.7 %collective-permute-done.13 = bf16[4,32,1152]{2,1,0:T(8,128)(2,1)S(1)} collective-permute-done((bf16[4,32,1152]{2,1,0:T(8,128)(2,1)S(1)}, bf16[4,32,1152]{2,1,0:T(8,128)(2,1)S(1)}, u32[]{:S(2)}, u32[]{:S(2)}) %collective-permute-start.13) | collective-permute-done | bytes 294944 | tf_op jit(solution)/shard_map/ppermute | solution.py:22
  91.8 1.5 add_bitcast_fusion
  93.3 2.7 %collective-permute-done.9 = bf16[4,32,1152]{2,1,0:T(8,128)(2,1)S(1)} collective-permute-done((bf16[4,32,1152]{2,1,0:T(8,128)(2,1)S(1)}, bf16[4,32,1152]{2,1,0:T(8,128)(2,1)S(1)}, u32[]{:S(2)}, u32[]{:S(2)}) %collective-permute-start.9) | collective-permute-done | bytes 294944 | tf_op jit(solution)/shard_map/ppermute | solution.py:22
  97.5 3.5 %collective-permute-start.16 = (bf16[2,32,1152]{2,1,0:T(8,128)(2,1)S(1)}, bf16[2,32,1152]{2,1,0:T(8,128)(2,1)S(1)}, u32[]{:S(2)}, u32[]{:S(2)}) collective-permute-start(bf16[2,32,1152]{2,1,0:T(8,128)(2,1)S(1)} %get-tuple-element.98), channel_id=1, source_target_pairs={{0,32},{32,64},{64,96},{1,33},{33,65},{65,97},{2,34},{34,66},{66,9... | collective-permute-start | bytes 442376 | tf_op jit(solution)/shard_map/ppermute | solution.py:28
  100.9 4.5 %collective-permute-start.17 = (bf16[2,32,1152]{2,1,0:T(8,128)(2,1)S(1)}, bf16[2,32,1152]{2,1,0:T(8,128)(2,1)S(1)}, u32[]{:S(2)}, u32[]{:S(2)}) collective-permute-start(bf16[2,32,1152]{2,1,0:T(8,128)(2,1)S(1)} %get-tuple-element.100), channel_id=1, source_target_pairs={{0,64},{32,96},{1,65},{33,97},{2,66},{34,98},{3,67},{35,99},{4,68}... | collective-permute-start | bytes 442376 | tf_op jit(solution)/shard_map/ppermute | solution.py:28
  107.8 2.7 %collective-permute-done.18 = bf16[2,32,1152]{2,1,0:T(8,128)(2,1)S(1)} collective-permute-done((bf16[2,32,1152]{2,1,0:T(8,128)(2,1)S(1)}, bf16[2,32,1152]{2,1,0:T(8,128)(2,1)S(1)}, u32[]{:S(2)}, u32[]{:S(2)}) %collective-permute-start.18) | collective-permute-done | bytes 147488 | tf_op jit(solution)/shard_map/ppermute | solution.py:28
  114.4 2.0 collective-permute-done.19
  116.4 2.8 %collective-permute-done.20 = bf16[2,32,1152]{2,1,0:T(8,128)(2,1)S(1)} collective-permute-done((bf16[2,32,1152]{2,1,0:T(8,128)(2,1)S(1)}, bf16[2,32,1152]{2,1,0:T(8,128)(2,1)S(1)}, u32[]{:S(2)}, u32[]{:S(2)}) %collective-permute-start.20) | collective-permute-done | bytes 147488 | tf_op jit(solution)/shard_map/ppermute | solution.py:28
  119.2 4.3 %collective-permute-done.21 = bf16[2,32,1152]{2,1,0:T(8,128)(2,1)S(1)} collective-permute-done((bf16[2,32,1152]{2,1,0:T(8,128)(2,1)S(1)}, bf16[2,32,1152]{2,1,0:T(8,128)(2,1)S(1)}, u32[]{:S(2)}, u32[]{:S(2)}) %collective-permute-start.21) | collective-permute-done | bytes 147488 | tf_op jit(solution)/shard_map/ppermute | solution.py:28
  123.8 3.0 %collective-permute-start.29 = (bf16[4,32,1152]{2,1,0:T(8,128)(2,1)S(1)}, bf16[4,32,1152]{2,1,0:T(8,128)(2,1)S(1)}, u32[]{:S(2)}, u32[]{:S(2)}) collective-permute-start(bf16[4,32,1152]{2,1,0:T(8,128)(2,1)S(1)} %get-tuple-element.96), channel_id=1, source_target_pairs={{0,16},{8,24},{16,0},{24,8},{1,17},{9,25},{17,1},{25,9},{2,18},{10... | collective-permute-start | bytes 884744 | tf_op jit(solution)/shard_map/ppermute | solution.py:22
  126.8 2.3 %collective-permute-start.22 = (bf16[4,32,1152]{2,1,0:T(8,128)(2,1)S(1)}, bf16[4,32,1152]{2,1,0:T(8,128)(2,1)S(1)}, u32[]{:S(2)}, u32[]{:S(2)}) collective-permute-start(bf16[4,32,1152]{2,1,0:T(8,128)(2,1)S(1)} %get-tuple-element.97), channel_id=1, source_target_pairs={{0,6},{2,0},{4,2},{6,4},{1,7},{3,1},{5,3},{7,5},{8,14},{10,8},{12,... | collective-permute-start | bytes 884744 | tf_op jit(solution)/shard_map/ppermute | solution.py:22
  131.0 7.3 %collective-permute-done.30 = bf16[4,32,1152]{2,1,0:T(8,128)(2,1)S(1)} collective-permute-done((bf16[4,32,1152]{2,1,0:T(8,128)(2,1)S(1)}, bf16[4,32,1152]{2,1,0:T(8,128)(2,1)S(1)}, u32[]{:S(2)}, u32[]{:S(2)}) %collective-permute-start.30) | collective-permute-done | bytes 294944 | tf_op jit(solution)/shard_map/ppermute | solution.py:22
  138.4 3.7 %collective-permute-start.31 = (bf16[4,128,1152]{2,1,0:T(8,128)(2,1)S(1)}, bf16[4,128,1152]{2,1,0:T(8,128)(2,1)S(1)}, u32[]{:S(2)}, u32[]{:S(2)}) collective-permute-start(bf16[4,128,1152]{2,1,0:T(8,128)(2,1)S(1)} %pad_maximum_fusion.2.refs_3_), channel_id=1, source_target_pairs={{0,6},{2,0},{4,2},{6,4},{1,7},{3,1},{5,3},{7,5},{8,14},{10,8},{12,... | collective-permute-start | bytes 3538952 | tf_op jit(solution)/shard_map/ppermute | solution.py:22
  142.4 1.9 collective-permute-start.26
  144.3 9.6 %collective-permute-start.25 = (bf16[512,1152]{0,1:T(8,128)(2,1)S(1)}, bf16[512,1152]{0,1:T(8,128)(2,1)S(1)}, u32[]{:S(2)}, u32[]{:S(2)}) collective-permute-start(bf16[512,1152]{0,1:T(8,128)(2,1)S(1)} %copy-done.29), channel_id=1, source_target_pairs={{0,1},{1,0},{2,3},{3,2},{4,5},{5,4},{6,7},{7,6},{8,9},{9,8},{10,11... | collective-permute-start | bytes 3538952 | tf_op jit(solution)/shard_map/ppermute | solution.py:32
  153.9 12.3 %collective-permute-done.31.refs_4_ = bf16[4,128,1152]{2,1,0:T(8,128)(2,1)S(1)} collective-permute-done((bf16[4,128,1152]{2,1,0:T(8,128)(2,1)S(1)}, bf16[4,128,1152]{2,1,0:T(8,128)(2,1)S(1)}, u32[]{:S(2)}, u32[]{:S(2)}) %collective-permute-start.31) | collective-permute-done | bytes 1179680 | tf_op jit(solution)/shard_map/ppermute | solution.py:22
  166.3 2.7 %collective-permute-start.35 = (bf16[4,64,1152]{2,1,0:T(8,128)(2,1)S(1)}, bf16[4,64,1152]{2,1,0:T(8,128)(2,1)S(1)}, u32[]{:S(2)}, u32[]{:S(2)}) collective-permute-start(bf16[4,64,1152]{2,1,0:T(8,128)(2,1)S(1)} %slice.164), channel_id=1, source_target_pairs={{0,6},{2,0},{4,2},{6,4},{1,7},{3,1},{5,3},{7,5},{8,14},{10,8},{12,... | collective-permute-start | bytes 1769480 | tf_op jit(solution)/shard_map/ppermute | solution.py:22
  169.7 2.7 %collective-permute-start.33 = (bf16[4,64,1152]{2,1,0:T(8,128)(2,1)S(1)}, bf16[4,64,1152]{2,1,0:T(8,128)(2,1)S(1)}, u32[]{:S(2)}, u32[]{:S(2)}) collective-permute-start(bf16[4,64,1152]{2,1,0:T(8,128)(2,1)S(1)} %slice.162), channel_id=1, source_target_pairs={{0,24},{8,0},{16,8},{24,16},{1,25},{9,1},{17,9},{25,17},{2,26},{10... | collective-permute-start | bytes 1769480 | tf_op jit(solution)/shard_map/ppermute | solution.py:22
  172.6 6.2 %shard_map.98 = (f32[768,512]{1,0:T(8,128)S(1)}, f32[1,1152]{1,0:T(1,128)S(1)}) custom-call(s32[4]{0:T(128)S(1)} %copy-done.26, bf16[4,512,1152]{2,1,0:T(8,128)(2,1)S(1)} %bitcast.74, bf16[4,128,1152]{2,1,0:T(8,128)(2,1)S(1)} %pad_maximum_fusion.1.refs_0_, bf16[4,128,1152]{2,1,0:T(8,128)(2,1)S(1)} %collective-permute-done.26.refs_1_, ...), custom_call_target="tpu_custom_call" | custom-call | flops 3623878656 | bytes 14680064 | tf_op jit(solution)/shard_map/pallas_call | solution.py:54
  179.2 3.9 %collective-permute-done.36.refs_9_.refs_3_ = bf16[4,64,1152]{2,1,0:T(8,128)(2,1)S(1)} collective-permute-done((bf16[4,64,1152]{2,1,0:T(8,128)(2,1)S(1)}, bf16[4,64,1152]{2,1,0:T(8,128)(2,1)S(1)}, u32[]{:S(2)}, u32[]{:S(2)}) %collective-permute-start.36) | collective-permute-done | bytes 589856 | tf_op jit(solution)/shard_map/ppermute | solution.py:22
  183.1 2.8 %collective-permute-done.34.refs_7_.refs_1_ = bf16[4,64,1152]{2,1,0:T(8,128)(2,1)S(1)} collective-permute-done((bf16[4,64,1152]{2,1,0:T(8,128)(2,1)S(1)}, bf16[4,64,1152]{2,1,0:T(8,128)(2,1)S(1)}, u32[]{:S(2)}, u32[]{:S(2)}) %collective-permute-start.34) | collective-permute-done | bytes 589856 | tf_op jit(solution)/shard_map/ppermute | solution.py:22
  185.8 4.1 %shard_map.99 = (f32[512,512]{1,0:T(8,128)S(1)}, f32[512,512]{1,0:T(8,128)}, f32[1,1152]{1,0:T(1,128)S(1)}) custom-call(s32[4]{0:T(128)S(1)} %copy-done.26, bf16[4,512,1152]{2,1,0:T(8,128)(2,1)S(1)} %bitcast.74, f32[768,512]{1,0:T(8,128)S(1)} %get-tuple-element.76.near_ref, f32[1,1152]{1,0:T(1,128)S(1)} %get-tuple-element.77.near_sum_ref, ...), custom_call_target="tpu_custom_call" | custom-call | flops 1207959552 | bytes 10485760 | tf_op jit(solution)/shard_map/pallas_call | solution.py:54
  191.0 3.7 %collective-permute-start.38 = (f32[512,512]{1,0:T(8,128)}, f32[512,512]{1,0:T(8,128)}, u32[]{:S(2)}, u32[]{:S(2)}) collective-permute-start(f32[512,512]{1,0:T(8,128)} %get-tuple-element.84), channel_id=1, source_target_pairs={{0,1},{1,0},{2,3},{3,2},{4,5},{5,4},{6,7},{7,6},{8,9},{9,8},{10,11... | collective-permute-start | bytes 3145736 | tf_op jit(solution)/shard_map/ppermute | solution.py:32
  194.6 2.3 %collective-permute-done.37 = f32[1,1152]{1,0:T(1,128)} collective-permute-done((f32[1,1152]{1,0:T(1,128)S(1)}, f32[1,1152]{1,0:T(1,128)}, u32[]{:S(2)}, u32[]{:S(2)}) %collective-permute-start.37) | collective-permute-done | bytes 4640 | tf_op jit(solution)/shard_map/ppermute | solution.py:32
  197.3 2.8 %convert_reduce_fusion = (f32[512]{0:T(512)S(1)}, bf16[512,512]{1,0:T(8,128)(2,1)S(1)}) fusion(f32[512,512]{1,0:T(8,128)} %get-tuple-element.85, f32[512,512]{1,0:T(8,128)} %copy-done.4, f32[512,512]{1,0:T(8,128)} %collective-permute-done.38), kind=kLoop, calls=%fused_computation.22 | loop fusion | flops 6028800 | bytes 3672064 | tf_op jit(solution)/shard_map/reduce_sum | solution.py:438
  205.7 8.5 %shard_map.97 = (f32[4,512,1152]{2,1,0:T(8,128)}, f32[1,1152]{1,0:T(1,128)}) custom-call(s32[4]{0:T(128)S(1)} %copy-done.26, bf16[512,512]{1,0:T(8,128)(2,1)S(1)} %copy-done.14, bf16[512,512]{1,0:T(8,128)(2,1)S(1)} %copy-done.16, bf16[4,128,1152]{2,1,0:T(8,128)(2,1)S(1)} %pad_maximum_fusion.1.refs_0_, bf16[4,128,1152]{2,1,0:T(8,128)(2,1)S(1)} %copy-done.22, ...), custom_call_target="tpu_custom_call" | custom-call | flops 4831838208 | bytes 20971520 | tf_op jit(solution)/shard_map/pallas_call | solution.py:54
  216.9 4.3 %shard_map.100 = f32[1152,512]{1,0:T(8,128)} custom-call(s32[4]{0:T(128)S(1)} %copy-done.26, bf16[1152,512]{1,0:T(8,128)(2,1)S(1)} %bitcast.75, bf16[1152,512]{1,0:T(8,128)(2,1)S(1)} %bitcast.76, bf16[512,512]{1,0:T(8,128)(2,1)S(1)} %get-tuple-element.87.grad_ref, bf16[512,512]{1,0:T(8,128)(2,1)S(1)} %collective-permute-done.39.other_grad_ref), custom_call_target="tpu_custom_call" | custom-call | flops 1207959552 | bytes 6291456 | tf_op jit(solution)/shard_map/pallas_call | solution.py:54
  (150 shorter events, 36.0 us)
Async XLA Ops:
  7.6 4.2 %collective-permute-start = (bf16[512,512]{1,0:T(8,128)(2,1)}, bf16[512,512]{1,0:T(8,128)(2,1)S(1)}, u32[]{:S(2)}, u32[]{:S(2)}) collective-permute-start(bf16[512,512]{1,0:T(8,128)(2,1)} %get-tuple-element.46), channel_id=1, source_target_pairs={{0,1},{1,0},{2,3},{3,2},{4,5},{5,4},{6,7},{7,6},{8,9},{9,8},{10,11... | collective-permute-start | bytes 1572872 | tf_op jit(solution)/shard_map/ppermute | solution.py:32
  11.9 10.9 %copy-start.31 = (bf16[1,512,144]{1,2,0:T(8,128)(2,1)S(1)}, bf16[1,512,144]{1,2,0:T(8,128)(2,1)}, u32[]{:S(2)}) copy-start(bf16[1,512,144]{1,2,0:T(8,128)(2,1)} %param.7) | copy-start | bytes 442372
  16.1 21.6 %collective-permute-start.1 = (bf16[4,64,1152]{2,1,0:T(8,128)(2,1)}, bf16[4,64,1152]{2,1,0:T(8,128)(2,1)S(1)}, u32[]{:S(2)}, u32[]{:S(2)}) collective-permute-start(bf16[4,64,1152]{2,1,0:T(8,128)(2,1)} %get-tuple-element.53), channel_id=1, source_target_pairs={{0,8},{8,16},{16,24},{24,0},{1,9},{9,17},{17,25},{25,1},{2,10},{10... | collective-permute-start | bytes 1769480 | tf_op jit(solution)/shard_map/ppermute | solution.py:22
  17.5 20.2 %collective-permute-start.2 = (bf16[4,64,1152]{2,1,0:T(8,128)(2,1)}, bf16[4,64,1152]{2,1,0:T(8,128)(2,1)S(1)}, u32[]{:S(2)}, u32[]{:S(2)}) collective-permute-start(bf16[4,64,1152]{2,1,0:T(8,128)(2,1)} %get-tuple-element.54), channel_id=1, source_target_pairs={{0,24},{8,0},{16,8},{24,16},{1,25},{9,1},{17,9},{25,17},{2,26},{10... | collective-permute-start | bytes 1769480 | tf_op jit(solution)/shard_map/ppermute | solution.py:22
  18.9 18.9 %collective-permute-start.3 = (bf16[4,64,1152]{2,1,0:T(8,128)(2,1)}, bf16[4,64,1152]{2,1,0:T(8,128)(2,1)S(1)}, u32[]{:S(2)}, u32[]{:S(2)}) collective-permute-start(bf16[4,64,1152]{2,1,0:T(8,128)(2,1)} %get-tuple-element.55), channel_id=1, source_target_pairs={{0,2},{2,4},{4,6},{6,0},{1,3},{3,5},{5,7},{7,1},{8,10},{10,12},{12... | collective-permute-start | bytes 1769480 | tf_op jit(solution)/shard_map/ppermute | solution.py:22
  20.6 17.2 %collective-permute-start.4 = (bf16[4,64,1152]{2,1,0:T(8,128)(2,1)}, bf16[4,64,1152]{2,1,0:T(8,128)(2,1)S(1)}, u32[]{:S(2)}, u32[]{:S(2)}) collective-permute-start(bf16[4,64,1152]{2,1,0:T(8,128)(2,1)} %get-tuple-element.56), channel_id=1, source_target_pairs={{0,6},{2,0},{4,2},{6,4},{1,7},{3,1},{5,3},{7,5},{8,14},{10,8},{12,... | collective-permute-start | bytes 1769480 | tf_op jit(solution)/shard_map/ppermute | solution.py:22
  23.6 9.0 %copy-start.32 = (f32[1,144]{1,0:T(1,128)S(1)}, f32[1,144]{1,0:T(1,128)}, u32[]{:S(2)}) copy-start(f32[1,144]{1,0:T(1,128)} %param.11) | copy-start | bytes 1732
  33.5 19.3 %all-to-all-start = ((f32[16,32,144]{2,1,0:T(8,128)}), f32[16,32,144]{2,1,0:T(8,128)}, u32[]{:S(2)}, u32[]{:S(2)}) async-start(f32[16,32,144]{2,1,0:T(8,128)} %convert_subtract_fusion), calls=%async_computation | async-start | bytes 1048576 | tf_op jit(solution)/shard_map/all_to_all | solution.py:384
  41.3 31.9 %collective-permute-start.10 = (bf16[4,128,1152]{2,1,0:T(8,128)(2,1)}, bf16[4,128,1152]{2,1,0:T(8,128)(2,1)}, u32[]{:S(2)}, u32[]{:S(2)}) collective-permute-start(bf16[4,128,1152]{2,1,0:T(8,128)(2,1)} %get-tuple-element.60), channel_id=1, source_target_pairs={{0,2},{2,4},{4,6},{6,0},{1,3},{3,5},{5,7},{7,1},{8,10},{10,12},{12... | collective-permute-start | bytes 3538952 | tf_op jit(solution)/shard_map/ppermute | solution.py:22
  42.5 30.7 %collective-permute-start.11 = (bf16[4,128,1152]{2,1,0:T(8,128)(2,1)}, bf16[4,128,1152]{2,1,0:T(8,128)(2,1)}, u32[]{:S(2)}, u32[]{:S(2)}) collective-permute-start(bf16[4,128,1152]{2,1,0:T(8,128)(2,1)} %get-tuple-element.61), channel_id=1, source_target_pairs={{0,6},{2,0},{4,2},{6,4},{1,7},{3,1},{5,3},{7,5},{8,14},{10,8},{12,... | collective-permute-start | bytes 3538952 | tf_op jit(solution)/shard_map/ppermute | solution.py:22
  44.0 35.3 %collective-permute-start.5 = (bf16[4,128,1152]{2,1,0:T(8,128)(2,1)S(1)}, bf16[4,128,1152]{2,1,0:T(8,128)(2,1)}, u32[]{:S(2)}, u32[]{:S(2)}) collective-permute-start(bf16[4,128,1152]{2,1,0:T(8,128)(2,1)S(1)} %get-tuple-element.57), channel_id=1, source_target_pairs={{0,8},{8,16},{16,24},{24,0},{1,9},{9,17},{17,25},{25,1},{2,10},{10... | collective-permute-start | bytes 3538952 | tf_op jit(solution)/shard_map/ppermute | solution.py:22
  45.2 34.1 %collective-permute-start.6 = (bf16[4,128,1152]{2,1,0:T(8,128)(2,1)}, bf16[4,128,1152]{2,1,0:T(8,128)(2,1)}, u32[]{:S(2)}, u32[]{:S(2)}) collective-permute-start(bf16[4,128,1152]{2,1,0:T(8,128)(2,1)} %get-tuple-element.58), channel_id=1, source_target_pairs={{0,24},{8,0},{16,8},{24,16},{1,25},{9,1},{17,9},{25,17},{2,26},{10... | collective-permute-start | bytes 3538952 | tf_op jit(solution)/shard_map/ppermute | solution.py:22
  54.2 3.4 %collective-permute-start.14 = (f32[32,1152]{1,0:T(8,128)S(1)}, f32[32,1152]{1,0:T(8,128)S(1)}, u32[]{:S(2)}, u32[]{:S(2)}) collective-permute-start(f32[32,1152]{1,0:T(8,128)S(1)} %reshape.39), channel_id=1, source_target_pairs={{0,1},{1,0},{2,3},{3,2},{4,5},{5,4},{6,7},{7,6},{8,9},{9,8},{10,11... | collective-permute-start | bytes 442376 | tf_op jit(solution)/shard_map/ppermute | solution.py:32
  75.6 7.6 %collective-permute-start.15 = (bf16[4,32,1152]{2,1,0:T(8,128)(2,1)S(1)}, bf16[4,32,1152]{2,1,0:T(8,128)(2,1)S(1)}, u32[]{:S(2)}, u32[]{:S(2)}) collective-permute-start(bf16[4,32,1152]{2,1,0:T(8,128)(2,1)S(1)} %get-tuple-element.89), channel_id=1, source_target_pairs={{0,24},{8,0},{16,8},{24,16},{1,25},{9,1},{17,9},{25,17},{2,26},{10... | collective-permute-start | bytes 884744 | tf_op jit(solution)/shard_map/ppermute | solution.py:22
  77.2 8.9 %collective-permute-start.12 = (bf16[4,32,1152]{2,1,0:T(8,128)(2,1)S(1)}, bf16[4,32,1152]{2,1,0:T(8,128)(2,1)S(1)}, u32[]{:S(2)}, u32[]{:S(2)}) collective-permute-start(bf16[4,32,1152]{2,1,0:T(8,128)(2,1)S(1)} %get-tuple-element.88), channel_id=1, source_target_pairs={{0,8},{8,16},{16,24},{24,0},{1,9},{9,17},{17,25},{25,1},{2,10},{10... | collective-permute-start | bytes 884744 | tf_op jit(solution)/shard_map/ppermute | solution.py:22
  77.2 14.5 %collective-permute-start.13 = (bf16[4,32,1152]{2,1,0:T(8,128)(2,1)S(1)}, bf16[4,32,1152]{2,1,0:T(8,128)(2,1)S(1)}, u32[]{:S(2)}, u32[]{:S(2)}) collective-permute-start(bf16[4,32,1152]{2,1,0:T(8,128)(2,1)S(1)} %get-tuple-element.90), channel_id=1, source_target_pairs={{0,16},{8,24},{16,0},{24,8},{1,17},{9,25},{17,1},{25,9},{2,18},{10... | collective-permute-start | bytes 884744 | tf_op jit(solution)/shard_map/ppermute | solution.py:22
  81.1 12.1 %collective-permute-start.7 = (bf16[4,32,1152]{2,1,0:T(8,128)(2,1)S(1)}, bf16[4,32,1152]{2,1,0:T(8,128)(2,1)S(1)}, u32[]{:S(2)}, u32[]{:S(2)}) collective-permute-start(bf16[4,32,1152]{2,1,0:T(8,128)(2,1)S(1)} %get-tuple-element.91), channel_id=1, source_target_pairs={{0,2},{2,4},{4,6},{6,0},{1,3},{3,5},{5,7},{7,1},{8,10},{10,12},{12... | collective-permute-start | bytes 884744 | tf_op jit(solution)/shard_map/ppermute | solution.py:22
  81.2 12.1 %collective-permute-start.8 = (bf16[4,32,1152]{2,1,0:T(8,128)(2,1)S(1)}, bf16[4,32,1152]{2,1,0:T(8,128)(2,1)S(1)}, u32[]{:S(2)}, u32[]{:S(2)}) collective-permute-start(bf16[4,32,1152]{2,1,0:T(8,128)(2,1)S(1)} %get-tuple-element.93), channel_id=1, source_target_pairs={{0,4},{2,6},{4,0},{6,2},{1,5},{3,7},{5,1},{7,3},{8,12},{10,14},{12... | collective-permute-start | bytes 884744 | tf_op jit(solution)/shard_map/ppermute | solution.py:22
  83.2 12.9 %collective-permute-start.9 = (bf16[4,32,1152]{2,1,0:T(8,128)(2,1)S(1)}, bf16[4,32,1152]{2,1,0:T(8,128)(2,1)S(1)}, u32[]{:S(2)}, u32[]{:S(2)}) collective-permute-start(bf16[4,32,1152]{2,1,0:T(8,128)(2,1)S(1)} %get-tuple-element.92), channel_id=1, source_target_pairs={{0,6},{2,0},{4,2},{6,4},{1,7},{3,1},{5,3},{7,5},{8,14},{10,8},{12,... | collective-permute-start | bytes 884744 | tf_op jit(solution)/shard_map/ppermute | solution.py:22
  97.4 75.2 %slice-start = ((s8[4718592]{0:T(1024)(128)(4,1)}), s8[4194304]{0:T(1024)(128)(4,1)S(1)}, s32[]{:S(2)}) async-start(s8[4718592]{0:T(1024)(128)(4,1)} %bitcast.73), calls=%async_computation.1 | async-start | bytes 8388608
  97.5 9.3 %collective-permute-start.16 = (bf16[2,32,1152]{2,1,0:T(8,128)(2,1)S(1)}, bf16[2,32,1152]{2,1,0:T(8,128)(2,1)S(1)}, u32[]{:S(2)}, u32[]{:S(2)}) collective-permute-start(bf16[2,32,1152]{2,1,0:T(8,128)(2,1)S(1)} %get-tuple-element.98), channel_id=1, source_target_pairs={{0,32},{32,64},{64,96},{1,33},{33,65},{65,97},{2,34},{34,66},{66,9... | collective-permute-start | bytes 442376 | tf_op jit(solution)/shard_map/ppermute | solution.py:28
  100.9 6.8 %collective-permute-start.17 = (bf16[2,32,1152]{2,1,0:T(8,128)(2,1)S(1)}, bf16[2,32,1152]{2,1,0:T(8,128)(2,1)S(1)}, u32[]{:S(2)}, u32[]{:S(2)}) collective-permute-start(bf16[2,32,1152]{2,1,0:T(8,128)(2,1)S(1)} %get-tuple-element.100), channel_id=1, source_target_pairs={{0,64},{32,96},{1,65},{33,97},{2,66},{34,98},{3,67},{35,99},{4,68}... | collective-permute-start | bytes 442376 | tf_op jit(solution)/shard_map/ppermute | solution.py:28
  105.5 4.9 %collective-permute-start.18 = (bf16[2,32,1152]{2,1,0:T(8,128)(2,1)S(1)}, bf16[2,32,1152]{2,1,0:T(8,128)(2,1)S(1)}, u32[]{:S(2)}, u32[]{:S(2)}) collective-permute-start(bf16[2,32,1152]{2,1,0:T(8,128)(2,1)S(1)} %get-tuple-element.99), channel_id=1, source_target_pairs={{0,96},{1,97},{2,98},{3,99},{4,100},{5,101},{6,102},{7,103},{8,104... | collective-permute-start | bytes 442376 | tf_op jit(solution)/shard_map/ppermute | solution.py:28
  110.5 5.9 %collective-permute-start.19 = (bf16[2,32,1152]{2,1,0:T(8,128)(2,1)S(1)}, bf16[2,32,1152]{2,1,0:T(8,128)(2,1)S(1)}, u32[]{:S(2)}, u32[]{:S(2)}) collective-permute-start(bf16[2,32,1152]{2,1,0:T(8,128)(2,1)S(1)} %fusion.17), channel_id=1, source_target_pairs={{32,0},{64,32},{96,64},{33,1},{65,33},{97,65},{34,2},{66,34},{98,6... | collective-permute-start | bytes 442376 | tf_op jit(solution)/shard_map/ppermute | solution.py:28
  111.8 7.4 %collective-permute-start.20 = (bf16[2,32,1152]{2,1,0:T(8,128)(2,1)S(1)}, bf16[2,32,1152]{2,1,0:T(8,128)(2,1)S(1)}, u32[]{:S(2)}, u32[]{:S(2)}) collective-permute-start(bf16[2,32,1152]{2,1,0:T(8,128)(2,1)S(1)} %fusion.17), channel_id=1, source_target_pairs={{64,0},{96,32},{65,1},{97,33},{66,2},{98,34},{67,3},{99,35},{68,4}... | collective-permute-start | bytes 442376 | tf_op jit(solution)/shard_map/ppermute | solution.py:28
  113.1 10.4 %collective-permute-start.21 = (bf16[2,32,1152]{2,1,0:T(8,128)(2,1)S(1)}, bf16[2,32,1152]{2,1,0:T(8,128)(2,1)S(1)}, u32[]{:S(2)}, u32[]{:S(2)}) collective-permute-start(bf16[2,32,1152]{2,1,0:T(8,128)(2,1)S(1)} %fusion.17), channel_id=1, source_target_pairs={{96,0},{97,1},{98,2},{99,3},{100,4},{101,5},{102,6},{103,7},{104,8... | collective-permute-start | bytes 442376 | tf_op jit(solution)/shard_map/ppermute | solution.py:28
  123.7 6.3 %collective-permute-start.28 = (bf16[4,32,1152]{2,1,0:T(8,128)(2,1)S(1)}, bf16[4,32,1152]{2,1,0:T(8,128)(2,1)S(1)}, u32[]{:S(2)}, u32[]{:S(2)}) collective-permute-start(bf16[4,32,1152]{2,1,0:T(8,128)(2,1)S(1)} %get-tuple-element.96), channel_id=1, source_target_pairs={{0,24},{8,0},{16,8},{24,16},{1,25},{9,1},{17,9},{25,17},{2,26},{10... | collective-permute-start | bytes 884744 | tf_op jit(solution)/shard_map/ppermute | solution.py:22
  123.8 7.2 %collective-permute-start.29 = (bf16[4,32,1152]{2,1,0:T(8,128)(2,1)S(1)}, bf16[4,32,1152]{2,1,0:T(8,128)(2,1)S(1)}, u32[]{:S(2)}, u32[]{:S(2)}) collective-permute-start(bf16[4,32,1152]{2,1,0:T(8,128)(2,1)S(1)} %get-tuple-element.96), channel_id=1, source_target_pairs={{0,16},{8,24},{16,0},{24,8},{1,17},{9,25},{17,1},{25,9},{2,18},{10... | collective-permute-start | bytes 884744 | tf_op jit(solution)/shard_map/ppermute | solution.py:22
  126.8 11.5 %collective-permute-start.30 = (bf16[4,32,1152]{2,1,0:T(8,128)(2,1)S(1)}, bf16[4,32,1152]{2,1,0:T(8,128)(2,1)S(1)}, u32[]{:S(2)}, u32[]{:S(2)}) collective-permute-start(bf16[4,32,1152]{2,1,0:T(8,128)(2,1)S(1)} %get-tuple-element.96), channel_id=1, source_target_pairs={{0,8},{8,16},{16,24},{24,0},{1,9},{9,17},{17,25},{25,1},{2,10},{10... | collective-permute-start | bytes 884744 | tf_op jit(solution)/shard_map/ppermute | solution.py:22
  126.8 45.8 %slice-start.1 = ((s8[4718592]{0:T(1024)(128)(4,1)}), s8[524288]{0:T(1024)(128)(4,1)S(1)}, s32[]{:S(2)}) async-start(s8[4718592]{0:T(1024)(128)(4,1)} %bitcast.73), calls=%async_computation.2 | async-start | bytes 1048576
  126.8 15.3 %collective-permute-start.22 = (bf16[4,32,1152]{2,1,0:T(8,128)(2,1)S(1)}, bf16[4,32,1152]{2,1,0:T(8,128)(2,1)S(1)}, u32[]{:S(2)}, u32[]{:S(2)}) collective-permute-start(bf16[4,32,1152]{2,1,0:T(8,128)(2,1)S(1)} %get-tuple-element.97), channel_id=1, source_target_pairs={{0,6},{2,0},{4,2},{6,4},{1,7},{3,1},{5,3},{7,5},{8,14},{10,8},{12,... | collective-permute-start | bytes 884744 | tf_op jit(solution)/shard_map/ppermute | solution.py:22
  129.1 13.0 %collective-permute-start.23 = (bf16[4,32,1152]{2,1,0:T(8,128)(2,1)S(1)}, bf16[4,32,1152]{2,1,0:T(8,128)(2,1)S(1)}, u32[]{:S(2)}, u32[]{:S(2)}) collective-permute-start(bf16[4,32,1152]{2,1,0:T(8,128)(2,1)S(1)} %get-tuple-element.97), channel_id=1, source_target_pairs={{0,4},{2,6},{4,0},{6,2},{1,5},{3,7},{5,1},{7,3},{8,12},{10,14},{12... | collective-permute-start | bytes 884744 | tf_op jit(solution)/shard_map/ppermute | solution.py:22
  130.0 12.3 %collective-permute-start.24 = (bf16[4,32,1152]{2,1,0:T(8,128)(2,1)S(1)}, bf16[4,32,1152]{2,1,0:T(8,128)(2,1)S(1)}, u32[]{:S(2)}, u32[]{:S(2)}) collective-permute-start(bf16[4,32,1152]{2,1,0:T(8,128)(2,1)S(1)} %get-tuple-element.97), channel_id=1, source_target_pairs={{0,2},{2,4},{4,6},{6,0},{1,3},{3,5},{5,7},{7,1},{8,10},{10,12},{12... | collective-permute-start | bytes 884744 | tf_op jit(solution)/shard_map/ppermute | solution.py:22
  138.4 27.8 %collective-permute-start.31 = (bf16[4,128,1152]{2,1,0:T(8,128)(2,1)S(1)}, bf16[4,128,1152]{2,1,0:T(8,128)(2,1)S(1)}, u32[]{:S(2)}, u32[]{:S(2)}) collective-permute-start(bf16[4,128,1152]{2,1,0:T(8,128)(2,1)S(1)} %pad_maximum_fusion.2.refs_3_), channel_id=1, source_target_pairs={{0,6},{2,0},{4,2},{6,4},{1,7},{3,1},{5,3},{7,5},{8,14},{10,8},{12,... | collective-permute-start | bytes 3538952 | tf_op jit(solution)/shard_map/ppermute | solution.py:22
  142.1 27.4 %collective-permute-start.32 = (bf16[4,128,1152]{2,1,0:T(8,128)(2,1)S(1)}, bf16[4,128,1152]{2,1,0:T(8,128)(2,1)S(1)}, u32[]{:S(2)}, u32[]{:S(2)}) collective-permute-start(bf16[4,128,1152]{2,1,0:T(8,128)(2,1)S(1)} %pad_maximum_fusion.2.refs_3_), channel_id=1, source_target_pairs={{0,2},{2,4},{4,6},{6,0},{1,3},{3,5},{5,7},{7,1},{8,10},{10,12},{12... | collective-permute-start | bytes 3538952 | tf_op jit(solution)/shard_map/ppermute | solution.py:22
  142.4 27.2 %collective-permute-start.26 = (bf16[4,128,1152]{2,1,0:T(8,128)(2,1)S(1)}, bf16[4,128,1152]{2,1,0:T(8,128)(2,1)S(1)}, u32[]{:S(2)}, u32[]{:S(2)}) collective-permute-start(bf16[4,128,1152]{2,1,0:T(8,128)(2,1)S(1)} %pad_maximum_fusion.1.refs_0_), channel_id=1, source_target_pairs={{0,24},{8,0},{16,8},{24,16},{1,25},{9,1},{17,9},{25,17},{2,26},{10... | collective-permute-start | bytes 3538952 | tf_op jit(solution)/shard_map/ppermute | solution.py:22
  144.3 28.1 %collective-permute-start.27 = (bf16[4,128,1152]{2,1,0:T(8,128)(2,1)S(1)}, bf16[4,128,1152]{2,1,0:T(8,128)(2,1)S(1)}, u32[]{:S(2)}, u32[]{:S(2)}) collective-permute-start(bf16[4,128,1152]{2,1,0:T(8,128)(2,1)S(1)} %pad_maximum_fusion.1.refs_0_), channel_id=1, source_target_pairs={{0,8},{8,16},{16,24},{24,0},{1,9},{9,17},{17,25},{25,1},{2,10},{10... | collective-permute-start | bytes 3538952 | tf_op jit(solution)/shard_map/ppermute | solution.py:22
  144.3 28.2 %collective-permute-start.25 = (bf16[512,1152]{0,1:T(8,128)(2,1)S(1)}, bf16[512,1152]{0,1:T(8,128)(2,1)S(1)}, u32[]{:S(2)}, u32[]{:S(2)}) collective-permute-start(bf16[512,1152]{0,1:T(8,128)(2,1)S(1)} %copy-done.29), channel_id=1, source_target_pairs={{0,1},{1,0},{2,3},{3,2},{4,5},{5,4},{6,7},{7,6},{8,9},{9,8},{10,11... | collective-permute-start | bytes 3538952 | tf_op jit(solution)/shard_map/ppermute | solution.py:32
  166.3 12.9 %collective-permute-start.35 = (bf16[4,64,1152]{2,1,0:T(8,128)(2,1)S(1)}, bf16[4,64,1152]{2,1,0:T(8,128)(2,1)S(1)}, u32[]{:S(2)}, u32[]{:S(2)}) collective-permute-start(bf16[4,64,1152]{2,1,0:T(8,128)(2,1)S(1)} %slice.164), channel_id=1, source_target_pairs={{0,6},{2,0},{4,2},{6,4},{1,7},{3,1},{5,3},{7,5},{8,14},{10,8},{12,... | collective-permute-start | bytes 1769480 | tf_op jit(solution)/shard_map/ppermute | solution.py:22
  169.6 13.5 %collective-permute-start.36 = (bf16[4,64,1152]{2,1,0:T(8,128)(2,1)S(1)}, bf16[4,64,1152]{2,1,0:T(8,128)(2,1)S(1)}, u32[]{:S(2)}, u32[]{:S(2)}) collective-permute-start(bf16[4,64,1152]{2,1,0:T(8,128)(2,1)S(1)} %slice.165), channel_id=1, source_target_pairs={{0,2},{2,4},{4,6},{6,0},{1,3},{3,5},{5,7},{7,1},{8,10},{10,12},{12... | collective-permute-start | bytes 1769480 | tf_op jit(solution)/shard_map/ppermute | solution.py:22
  169.7 13.3 %collective-permute-start.33 = (bf16[4,64,1152]{2,1,0:T(8,128)(2,1)S(1)}, bf16[4,64,1152]{2,1,0:T(8,128)(2,1)S(1)}, u32[]{:S(2)}, u32[]{:S(2)}) collective-permute-start(bf16[4,64,1152]{2,1,0:T(8,128)(2,1)S(1)} %slice.162), channel_id=1, source_target_pairs={{0,24},{8,0},{16,8},{24,16},{1,25},{9,1},{17,9},{25,17},{2,26},{10... | collective-permute-start | bytes 1769480 | tf_op jit(solution)/shard_map/ppermute | solution.py:22
  172.5 13.4 %collective-permute-start.34 = (bf16[4,64,1152]{2,1,0:T(8,128)(2,1)S(1)}, bf16[4,64,1152]{2,1,0:T(8,128)(2,1)S(1)}, u32[]{:S(2)}, u32[]{:S(2)}) collective-permute-start(bf16[4,64,1152]{2,1,0:T(8,128)(2,1)S(1)} %slice.163), channel_id=1, source_target_pairs={{0,8},{8,16},{16,24},{24,0},{1,9},{9,17},{17,25},{25,1},{2,10},{10... | collective-permute-start | bytes 1769480 | tf_op jit(solution)/shard_map/ppermute | solution.py:22
  179.1 10.8 %copy-start.5 = (bf16[4,64,1152]{2,1,0:T(8,128)(2,1)}, bf16[4,64,1152]{2,1,0:T(8,128)(2,1)S(1)}, u32[]{:S(2)}) copy-start(bf16[4,64,1152]{2,1,0:T(8,128)(2,1)S(1)} %collective-permute-done.35.refs_8_.refs_2_) | copy-start | bytes 1769476
  191.0 6.3 %collective-permute-start.38 = (f32[512,512]{1,0:T(8,128)}, f32[512,512]{1,0:T(8,128)}, u32[]{:S(2)}, u32[]{:S(2)}) collective-permute-start(f32[512,512]{1,0:T(8,128)} %get-tuple-element.84), channel_id=1, source_target_pairs={{0,1},{1,0},{2,3},{3,2},{4,5},{5,4},{6,7},{7,6},{8,9},{9,8},{10,11... | collective-permute-start | bytes 3145736 | tf_op jit(solution)/shard_map/ppermute | solution.py:32
  194.6 2.3 %collective-permute-start.37 = (f32[1,1152]{1,0:T(1,128)S(1)}, f32[1,1152]{1,0:T(1,128)}, u32[]{:S(2)}, u32[]{:S(2)}) collective-permute-start(f32[1,1152]{1,0:T(1,128)S(1)} %get-tuple-element.78), channel_id=1, source_target_pairs={{0,1},{1,0},{2,3},{3,2},{4,5},{5,4},{6,7},{7,6},{8,9},{9,8},{10,11... | collective-permute-start | bytes 13832 | tf_op jit(solution)/shard_map/ppermute | solution.py:32
  200.1 16.8 %copy-start.3 = (bf16[512,1152]{0,1:T(8,128)(2,1)S(1)}, bf16[512,1152]{0,1:T(8,128)(2,1)}, u32[]{:S(2)}) copy-start(bf16[512,1152]{0,1:T(8,128)(2,1)} %copy-done.2) | copy-start | bytes 3538948
  200.1 16.8 %collective-permute-start.39 = (bf16[512,512]{1,0:T(8,128)(2,1)S(1)}, bf16[512,512]{1,0:T(8,128)(2,1)S(1)}, u32[]{:S(2)}, u32[]{:S(2)}) collective-permute-start(bf16[512,512]{1,0:T(8,128)(2,1)S(1)} %get-tuple-element.87.grad_ref), channel_id=1, source_target_pairs={{0,1},{1,0},{2,3},{3,2},{4,5},{5,4},{6,7},{7,6},{8,9},{9,8},{10,11... | collective-permute-start | bytes 1572872 | tf_op jit(solution)/shard_map/ppermute | solution.py:32
  215.0 1.2 collective-permute-start.40
  (29 other events, 123.4 us)
